TPU v7x, 32 devices: a whole 2x2x4 slice. The times are simulated.
32 devices in a mesh: dp: 16 (over z, x, core), blk: 2 (over y).
Axes of the slice: x: 2, y: 2, z: 4, core: 2. Of those that a mesh axis runs over, the one named last changes fastest.
Arguments:
- hidden_in: bfloat16 [32, 1024, 768], P('dp', 'blk'), may hold values from -6 to 6
- cell_lengths: int32 [32], P('dp'), may hold values from 1 to 1024, as said below
- cotangent: bfloat16 [32, 1024, 768], P('dp', 'blk'), may hold values from -6 to 6
- ln_gains: float32 [2, 2, 768], replicated, may hold values from 0.5 to 1.5
- ln_biases: float32 [2, 2, 768], replicated, may hold values from -1.75 to 1.75
- w_qkv: bfloat16 [2, 768, 2304], replicated, may hold values from -0.21875 to 0.21875
- b_query: float32 [2, 768], replicated, may hold values from -3 to 3
- b_value: float32 [2, 768], replicated, may hold values from -1.75 to 1.75
- w_out: bfloat16 [2, 768, 768], replicated, may hold values from -1.75 to 1.75
- b_out: float32 [2, 768], replicated, may hold values from -1.75 to 1.75
- w_up: bfloat16 [2, 768, 3072], replicated, may hold values from -0.21875 to 0.21875
- b_up: float32 [2, 3072], replicated, may hold values from -3 to 3
- w_down: bfloat16 [2, 3072, 768], replicated, may hold values from -0.109375 to 0.109375
- b_down: float32 [2, 768], replicated, may hold values from -1.75 to 1.75
Outputs:
- hidden_out: bfloat16 [32, 1024, 768], P('dp', 'blk')
- grad_in: float32 [32, 1024, 768], P('dp', 'blk')
- grad_ln_gains: float32 [2, 2, 768], P(None, None, ('dp', 'blk'))
- grad_ln_biases: float32 [2, 2, 768], P(None, None, ('dp', 'blk'))
- grad_w_qkv: float32 [2, 768, 2304], P(None, None, ('dp', 'blk'))
- grad_b_query: float32 [2, 768], P(None, ('dp', 'blk'))
- grad_b_value: float32 [2, 768], P(None, ('dp', 'blk'))
- grad_w_out: float32 [2, 768, 768], P(None, None, ('dp', 'blk'))
- grad_b_out: float32 [2, 768], P(None, ('dp', 'blk'))
- grad_w_up: float32 [2, 768, 3072], P(None, None, ('dp', 'blk'))
- grad_b_up: float32 [2, 3072], P(None, ('dp', 'blk'))
- grad_w_down: float32 [2, 3072, 768], P(None, None, ('dp', 'blk'))
- grad_b_down: float32 [2, 768], P(None, ('dp', 'blk'))
Inputs may be any that keep to these rules, and one draw needn't show every extreme that they name: `cell_lengths`: among the 2 cells of each index of dp one has more than 512 genes, and some cell has 1024.
All inputs are finite; a program needn't handle non-finite values.
Results may differ from a plain program's by a relative error of at most 0.01.
Values may be sent and summed in bfloat16 or wider, within the bound.
No kernel may reach another device: no remote copies, remote signals or barrier semaphores. Data moves between devices by JAX's collectives and lax.ppermute only.
A program may use at most 384 MiB of HBM per device.

v0:
```python
import math

import jax
import jax.numpy as jnp
from jax import lax
from jax.sharding import PartitionSpec as P

HEAD_DIM = 64
LAYERS = 2


EPSILON = 1e-05


def layer_norm(values, gain_vec, shift_vec):
    row_mean = jnp.mean(values, -1, keepdims=True)
    centered = values - row_mean
    variance = jnp.mean(centered * centered, -1, keepdims=True)
    return centered * lax.rsqrt(variance + EPSILON) * gain_vec + shift_vec


def exact_gelu(values):
    return jax.nn.gelu(values, approximate=False)


def contract_rows(left_side, right_side):
    return lax.dot_general(
        left_side, right_side, (((0,), (0,)), ((), ())), preferred_element_type=jnp.float32
    )


def times_transposed(left_side, right_side):
    return lax.dot_general(
        left_side, right_side, (((1,), (1,)), ((), ())), preferred_element_type=jnp.float32
    )


def masked_scores(queries, key_rows, length):
    raw_scores = jnp.einsum(
        "qhd,khd->hqk", queries, key_rows, preferred_element_type=jnp.float32
    ) * (1.0 / math.sqrt(HEAD_DIM))
    valid_keys = jnp.arange(key_rows.shape[0]) < length
    return jnp.where(valid_keys[None, None, :], raw_scores, -jnp.inf)


def attend_rows(cell_items):
    queries, key_rows, values, length = cell_items
    scores = masked_scores(queries, key_rows, length)
    row_max = jnp.max(scores, -1, keepdims=True)
    exponent = jnp.exp(scores - row_max)
    row_total = jnp.sum(exponent, -1, keepdims=True)
    attention = (exponent / row_total).astype(jnp.bfloat16)
    mixed_heads = jnp.einsum("hqk,khd->qhd", attention, values, preferred_element_type=jnp.float32)
    return (mixed_heads, (row_max + jnp.log(row_total))[..., 0])


def attend_back(cell_items):
    queries, key_rows, values, length, logsum, grad_mixed = cell_items
    scores = masked_scores(queries, key_rows, length)
    attention = jnp.exp(scores - logsum[..., None])
    grad_values = jnp.einsum(
        "hqk,qhd->khd",
        attention.astype(jnp.bfloat16),
        grad_mixed,
        preferred_element_type=jnp.float32,
    )
    grad_attention = jnp.einsum(
        "qhd,khd->hqk", grad_mixed, values, preferred_element_type=jnp.float32
    )
    inner_sum = jnp.sum(attention * grad_attention, -1, keepdims=True)
    grad_scores = (attention * (grad_attention - inner_sum)).astype(jnp.bfloat16)
    scale_factor = 1.0 / math.sqrt(HEAD_DIM)
    grad_query = (
        jnp.einsum("hqk,khd->qhd", grad_scores, key_rows, preferred_element_type=jnp.float32)
        * scale_factor
    )
    grad_keys = (
        jnp.einsum("hqk,qhd->khd", grad_scores, queries, preferred_element_type=jnp.float32)
        * scale_factor
    )
    return (grad_query, grad_keys, grad_values)


def split_pairs(every_pair, cell_count, head_count):
    key_rows = every_pair[:, :, 0].reshape(cell_count, -1, head_count, HEAD_DIM)
    values = every_pair[:, :, 1].reshape(cell_count, -1, head_count, HEAD_DIM)
    return (key_rows, values)


def shards(
    hidden_in,
    cell_lengths,
    cotangent,
    ln_gains,
    ln_biases,
    w_qkv,
    b_query,
    b_value,
    w_out,
    b_out,
    w_up,
    b_up,
    w_down,
    b_down,
):
    cell_count, shard_rows, model_width = hidden_in.shape
    head_count = model_width // HEAD_DIM
    row_count = cell_count * shard_rows
    carried = hidden_in.astype(jnp.float32).reshape(row_count, model_width)
    saved_layers = []
    for depth_index in range(LAYERS):
        normed = layer_norm(carried, ln_gains[depth_index, 0], ln_biases[depth_index, 0]).astype(
            jnp.bfloat16
        )
        bias_all = jnp.concatenate(
            [b_query[depth_index], jnp.zeros_like(b_query[depth_index]), b_value[depth_index]]
        )
        projected = (
            jnp.dot(normed, w_qkv[depth_index], preferred_element_type=jnp.float32) + bias_all
        ).astype(jnp.bfloat16)
        local_pairs = projected[:, model_width:].reshape(cell_count, shard_rows, 2, model_width)
        every_pair = lax.all_gather(local_pairs, "blk", axis=1, tiled=True)
        key_rows, values = split_pairs(every_pair, cell_count, head_count)
        queries = projected[:, :model_width].reshape(cell_count, shard_rows, head_count, HEAD_DIM)
        mixed_heads, logsum = lax.map(attend_rows, (queries, key_rows, values, cell_lengths))
        mixed16 = mixed_heads.reshape(row_count, model_width).astype(jnp.bfloat16)
        residual = (
            carried
            + jnp.dot(mixed16, w_out[depth_index], preferred_element_type=jnp.float32)
            + b_out[depth_index]
        )
        normed2 = layer_norm(residual, ln_gains[depth_index, 1], ln_biases[depth_index, 1]).astype(
            jnp.bfloat16
        )
        upper_pre = (
            jnp.dot(normed2, w_up[depth_index], preferred_element_type=jnp.float32)
            + b_up[depth_index]
        )
        active = exact_gelu(upper_pre).astype(jnp.bfloat16)
        next_carried = (
            residual
            + jnp.dot(active, w_down[depth_index], preferred_element_type=jnp.float32)
            + b_down[depth_index]
        )
        kept_pairs = every_pair
        saved_layers.append(
            (carried, projected, kept_pairs, logsum, mixed16, residual, normed2, upper_pre, active)
        )
        carried = next_carried
    hidden_out = carried.reshape(cell_count, shard_rows, model_width).astype(jnp.bfloat16)
    grad_carried = cotangent.astype(jnp.float32).reshape(row_count, model_width)
    collected = []
    for depth_index in reversed(range(LAYERS)):
        (
            layer_input,
            projected,
            kept_pairs,
            logsum,
            mixed16,
            residual,
            normed2,
            upper_pre,
            active,
        ) = saved_layers[depth_index]
        grad_down16 = grad_carried.astype(jnp.bfloat16)
        grad_wdown = contract_rows(active, grad_down16)
        grad_bdown = jnp.sum(grad_down16.astype(jnp.float32), 0)
        grad_active = times_transposed(grad_down16, w_down[depth_index])
        _, gelu_pull = jax.vjp(exact_gelu, upper_pre)
        grad_upper16 = gelu_pull(grad_active)[0].astype(jnp.bfloat16)
        grad_wup = contract_rows(normed2, grad_upper16)
        grad_bup = jnp.sum(grad_upper16.astype(jnp.float32), 0)
        grad_normed2 = times_transposed(grad_upper16, w_up[depth_index])
        _, norm2_pull = jax.vjp(
            layer_norm, residual, ln_gains[depth_index, 1], ln_biases[depth_index, 1]
        )
        grad_resid_part, grad_gain2, grad_shift2 = norm2_pull(grad_normed2)
        grad_residual = grad_carried + grad_resid_part
        grad_attn16 = grad_residual.astype(jnp.bfloat16)
        grad_wout = contract_rows(mixed16, grad_attn16)
        grad_bout = jnp.sum(grad_attn16.astype(jnp.float32), 0)
        grad_mixed16 = times_transposed(grad_attn16, w_out[depth_index]).astype(jnp.bfloat16)
        every_pair = kept_pairs
        key_rows, values = split_pairs(every_pair, cell_count, head_count)
        queries = projected[:, :model_width].reshape(cell_count, shard_rows, head_count, HEAD_DIM)
        grad_mixed_heads = grad_mixed16.reshape(cell_count, shard_rows, head_count, HEAD_DIM)
        grad_query, grad_keys, grad_values = lax.map(
            attend_back, (queries, key_rows, values, cell_lengths, logsum, grad_mixed_heads)
        )
        full_rows = grad_keys.shape[1]
        grad_pairs = jnp.stack(
            [
                grad_keys.reshape(cell_count, full_rows, model_width),
                grad_values.reshape(cell_count, full_rows, model_width),
            ],
            2,
        )
        grad_local_pairs = lax.psum_scatter(grad_pairs, "blk", scatter_dimension=1, tiled=True)
        grad_proj16 = jnp.concatenate(
            [
                grad_query.reshape(row_count, model_width),
                grad_local_pairs.reshape(row_count, 2 * model_width),
            ],
            1,
        ).astype(jnp.bfloat16)
        normed, norm1_pull = jax.vjp(
            layer_norm, layer_input, ln_gains[depth_index, 0], ln_biases[depth_index, 0]
        )
        grad_wqkv = contract_rows(normed.astype(jnp.bfloat16), grad_proj16)
        proj_sums = jnp.sum(grad_proj16.astype(jnp.float32), 0)
        grad_bquery = proj_sums[:model_width]
        grad_bvalue = proj_sums[2 * model_width :]
        grad_normed = times_transposed(grad_proj16, w_qkv[depth_index])
        grad_input_part, grad_gain1, grad_shift1 = norm1_pull(grad_normed)
        grad_carried = grad_residual + grad_input_part
        layer_grads = (
            jnp.stack([grad_gain1, grad_gain2]),
            jnp.stack([grad_shift1, grad_shift2]),
            grad_wqkv,
            grad_bquery,
            grad_bvalue,
            grad_wout,
            grad_bout,
            grad_wup,
            grad_bup,
            grad_wdown,
            grad_bdown,
        )
        collected.append(layer_grads)
    ordered = collected[::-1]
    stacked = tuple((jnp.stack([member[position] for member in ordered]) for position in range(11)))
    stacked = (
        lax.psum_scatter(stacked[0], ("dp", "blk"), scatter_dimension=2, tiled=True),
        lax.psum_scatter(stacked[1], ("dp", "blk"), scatter_dimension=2, tiled=True),
        lax.psum_scatter(stacked[2], ("dp", "blk"), scatter_dimension=2, tiled=True),
        lax.psum_scatter(stacked[3], ("dp", "blk"), scatter_dimension=1, tiled=True),
        lax.psum_scatter(stacked[4], ("dp", "blk"), scatter_dimension=1, tiled=True),
        lax.psum_scatter(stacked[5], ("dp", "blk"), scatter_dimension=2, tiled=True),
        lax.psum_scatter(stacked[6], ("dp", "blk"), scatter_dimension=1, tiled=True),
        lax.psum_scatter(stacked[7], ("dp", "blk"), scatter_dimension=2, tiled=True),
        lax.psum_scatter(stacked[8], ("dp", "blk"), scatter_dimension=1, tiled=True),
        lax.psum_scatter(stacked[9], ("dp", "blk"), scatter_dimension=2, tiled=True),
        lax.psum_scatter(stacked[10], ("dp", "blk"), scatter_dimension=1, tiled=True),
    )
    grad_in = grad_carried.reshape(cell_count, shard_rows, model_width)
    return (hidden_out, grad_in) + tuple(stacked)


def solution(mesh):
    return jax.shard_map(
        shards,
        mesh=mesh,
        in_specs=(
            P("dp", "blk", None),
            P("dp"),
            P("dp", "blk", None),
            P(),
            P(),
            P(),
            P(),
            P(),
            P(),
            P(),
            P(),
            P(),
            P(),
            P(),
        ),
        out_specs=(
            P("dp", "blk", None),
            P("dp", "blk", None),
            P(None, None, ("dp", "blk")),
            P(None, None, ("dp", "blk")),
            P(None, None, ("dp", "blk")),
            P(None, ("dp", "blk")),
            P(None, ("dp", "blk")),
            P(None, None, ("dp", "blk")),
            P(None, ("dp", "blk")),
            P(None, None, ("dp", "blk")),
            P(None, ("dp", "blk")),
            P(None, None, ("dp", "blk")),
            P(None, ("dp", "blk")),
        ),
        check_vma=False,
    )
```

profile of v0, /device:TPU:0, one launch (start us, length us, event | category | flops | bytes accessed | tf_op | source)
XLA Modules:
  0.0 2379.7 jit_solution(16668385886166084357)
XLA Ops:
  34.8 76.6 %all-gather.3.cloned.1.call-done = bf16[2,1024,2,768]{3,2,1,0:T(2,128)(2,1)} async-done(((bf16[2,512,2,768]{3,2,1,0:T(2,128)(2,1)}), bf16[2,1024,2,768]{3,2,1,0:T(2,128)(2,1)}) %all-gather.3.cloned.1.call-update) | async-done | bytes 6291472 | tf_op jit(solution)/shard_map/all_gather | solution.py:122
  125.0 15.2 copy.101
  155.0 72.9 %while.52 = (s32[]{:T(128)}, bf16[2,512,12,64]{1,3,2,0:T(8,128)(2,1)}, f32[2,12,512]{2,1,0:T(8,128)S(1)}, bf16[2,1024,12,64]{1,3,2,0:T(8,128)(2,1)}, s32[2]{0:T(...) while((s32[]{:T(128)}, ...), condition=%wide.region_5.6_spmd, body=%wide.region_2.5_spmd.sunk | while | flops 1686105088 | bytes 93829256 | solution.py:125
  237.6 35.5 %multiply_convert_fusion.3 = (bf16[1024,3072]{1,0:T(8,128)(2,1)}, f32[1024,3072]{1,0:T(8,128)}, f32[1024,3072]{1,0:T(8,128)}) fusion(f32[3072]{0:T(1024)S(1)} %bitcast.471, bf16[2,768,3072]{2,1,0:T(8,128)(2,1)S(1)} %bitcast.478, f32[1024,768]{1,0:T(8,128)S(1)} %get-tuple-element.545, f32[768]{0:T(1024)S(1)} %copy-done.68, f32[768]{0:T(1024)S(1)} %copy-done.61, ...), kind=kOutput, calls=%fused_computation.136 | convolution fusion | flops 5043388416 | bytes 39350272 | tf_op jit(solution)/shard_map/dot_general | solution.py:136
  306.2 67.3 %all-gather.5.cloned.1.call-done = bf16[2,1024,2,768]{3,2,1,0:T(2,128)(2,1)} async-done(((bf16[2,512,2,768]{3,2,1,0:T(2,128)(2,1)}), bf16[2,1024,2,768]{3,2,1,0:T(2,128)(2,1)}) %all-gather.5.cloned.1.call-update) | async-done | bytes 6291472 | tf_op jit(solution)/shard_map/all_gather | solution.py:122
  387.3 15.3 copy.106
  417.4 72.7 %while.53 = (s32[]{:T(128)}, bf16[2,512,12,64]{1,3,2,0:T(8,128)(2,1)}, f32[2,12,512]{2,1,0:T(8,128)S(1)}, bf16[2,1024,12,64]{1,3,2,0:T(8,128)(2,1)}, s32[2]{0:T(...) while((s32[]{:T(128)}, ...), condition=%wide.region_13.14_spmd, body=%wide.region_10.13_spmd.sunk | while | flops 1686105088 | bytes 93829256 | solution.py:125
  499.7 35.8 %multiply_convert_fusion.2 = (bf16[1024,3072]{1,0:T(8,128)(2,1)}, f32[1024,3072]{1,0:T(8,128)}, f32[1024,3072]{1,0:T(8,128)}) fusion(f32[3072]{0:T(1024)S(1)} %bitcast.474, bf16[2,768,3072]{2,1,0:T(8,128)(2,1)S(1)} %bitcast.480, f32[1024,768]{1,0:T(8,128)S(1)} %get-tuple-element.550, f32[768]{0:T(1024)S(1)} %copy-done.70, f32[768]{0:T(1024)S(1)} %copy-done.64, ...), kind=kOutput, calls=%fused_computation.123 | convolution fusion | flops 5043388416 | bytes 39350272 | tf_op jit(solution)/shard_map/dot_general | solution.py:136
  535.5 17.3 convert_reduce_fusion
  581.2 149.4 %while.54 = (s32[]{:T(128)}, bf16[2,512,12,64]{1,3,2,0:T(8,128)(2,1)}, f32[2,1024,12,64]{1,3,2,0:T(8,128)}, f32[2,1024,12,64]{1,3,2,0:T(8,128)}, bf16[2,1024,12,...) while((s32[]{:T(128)}, ...), condition=%wide.region_20.21_spmd, body=%wide.region_18.20_spmd.sunk | while | flops 4122078208 | bytes 267576560 | solution.py:187
  594.0 17.4 multiply_reduce_fusion.13
  611.4 16.9 multiply_convert_fusion.6
  668.3 17.4 multiply_reduce_fusion.13
  685.7 16.9 multiply_convert_fusion.6
  742.5 19.4 copy.131
  761.9 16.4 reshape.355
  783.5 139.5 %reduce-scatter.18.cloned.1.call-done = f32[512,3072]{1,0:T(8,128)} async-done(((f32[1024,3072]{1,0:T(8,128)}), f32[512,3072]{1,0:T(8,128)}) %reduce-scatter.18.cloned.1.call-update) | async-done | bytes 6291472
  948.3 19.5 convert_reduce_fusion.1
  995.3 149.5 %while.55 = (s32[]{:T(128)}, bf16[2,512,12,64]{1,3,2,0:T(8,128)(2,1)}, f32[2,1024,12,64]{1,3,2,0:T(8,128)}, f32[2,1024,12,64]{1,3,2,0:T(8,128)}, bf16[2,1024,12,...) while((s32[]{:T(128)}, ...), condition=%wide.region_28.29_spmd, body=%wide.region_26.28_spmd.sunk | while | flops 4122078208 | bytes 267576560 | solution.py:187
  1008.1 17.4 multiply_reduce_fusion.14
  1025.5 16.9 multiply_convert_fusion.7
  1082.6 17.4 multiply_reduce_fusion.14
  1100.0 16.9 multiply_convert_fusion.7
  1156.7 19.4 copy.133
  1176.1 16.4 reshape.357
  1231.3 28.6 %copy.126 = f32[2,3072,768]{1,0,2:T(2,128)} copy(f32[2,3072,768]{2,1,0:T(8,128)} %pad_maximum_fusion.1) | data formatting | bytes 37748736 | tf_op jit(solution)/shard_map/stack | solution.py:231
  1285.1 28.5 %copy.125 = f32[2,768,3072]{1,0,2:T(2,128)} copy(f32[2,768,3072]{2,1,0:T(8,128)} %pad_maximum_fusion) | data formatting | bytes 37748736 | tf_op jit(solution)/shard_map/stack | solution.py:231
  1391.8 21.6 copy.123
  1440.7 307.0 %all-reduce.18.cloned.1.call-done = f32[2,3072,768]{1,0,2:T(2,128)} async-done(((f32[2,3072,768]{1,0,2:T(2,128)}), f32[2,3072,768]{1,0,2:T(2,128)}) %all-reduce.18.cloned.1.call-update) | async-done | bytes 18874384
  1749.8 307.4 %all-reduce.16.cloned.1.call-done = f32[2,768,3072]{1,0,2:T(2,128)} async-done(((f32[2,768,3072]{1,0,2:T(2,128)}), f32[2,768,3072]{1,0,2:T(2,128)}) %all-reduce.16.cloned.1.call-update) | async-done | bytes 18874384
  2061.5 43.0 %all-reduce.10 = (f32[2,2,768]{2,1,0:T(2,128)S(1)}, f32[2,2,768]{2,1,0:T(2,128)S(1)}, f32[2,768]{1,0:T(2,128)S(1)}, f32[2,768]{1,0:T(2,128)S(1)}, f32[2,768]{1,0:T(2,128)S(1)}, /*index=5*/f32[2,768]{1,0:T(2,128)S(1)}) all-reduce(f32[2,2,768]{2,1,0:T(2,128)S(1)} %pad_maximum_fusion.15, ...), channel_id=4, replica_groups=mesh['dp'=16,'blk'=2] {'dp','blk'}, use_global_device_ids=true, to_apply=%region_36.37.clone | all-reduce | flops 12288 | bytes 98304
  2108.3 260.6 %all-reduce.20.cloned.1.call-done = (f32[2,768,2304]{1,0,2:T(2,128)}, f32[2,768,768]{1,0,2:T(2,128)}) async-done(((f32[2,768,2304]{1,0,2:T(2,128)}, f32[2,768,768]{1,0,2:T(2,128)}), (f32[2,768,2304]{1,0,2:T(2,128)}, f32[2,768,768]{1,0,2:T(2,128)})) %all-reduce.20.cloned.1.call-update) | async-done | bytes 18874384
  (520 shorter events, 734.5 us)
Async XLA Ops:
  7.2 104.1 %all-gather.3.cloned.1.call-start = ((), (), s32[]{:S(2)}) async-start(), calls=%async_computation.3 | async-start | bytes 9437184 | tf_op jit(solution)/shard_map/all_gather | solution.py:122
  28.1 345.5 %all-gather.5.cloned.1.call-start = ((), (), s32[]{:S(2)}) async-start(), calls=%async_computation.4 | async-start | bytes 9437184 | tf_op jit(solution)/shard_map/all_gather | solution.py:122
  140.2 14.8 copy-start.121
  204.2 11.4 copy-start.10
  232.7 40.4 %slice-start.8 = ((s8[9437184]{0:T(1024)(128)(4,1)}), s8[4194304]{0:T(1024)(128)(4,1)S(1)}, s32[]{:S(2)}) async-start(s8[9437184]{0:T(1024)(128)(4,1)} %bitcast.481), calls=%async_computation.19 | async-start | bytes 8388608
  234.4 38.7 %copy-start.14 = (f32[1024,768]{1,0:T(8,128)}, f32[1024,768]{1,0:T(8,128)S(1)}, u32[]{:S(2)}) copy-start(f32[1024,768]{1,0:T(8,128)S(1)} %get-tuple-element.545) | copy-start | bytes 9437188
  234.4 38.6 %copy-start.51 = (f32[1024]{0:T(1024)}, f32[1024]{0:T(1024)S(1)}, u32[]{:S(2)}) copy-start(f32[1024]{0:T(1024)S(1)} %broadcast_multiply_fusion.2) | copy-start | bytes 12292
  235.6 37.5 %copy-start.56 = (f32[1024]{0:T(1024)}, f32[1024]{0:T(1024)S(1)}, u32[]{:S(2)}) copy-start(f32[1024]{0:T(1024)S(1)} %fusion.172) | copy-start | bytes 12292
  237.6 35.5 %copy-start.109 = (f32[768]{0:T(1024)S(1)}, f32[768]{0:T(1024)}, u32[]{:S(2)}) copy-start(f32[768]{0:T(1024)} %get-tuple-element.417) | copy-start | bytes 9220
  237.6 35.5 %slice-start.9 = ((s8[9437184]{0:T(1024)(128)(4,1)}), s8[4194304]{0:T(1024)(128)(4,1)S(1)}, s32[]{:S(2)}) async-start(s8[9437184]{0:T(1024)(128)(4,1)} %bitcast.481), calls=%async_computation.20 | async-start | bytes 8388608
  237.6 35.5 %slice-start.10 = ((s8[9437184]{0:T(1024)(128)(4,1)}), s8[1048576]{0:T(1024)(128)(4,1)S(1)}, s32[]{:S(2)}) async-start(s8[9437184]{0:T(1024)(128)(4,1)} %bitcast.481), calls=%async_computation.21 | async-start | bytes 2097152
  293.0 630.0 %reduce-scatter.18.cloned.1.call-start = ((), (), s32[]{:S(2)}) async-start(), calls=%async_computation.5 | async-start | bytes 18874368
  496.6 66.1 %copy-start.12 = (f32[1024,768]{1,0:T(8,128)}, f32[1024,768]{1,0:T(8,128)S(1)}, u32[]{:S(2)}) copy-start(f32[1024,768]{1,0:T(8,128)S(1)} %get-tuple-element.550) | copy-start | bytes 9437188
  496.6 66.0 %copy-start.54 = (f32[1024]{0:T(1024)}, f32[1024]{0:T(1024)S(1)}, u32[]{:S(2)}) copy-start(f32[1024]{0:T(1024)S(1)} %broadcast_multiply_fusion) | copy-start | bytes 12292
  497.1 65.5 %copy-start.59 = (f32[1024]{0:T(1024)}, f32[1024]{0:T(1024)S(1)}, u32[]{:S(2)}) copy-start(f32[1024]{0:T(1024)S(1)} %fusion.174) | copy-start | bytes 12292
  499.7 35.8 %copy-start.24 = (bf16[2,512,768]{2,1,0:T(8,128)(2,1)S(1)}, bf16[2,512,768]{2,1,0:T(8,128)(2,1)}, u32[]{:S(2)}) copy-start(bf16[2,512,768]{2,1,0:T(8,128)(2,1)} %param.24) | copy-start | bytes 4718596
  611.4 16.9 copy-start.7
  685.7 16.9 copy-start.7
  778.3 569.5 %reduce-scatter.20.cloned.1.call-start = ((), (), s32[]{:S(2)}) async-start(), calls=%async_computation.6 | async-start | bytes 18874368
  948.2 19.5 copy-start.15
  948.2 19.5 copy-start.52
  948.2 19.5 copy-start.57
  948.3 19.5 copy-start.62
  1025.5 16.9 copy-start.6
  1100.0 16.9 copy-start.6
  1192.5 246.7 %reduce-scatter.22.cloned.1.call-start = ((), (), s32[]{:S(2)}) async-start(), calls=%async_computation.7 | async-start | bytes 1622016
  1194.0 12.1 copy-start.18
  1216.4 531.2 %all-reduce.18.cloned.1.call-start = ((), (), s32[]{:S(2)}) async-start(), calls=%async_computation.9 | async-start | bytes 37748736
  1260.0 797.2 %all-reduce.16.cloned.1.call-start = ((), (), s32[]{:S(2)}) async-start(), calls=%async_computation.8 | async-start | bytes 37748736
  1313.6 1055.3 %all-reduce.20.cloned.1.call-start = ((), (), s32[]{:S(2)}) async-start(), calls=%async_computation.10 | async-start | bytes 37748736
  1361.4 13.3 copy-start.34
  1425.3 633.9 %copy-start.35 = (bf16[128,8,2,768]{3,1,2,0:T(8,128)(2,1)S(1)}, bf16[128,8,2,768]{3,1,2,0:T(8,128)(2,1)}, u32[]{:S(2)}) copy-start(bf16[128,8,2,768]{3,1,2,0:T(8,128)(2,1)} %copy-done.34) | copy-start | bytes 9437188
  (119 other events, 557.4 us)
Sparse Core Ops, SparseCore 0:
  28.2 83.0 all-gather.2
  293.1 80.3 all-gather.4
  778.5 144.4 reduce-scatter.17
  1192.6 144.4 reduce-scatter.19
  1342.2 96.9 reduce-scatter.21
  1445.2 302.4 all-reduce.17
  1753.8 303.3 all-reduce.15
  2063.7 305.2 all-reduce.19
where the time goes:
time: 2400 us; the launch traced here: 2380 us
  waiting for transfers between devices  1170 us (49%)
  matrix products  552 us (23%)
  local copies, waits for them, and re-layouts  390 us (16%)
  other arithmetic  205 us (9%)
  blocking collectives  43 us (2%)
    unnamed x14, waiting for transfers between devices  1030 us
    all_gather x2, waiting for transfers between devices, shards(): every_pair = lax.all_gather(local_pairs, 'blk', axis=1, tiled=True)  144 us
    unnamed x282, local copies, waits for them, and re-layouts  138 us
    dot_general x8, matrix products, masked_scores(): jnp.einsum('qhd,khd->hqk', queries, key_rows, preferred_element_type=jnp....  91.8 us
    another operation x12, local copies, waits for them, and re-layouts, shards(): jnp.stack([member[position] for member in ordered])  87.2 us
    dot_general x8, matrix products, times_transposed(): lax.dot_general(left_side, right_side, (((1,), (1,)), ((), ())), preferre...  72.5 us
    dot_general x2, matrix products, shards(): jnp.dot(normed2, w_up[depth_index], preferred_element_type=jnp.float32)  71.2 us
    dot_general x4, matrix products, attend_back(): jnp.einsum('qhd,khd->hqk', grad_mixed, values, preferred_element_type=jnp...  69.4 us
  transfers between devices with their start and end apart: 8, of which 7 were waited for; matrix products, arithmetic and copies ran while one was open for 11% of the time, Pallas kernels for 0%

commit v1 on v0

v1 whole, which is shorter than its diff:
```python
import functools
import math

import jax
import jax.numpy as jnp
from jax import lax
from jax.experimental import pallas as pl
from jax.experimental.pallas import tpu as pltpu
from jax.sharding import PartitionSpec as P

HEAD_DIM = 64
LAYERS = 2
EPSILON = 1e-05
NEG = -1e30
BF = jnp.bfloat16
F32 = jnp.float32
QSCALE = math.log2(math.e) / math.sqrt(HEAD_DIM)


def dot_nn(a, b):
    return lax.dot_general(a, b, (((1,), (0,)), ((), ())), preferred_element_type=F32)


def dot_nt(a, b):
    return lax.dot_general(a, b, (((1,), (1,)), ((), ())), preferred_element_type=F32)


def dot_tn(a, b):
    return lax.dot_general(a, b, (((0,), (0,)), ((), ())), preferred_element_type=F32)


def mask_block(meta_ref, kaug, qone, tokens):
    rows = lax.broadcasted_iota(jnp.int32, (tokens, 128), 0)
    lanes = lax.broadcasted_iota(jnp.int32, (tokens, 128), 1)
    half = tokens // 2
    position = jnp.where(rows < half, rows + meta_ref[1], rows - meta_ref[1])
    masked = jnp.logical_and(lanes == 0, position >= meta_ref[0])
    kaug[...] = jnp.where(masked, NEG, 0.0).astype(BF)
    qone[...] = jnp.where(lanes == 0, 1.0, 0.0).astype(BF)


def attn_fwd_kernel(
    chunk, ahead, meta_ref, q_ref, k_ref, v_ref, o_ref, low_ref, lse_ref, kaug, qone
):
    tokens = q_ref.shape[0]

    @pl.when(pl.program_id(0) == 0)
    def _():
        mask_block(meta_ref, kaug, qone, tokens)

    first = lax.broadcasted_iota(jnp.int32, (tokens, 128), 1) < HEAD_DIM
    q, k, v = q_ref[...], k_ref[...], v_ref[...]
    zero = jnp.zeros_like(k)
    sel = [first, jnp.logical_not(first)]
    keys = [jnp.concatenate([jnp.where(sel[h], k, zero), kaug[...]], 1) for h in range(2)]
    vals = [jnp.where(sel[h], v, zero).T for h in range(2)]
    qa = jnp.concatenate([q, qone[...]], 1)
    units = [(c, h) for c in range(tokens // chunk) for h in range(2)]
    ready = {}

    def scores(unit):
        c, h = unit
        ready[unit] = dot_nt(keys[h], qa[c * chunk : (c + 1) * chunk])

    for unit in units[:ahead]:
        scores(unit)
    kept = {}
    for n, unit in enumerate(units):
        if n + ahead < len(units):
            scores(units[n + ahead])
        c, h = unit
        cols = slice(c * chunk, (c + 1) * chunk)
        st = ready.pop(unit)
        top = jnp.max(st, axis=0, keepdims=True)
        p = jnp.exp2(st - top)
        p = p.astype(BF)
        total = jnp.sum(p.astype(F32), axis=0, keepdims=True)
        kept[h] = (dot_nn(vals[h], p), top, total)
        if h == 1:
            head = lax.broadcasted_iota(jnp.int32, (128, chunk), 0) < HEAD_DIM
            inv = jnp.where(head, 1.0 / kept[0][2], 1.0 / kept[1][2])
            out = ((kept[0][0] + kept[1][0]) * inv).T
            high = out.astype(BF)
            o_ref[cols, :] = high
            low_ref[cols, :] = (out - high.astype(F32)).astype(BF)
            for g in range(2):
                lse_ref[0, g : g + 1, cols] = kept[g][1] + jnp.log2(kept[g][2])


def attn_fwd(proj, meta):
    tokens, width = proj.shape[0], proj.shape[1] // 3
    pairs = width // 128
    spec = lambda off: pl.BlockSpec((tokens, 128), lambda i, m: (0, off + i))
    return pl.pallas_call(
        functools.partial(attn_fwd_kernel, tokens // 2, 2),
        grid_spec=pltpu.PrefetchScalarGridSpec(
            num_scalar_prefetch=1,
            grid=(pairs,),
            in_specs=[spec(0), spec(pairs), spec(2 * pairs)],
            out_specs=[spec(0), spec(0), pl.BlockSpec((1, 8, tokens), lambda i, m: (i, 0, 0))],
            scratch_shapes=[pltpu.VMEM((tokens, 128), BF), pltpu.VMEM((tokens, 128), BF)],
        ),
        out_shape=[
            jax.ShapeDtypeStruct((tokens, width), BF),
            jax.ShapeDtypeStruct((tokens, width), BF),
            jax.ShapeDtypeStruct((pairs, 8, tokens), F32),
        ],
        compiler_params=pltpu.CompilerParams(
            vmem_limit_bytes=56 << 20, dimension_semantics=("arbitrary",)
        ),
        cost_estimate=pl.CostEstimate(
            flops=4 * tokens * tokens * width * 3,
            bytes_accessed=tokens * width * 8,
            transcendentals=pairs * 2 * tokens * tokens,
        ),
        name="attn_fwd",
    )(meta, proj, proj, proj)


def attn_bwd_kernel(
    meta_ref, q_ref, k_ref, v_ref, o_ref, low_ref, do_ref, lse_ref, dq_ref, dk_ref, dv_ref, kaug, qone
):
    tokens = q_ref.shape[0]

    @pl.when(pl.program_id(0) == 0)
    def _():
        mask_block(meta_ref, kaug, qone, tokens)

    first = lax.broadcasted_iota(jnp.int32, (tokens, 128), 1) < HEAD_DIM
    q, k, v, do = q_ref[...], k_ref[...], v_ref[...], do_ref[...]
    zero = jnp.zeros_like(k)
    sel = [first, jnp.logical_not(first)]
    qa = jnp.concatenate([q, qone[...]], 1)
    prod = ((o_ref[...].astype(F32) + low_ref[...].astype(F32)) * do.astype(F32)).T
    dq = dk = dv = None
    for h in range(2):
        kh = jnp.where(sel[h], k, zero)
        delta = jnp.sum(prod[h * HEAD_DIM : (h + 1) * HEAD_DIM], 0, keepdims=True)
        st = dot_nt(jnp.concatenate([kh, kaug[...]], 1), qa)
        dpt = dot_nt(jnp.where(sel[h], v, zero), do)
        p = jnp.exp2(st - lse_ref[0, h : h + 1, :])
        ds = (p * (dpt - delta)).astype(BF)
        dvh = dot_nn(p.astype(BF), jnp.where(sel[h], do, zero))
        dkh = dot_nn(ds, jnp.where(sel[h], q, zero))
        dqh = dot_nn(kh.T, ds)
        dq, dk, dv = (dqh, dkh, dvh) if h == 0 else (dq + dqh, dk + dkh, dv + dvh)
    dq_ref[...] = (dq * (1.0 / math.sqrt(HEAD_DIM))).T.astype(BF)
    dk_ref[...] = (dk * math.log(2.0)).astype(BF)
    dv_ref[...] = dv.astype(BF)


def attn_bwd(proj, mixed, low, g_mixed, lse, meta):
    tokens, width = mixed.shape
    pairs = width // 128
    spec = lambda off: pl.BlockSpec((tokens, 128), lambda i, m: (0, off + i))
    return pl.pallas_call(
        attn_bwd_kernel,
        grid_spec=pltpu.PrefetchScalarGridSpec(
            num_scalar_prefetch=1,
            grid=(pairs,),
            in_specs=[spec(0), spec(pairs), spec(2 * pairs), spec(0), spec(0), spec(0)]
            + [pl.BlockSpec((1, 8, tokens), lambda i, m: (i, 0, 0))],
            out_specs=[spec(0)] * 3,
            scratch_shapes=[pltpu.VMEM((tokens, 128), BF), pltpu.VMEM((tokens, 128), BF)],
        ),
        out_shape=[jax.ShapeDtypeStruct((tokens, width), BF)] * 3,
        compiler_params=pltpu.CompilerParams(
            vmem_limit_bytes=56 << 20, dimension_semantics=("arbitrary",)
        ),
        cost_estimate=pl.CostEstimate(
            flops=10 * tokens * tokens * width * 2,
            bytes_accessed=tokens * width * 16,
            transcendentals=pairs * 2 * tokens * tokens,
        ),
        name="attn_bwd",
    )(meta, proj, proj, proj, mixed, low, g_mixed, lse)


VMEM = pltpu.CompilerParams(vmem_limit_bytes=58 << 20, dimension_semantics=("arbitrary",))


def whole(arr):
    return pl.BlockSpec(arr.shape, lambda *_: (0,) * arr.ndim, pipeline_mode=pl.Buffered(1))


def tile(rows, width, first=0):
    return pl.BlockSpec((rows, width), lambda i, *_: (first + i, 0))


def sds(rows, width, dtype):
    return jax.ShapeDtypeStruct((rows, width), dtype)


def cost(flops, nbytes, trans=0):
    return pl.CostEstimate(flops=int(flops), bytes_accessed=int(nbytes), transcendentals=int(trans))


def normalize(x):
    mean = jnp.mean(x, -1, keepdims=True)
    centered = x - mean
    variance = jnp.mean(centered * centered, -1, keepdims=True)
    rstd = lax.rsqrt(variance + EPSILON)
    return centered * rstd, rstd


def project(n1, wqkv_ref, bias_ref, proj_ref, width):
    for j, factor in enumerate((QSCALE, 1.0, 1.0)):
        cols = slice(j * width, (j + 1) * width)
        part = dot_nn(n1, wqkv_ref[:, cols]) + bias_ref[:, cols]
        proj_ref[:, cols] = (part * factor).astype(BF)


def enter_kernel(x_ref, gain_ref, shift_ref, wqkv_ref, bias_ref, *refs):
    n1_ref, proj_ref = refs[-2:]
    width = x_ref.shape[1]
    xhat, _ = normalize(x_ref[...].astype(F32))
    n1 = (xhat * gain_ref[...] + shift_ref[...]).astype(BF)
    n1_ref[...] = n1
    project(n1, wqkv_ref, bias_ref, proj_ref, width)


def enter(x, gain, shift, wqkv, bias, into, tokens, first):
    rows, width = x.shape
    block = 256
    at = first // block
    ops = [x, gain, shift, wqkv, bias]
    specs = [tile(block, width)] + [whole(a) for a in ops[1:]]
    alias = {}
    if into is not None:
        ops += list(into)
        specs += [pl.BlockSpec(memory_space=pl.ANY)] * 2
        alias = {5: 0, 6: 1}
    return pl.pallas_call(
        enter_kernel,
        grid=(rows // block,),
        in_specs=specs,
        out_specs=[tile(block, width, at), tile(block, 3 * width, at)],
        out_shape=[sds(tokens, width, BF), sds(tokens, 3 * width, BF)],
        input_output_aliases=alias,
        compiler_params=VMEM,
        cost_estimate=cost(6 * rows * width * width, rows * width * 10 + 6 * width * width),
        name="enter",
    )(*ops)


def post_kernel(last, parts, *refs):
    it = iter(refs)
    mixed_ref, x_ref = next(it), next(it)
    wout_ref, bout_ref, gain_ref, shift_ref = next(it), next(it), next(it), next(it)
    wup_ref, bup_ref, wdown_ref, bdown_ref = next(it), next(it), next(it), next(it)
    if not last:
        gain1_ref, shift1_ref, wqkv_ref, bias_ref = next(it), next(it), next(it), next(it)
    resid_ref, n2_ref, active_ref, slope_ref = next(it), next(it), next(it), next(it)
    width = x_ref.shape[1]
    resid = x_ref[...].astype(F32) + dot_nn(mixed_ref[...], wout_ref[...]) + bout_ref[...]
    resid_ref[...] = resid
    xhat, _ = normalize(resid)
    n2 = (xhat * gain_ref[...] + shift_ref[...]).astype(BF)
    n2_ref[...] = n2
    hidden = wup_ref.shape[1] // parts
    total = resid + bdown_ref[...]
    for j in range(parts):
        cols = slice(j * hidden, (j + 1) * hidden)
        upper = dot_nn(n2, wup_ref[:, cols]) + bup_ref[:, cols]
        cdf = 0.5 + 0.5 * lax.erf(upper * math.sqrt(0.5))
        dens = jnp.exp2(upper * upper * (-0.5 * math.log2(math.e))) * (1.0 / math.sqrt(2.0 * math.pi))
        active = (upper * cdf).astype(BF)
        active_ref[:, cols] = active
        slope_ref[:, cols] = (cdf + upper * dens).astype(BF)
        total = total + dot_nn(active, wdown_ref[cols, :])
    if last:
        next(it)[...] = total.astype(BF)
    else:
        x_out, n1_ref, proj_ref = next(it), next(it), next(it)
        x_out[...] = total
        xhat, _ = normalize(total)
        n1 = (xhat * gain1_ref[...] + shift1_ref[...]).astype(BF)
        n1_ref[...] = n1
        project(n1, wqkv_ref, bias_ref, proj_ref, width)


def post(mixed, x, weights, following):
    tokens, width = x.shape
    block = 256
    ff = weights[4].shape[1]
    last = following is None
    ops = [mixed, x] + list(weights) + ([] if last else list(following))
    outs = [(width, F32), (width, BF), (ff, BF), (ff, BF)]
    outs += [(width, BF)] if last else [(width, F32), (width, BF), (3 * width, BF)]
    flops = 2 * tokens * width * (width + 2 * ff + (0 if last else 3 * width))
    return pl.pallas_call(
        functools.partial(post_kernel, last, 4),
        grid=(tokens // block,),
        in_specs=[tile(block, width)] * 2 + [whole(a) for a in ops[2:]],
        out_specs=[tile(block, w) for w, _ in outs],
        out_shape=[sds(tokens, w, t) for w, t in outs],
        compiler_params=VMEM,
        cost_estimate=cost(flops, tokens * ff * 10, 2 * tokens * ff),
        name="post",
    )(*ops)


def norm_back(g_normed, xhat, rstd, gain):
    scaled = g_normed * gain
    mean1 = jnp.mean(scaled, -1, keepdims=True)
    mean2 = jnp.mean(scaled * xhat, -1, keepdims=True)
    return rstd * (scaled - mean1 - xhat * mean2)


def add_row(ref, row, start, value, fresh):
    cols = slice(start, start + value.shape[1])

    @pl.when(fresh)
    def _():
        ref[row : row + 1, cols] = value

    @pl.when(jnp.logical_not(fresh))
    def _():
        ref[row : row + 1, cols] += value


def colsum(x):
    return jnp.sum(x, 0, keepdims=True)


def ff_back_kernel(parts, gx_ref, slope_ref, resid_ref, wdown_ref, wup_ref, wout_ref, gain_ref, *outs):
    gy_ref, gu_ref, gres_ref, ga_ref, gmix_ref, vec_ref = outs
    fresh = pl.program_id(0) == 0
    width = gx_ref.shape[1]
    gx = gx_ref[...].astype(F32)
    gy = gx.astype(BF)
    gy_ref[...] = gy
    hidden = wup_ref.shape[1] // parts
    g_n2 = None
    for j in range(parts):
        cols = slice(j * hidden, (j + 1) * hidden)
        g_act = dot_nt(gy, wdown_ref[cols, :])
        gu = (g_act * slope_ref[:, cols].astype(F32)).astype(BF)
        gu_ref[:, cols] = gu
        add_row(vec_ref, 0, j * hidden, colsum(gu.astype(F32)), fresh)
        part = dot_nt(gu, wup_ref[:, cols])
        g_n2 = part if g_n2 is None else g_n2 + part
    xhat, rstd = normalize(resid_ref[...])
    g_resid = gx + norm_back(g_n2, xhat, rstd, gain_ref[...])
    gres_ref[...] = g_resid
    ga = g_resid.astype(BF)
    ga_ref[...] = ga
    gmix_ref[...] = dot_nt(ga, wout_ref[...]).astype(BF)
    add_row(vec_ref, 1, 0, colsum(g_n2 * xhat), fresh)
    add_row(vec_ref, 1, width, colsum(g_n2), fresh)
    add_row(vec_ref, 1, 2 * width, colsum(gy.astype(F32)), fresh)
    add_row(vec_ref, 1, 3 * width, colsum(ga.astype(F32)), fresh)


def ff_back(gx, slope, resid, wdown, wup, wout, gain):
    tokens, width = resid.shape
    ff = slope.shape[1]
    block = 256
    outs = [(width, BF), (ff, BF), (width, F32), (width, BF), (width, BF)]
    assert ff == 4 * width
    return pl.pallas_call(
        functools.partial(ff_back_kernel, 4),
        grid=(tokens // block,),
        in_specs=[tile(block, width), tile(block, ff), tile(block, width)]
        + [whole(a) for a in (wdown, wup, wout, gain)],
        out_specs=[tile(block, w) for w, _ in outs] + [pl.BlockSpec((8, ff), lambda i: (0, 0))],
        out_shape=[sds(tokens, w, t) for w, t in outs] + [sds(8, ff, F32)],
        compiler_params=VMEM,
        cost_estimate=cost(2 * tokens * width * (2 * ff + width), tokens * ff * 8),
        name="ff_back",
    )(gx, slope, resid, wdown, wup, wout, gain)


def qkv_back_kernel(dq_ref, dk_ref, dv_ref, wqkv_ref, x_ref, gres_ref, gain_ref, *refs):
    gx_ref, vec_ref = refs[-2:]
    fresh = pl.program_id(0) == 0
    width = x_ref.shape[1]
    grads = [dq_ref[...], dk_ref[...], dv_ref[...]]
    g_norm = dot_nt(jnp.concatenate(grads, 1), wqkv_ref[...])
    xhat, rstd = normalize(x_ref[...].astype(F32))
    gx = gres_ref[...] + norm_back(g_norm, xhat, rstd, gain_ref[...])
    gx_ref[...] = gx.astype(gx_ref.dtype)
    add_row(vec_ref, 0, 0, colsum(g_norm * xhat), fresh)
    add_row(vec_ref, 0, width, colsum(g_norm), fresh)
    add_row(vec_ref, 0, 2 * width, colsum(grads[0].astype(F32)), fresh)
    add_row(vec_ref, 0, 3 * width, colsum(grads[2].astype(F32)), fresh)


def qkv_back(grads, wqkv, x, x_first, g_resid, gain, first, rows, dtype):
    width = x.shape[1]
    block = 256
    at = first // block
    return pl.pallas_call(
        qkv_back_kernel,
        grid=(rows // block,),
        in_specs=[tile(block, width, at)] * 3
        + [whole(wqkv), tile(block, width, x_first // block), tile(block, width, at), whole(gain)],
        out_specs=[tile(block, width), pl.BlockSpec((8, 4 * width), lambda i: (0, 0))],
        out_shape=[sds(rows, width, dtype), sds(8, 4 * width, F32)],
        compiler_params=VMEM,
        cost_estimate=cost(6 * rows * width * width, rows * width * 20),
        name="qkv_back",
    )(*grads, wqkv, x, g_resid, gain)


def plain_grad(lefts, right):
    return jnp.concatenate([dot_tn(left, right) for left in lefts], 0).astype(BF)


def swap_halves(x):
    return lax.ppermute(x, "blk", [(0, 1), (1, 0)])


class Halving:
    def __init__(self, mesh):
        self.dp = mesh.shape["dp"]
        self.blk = mesh.shape["blk"]
        self.bits = self.dp.bit_length() - 1
        assert self.blk == 2 and 1 << self.bits == self.dp

    def stages(self, blk_first):
        dp_bits = list(range(self.bits))
        rest = ["blk", 1] if blk_first else [1, "blk"]
        return [0] + rest + dp_bits[2:]

    def split(self, rows):
        owners = self.dp * self.blk
        return rows.reshape((2,) * (self.bits + 1) + (rows.shape[0] // owners, rows.shape[1]))

    def run(self, rows, blk_first, wide=False):
        arr = self.split(rows)
        names = list(reversed(range(self.bits))) + ["blk"]
        order = self.stages(blk_first)
        for n, stage in enumerate(order):
            dim = names.index(stage)
            names.pop(dim)
            if stage == "blk":
                mine = lax.axis_index("blk")
                send = lambda x: lax.ppermute(x, "blk", [(0, 1), (1, 0)])
            else:
                mine = (lax.axis_index("dp") >> stage) & 1
                perm = [(i, i ^ (1 << stage)) for i in range(self.dp)]
                send = lambda x: lax.ppermute(x, "dp", perm)
            keep = lax.dynamic_index_in_dim(arr, mine, dim, keepdims=False)
            other = lax.dynamic_index_in_dim(arr, 1 - mine, dim, keepdims=False)
            arr = keep.astype(F32) + send(other).astype(F32)
            if not wide and n + 1 < len(order):
                arr = arr.astype(BF)
        return arr


def shards(
    mesh,
    hidden_in,
    cell_lengths,
    cotangent,
    ln_gains,
    ln_biases,
    w_qkv,
    b_query,
    b_value,
    w_out,
    b_out,
    w_up,
    b_up,
    w_down,
    b_down,
):
    cells, half, width = hidden_in.shape
    tokens = cells * half
    halving = Halving(mesh)
    assert cells == halving.blk
    owners = halving.dp * halving.blk
    side = lax.axis_index("blk")
    meta = jnp.stack([lax.dynamic_index_in_dim(cell_lengths, side, 0, False), side * half])
    meta = meta.astype(jnp.int32)

    def split_cell(both):
        own = lax.dynamic_index_in_dim(both, side, 0, False)
        other = lax.dynamic_index_in_dim(both, 1 - side, 0, False)
        return own, swap_halves(other)

    def return_cell(own, back):
        return jnp.where(side == 0, jnp.stack([own, back]), jnp.stack([back, own]))

    row = lambda v: v[None, :]
    biases = [
        row(jnp.concatenate([b_query[d], jnp.zeros_like(b_query[d]), b_value[d]]))
        for d in range(LAYERS)
    ]
    first = [(row(ln_gains[d, 0]), row(ln_biases[d, 0]), w_qkv[d], biases[d]) for d in range(LAYERS)]
    own, other = split_cell(hidden_in)
    entered = enter(own, *first[0], None, tokens, 0)
    n1, proj = enter(other, *first[0], entered, tokens, half)
    carried = jnp.concatenate([own, other], 0)
    saved = []
    for d in range(LAYERS):
        mixed, low, lse = attn_fwd(proj, meta)
        weights = (
            w_out[d],
            row(b_out[d]),
            row(ln_gains[d, 1]),
            row(ln_biases[d, 1]),
            w_up[d],
            row(b_up[d]),
            w_down[d],
            row(b_down[d]),
        )
        last = d + 1 == LAYERS
        outs = post(mixed, carried, weights, None if last else first[d + 1])
        saved.append((carried, n1, proj, mixed, low, lse) + tuple(outs[:4]))
        if not last:
            carried, n1, proj = outs[4:]
    out16 = outs[4]
    hidden_out = return_cell(out16[:half], swap_halves(out16[half:]))

    gx = jnp.concatenate(split_cell(cotangent), 0)
    sums = {}
    vectors = {}
    for d in reversed(range(LAYERS)):
        layer_in, n1, proj, mixed, low, lse, resid, n2, active, slope = saved[d]
        gy, gu, g_resid, ga, g_mixed, vec2 = ff_back(
            gx, slope, resid, w_down[d], w_up[d], w_out[d], row(ln_gains[d, 1])
        )
        sums["down", d] = halving.run(plain_grad([gy], active), False)
        sums["up", d] = halving.run(plain_grad([gu], n2), True)
        sums["out", d] = halving.run(plain_grad([ga], mixed), False)
        grads = attn_bwd(proj, mixed, low, g_mixed, lse, meta)
        sums["qkv", d] = halving.run(plain_grad(grads, n1), d == 0)
        gain1 = row(ln_gains[d, 0])
        if d > 0:
            gx, vec1 = qkv_back(grads, w_qkv[d], layer_in, 0, g_resid, gain1, 0, tokens, F32)
        else:
            theirs, vec_a = qkv_back(
                grads, w_qkv[d], layer_in, half, g_resid, gain1, half, half, BF
            )
            back = swap_halves(theirs)
            mine, vec_b = qkv_back(grads, w_qkv[d], layer_in, 0, g_resid, gain1, 0, half, F32)
            vec1 = vec_a + vec_b
        at = lambda v, r, n: v[r, n * width : (n + 1) * width]
        vectors[d] = [
            at(vec1, 0, 0),
            at(vec2, 1, 0),
            at(vec1, 0, 1),
            at(vec2, 1, 1),
            at(vec1, 0, 2),
            at(vec1, 0, 3),
            at(vec2, 1, 3),
            at(vec2, 1, 2),
            vec2[0],
        ]
    grad_in = return_cell(mine, back.astype(F32))

    flat = [v.reshape(owners, -1) for d in range(LAYERS) for v in vectors[d]]
    widths = [f.shape[1] for f in flat]
    flat = halving.run(jnp.concatenate(flat, 1), False, wide=True)[0]
    pieces = jnp.split(flat, [sum(widths[: i + 1]) for i in range(len(widths) - 1)])
    per = [pieces[:9], pieces[9:]]
    pick = lambda i: jnp.stack([per[0][i], per[1][i]])
    gains = jnp.stack([jnp.stack([per[d][0], per[d][1]]) for d in range(LAYERS)])
    shifts = jnp.stack([jnp.stack([per[d][2], per[d][3]]) for d in range(LAYERS)])
    mat = lambda name: jnp.stack([sums[name, d].T for d in range(LAYERS)])
    return (
        hidden_out,
        grad_in,
        gains,
        shifts,
        mat("qkv"),
        pick(4),
        pick(5),
        mat("out"),
        pick(6),
        mat("up"),
        pick(8),
        mat("down"),
        pick(7),
    )


def solution(mesh):
    both = ("dp", "blk")
    row = P("dp", "blk", None)
    last3 = P(None, None, both)
    last2 = P(None, both)
    return jax.shard_map(
        functools.partial(shards, mesh),
        mesh=mesh,
        in_specs=(row, P("dp"), row) + (P(),) * 11,
        out_specs=(
            row,
            row,
            last3,
            last3,
            last3,
            last2,
            last2,
            last3,
            last2,
            last3,
            last2,
            last3,
            last2,
        ),
        check_vma=False,
    )
```

time: 2400 us -> 637 us (0.27)
  waiting for transfers between devices: 1170 us -> 190 us
  matrix products: 552 us -> 49.7 us
  local copies, waits for them, and re-layouts: 390 us -> 50.7 us
  Pallas kernels: 0 us -> 253 us
  other arithmetic: 205 us -> 29.4 us
  starting transfers between devices: 0.33 us -> 59.1 us
  blocking collectives: 43 us -> 0 us
    unnamed x14 -> x0, waiting for transfers between devices: 1030 us -> none
    dot_general x52 -> x12, matrix products: 552 us -> 49.7 us  [dot_tn(): lax.dot_general(a, b, (((0,), (0,)), ((), ())), preferred_element_type=F32)]
    pallas_call x0 -> x13, Pallas kernels: none -> 253 us  [the longest x2 69.9 us: attn_bwd(): pl.pallas_call(attn_bwd_kernel, grid_spec=pltpu.PrefetchScalarGridSpec(nu...]
    ppermute x0 -> x49, waiting for transfers between devices: none -> 190 us  [the longest x36 130 us: run(): send = lambda x: lax.ppermute(x, 'dp', perm)]
    all_gather x2 -> x0, waiting for transfers between devices: 144 us -> none  [shards(): every_pair = lax.all_gather(local_pairs, 'blk', axis=1, tiled=True)]
    unnamed x282 -> x88, local copies, waits for them, and re-layouts: 138 us -> 3.81 us
    another operation x25 -> x4, local copies, waits for them, and re-layouts: 112 us -> 2.21 us  [the longest x2 1.22 us: shards(): row = lambda v: v[None, :]]
    slice x21 -> x9, local copies, waits for them, and re-layouts: 102 us -> 5.63 us  [the longest x4 2.52 us: shards(): at = lambda v, r, n: v[r, n * width:(n + 1) * width]]
  transfers between devices with their start and end apart: 8 -> 49, of which waited for: 7 -> 28; matrix products, arithmetic and copies ran while one was open for 11% -> 16% of each run, Pallas kernels for 0% -> 16%
where the time goes in v1:
time: 637 us; the launch traced here: 634 us
  Pallas kernels  253 us (40%)
  waiting for transfers between devices  190 us (30%)
  starting transfers between devices  59.1 us (9%)
  local copies, waits for them, and re-layouts  50.7 us (8%)
  matrix products  49.7 us (8%)
  other arithmetic  29.4 us (5%)
    ppermute x36, waiting for transfers between devices, run(): send = lambda x: lax.ppermute(x, 'dp', perm)  130 us
    pallas_call x2, Pallas kernels, attn_bwd(): pl.pallas_call(attn_bwd_kernel, grid_spec=pltpu.PrefetchScalarGridSpec(nu...  69.9 us
    pallas_call x2, Pallas kernels, ff_back(): pl.pallas_call(functools.partial(ff_back_kernel, 4), grid=(tokens // bloc...  53.7 us
    pallas_call x2, Pallas kernels, post(): pl.pallas_call(functools.partial(post_kernel, last, 4), grid=(tokens // b...  49.7 us
    dot_general x12, matrix products, dot_tn(): lax.dot_general(a, b, (((0,), (0,)), ((), ())), preferred_element_type=F32)  49.7 us
    ppermute x36, starting transfers between devices, run(): send = lambda x: lax.ppermute(x, 'dp', perm)  42.4 us
    pallas_call x2, Pallas kernels, attn_fwd(): pl.pallas_call(functools.partial(attn_fwd_kernel, tokens // 2, 2), grid_s...  42 us
    ppermute x9, waiting for transfers between devices, run(): send = lambda x: lax.ppermute(x, 'blk', [(0, 1), (1, 0)])  33.7 us
  transfers between devices with their start and end apart: 49, of which 28 were waited for; matrix products, arithmetic and copies ran while one was open for 16% of the time, Pallas kernels for 16%

profile of v1, /device:TPU:0, one launch (start us, length us, event | category | flops | bytes accessed | tf_op | source)
XLA Modules:
  0.0 633.7 jit_solution(11489717102517705098)
XLA Ops:
  9.1 7.3 %slice_bitcast_fusion.4 = (bf16[768,2304]{1,0:T(8,128)(2,1)}, bf16[768,2304]{1,0:T(8,128)(2,1)}) fusion(bf16[2,768,2304]{2,1,0:T(8,128)(2,1)} %param.19), kind=kLoop, calls=%fused_computation.22 | loop fusion | bytes 14155776 | tf_op jit(solution)/shard_map/squeeze | solution.py:491
  21.6 8.3 %slice_bitcast_fusion.1 = (bf16[768,3072]{1,0:T(8,128)(2,1)}, bf16[768,3072]{1,0:T(8,128)(2,1)}) fusion(bf16[2,768,3072]{2,1,0:T(8,128)(2,1)} %param.24), kind=kLoop, calls=%fused_computation.13 | loop fusion | bytes 18874368 | tf_op jit(solution)/shard_map/squeeze | solution.py:504
  32.1 6.3 enter.2
  41.4 5.9 enter.3
  47.3 21.0 %attn_fwd.2 = (bf16[1024,768]{1,0:T(8,128)(2,1)}, bf16[1024,768]{1,0:T(8,128)(2,1)}, f32[6,8,1024]{2,1,0:T(8,128)}) custom-call(s32[2]{0:T(128)} %pad_add_fusion.meta_ref, bf16[1024,2304]{1,0:T(8,128)(2,1)} %get-tuple-element.61.q_ref.k_ref.v_ref, bf16[1024,2304]{1,0:T(8,128)(2,1)} %get-tuple-element.61.q_ref.k_ref.v_ref, ...), custom_call_target="tpu_custom_call" | custom-call | flops 9663676416 | bytes 6291456 | tf_op jit(solution)/shard_map/attn_fwd/pallas_call | solution.py:94
  70.6 27.8 %post.2 = (f32[1024,768]{1,0:T(8,128)}, bf16[1024,768]{1,0:T(8,128)(2,1)}, bf16[1024,3072]{1,0:T(8,128)(2,1)}, bf16[1024,3072]{1,0:T(8,128)(2,1)}, f32[1024,768]...) custom-call(bf16[1024,768]{1,0:T(8,128)(2,1)} %get-tuple-element.62.refs_0_.o_ref, ...), custom_call_target="tpu_custom_call" | custom-call | flops 14495514624 | bytes 31457280 | tf_op jit(solution)/shard_map/post/pallas_call | solution.py:291
  98.5 21.0 %attn_fwd.3 = (bf16[1024,768]{1,0:T(8,128)(2,1)}, bf16[1024,768]{1,0:T(8,128)(2,1)}, f32[6,8,1024]{2,1,0:T(8,128)}) custom-call(s32[2]{0:T(128)} %pad_add_fusion.meta_ref, bf16[1024,2304]{1,0:T(8,128)(2,1)} %get-tuple-element.63.q_ref.k_ref.v_ref, bf16[1024,2304]{1,0:T(8,128)(2,1)} %get-tuple-element.63.q_ref.k_ref.v_ref, ...), custom_call_target="tpu_custom_call" | custom-call | flops 9663676416 | bytes 6291456 | tf_op jit(solution)/shard_map/attn_fwd/pallas_call | solution.py:94
  119.5 21.9 %post.3 = (f32[1024,768]{1,0:T(8,128)}, bf16[1024,768]{1,0:T(8,128)(2,1)}, bf16[1024,3072]{1,0:T(8,128)(2,1)}, bf16[1024,3072]{1,0:T(8,128)(2,1)}, bf16[1024,768]{1,0:T(8,128)(2,1)}) custom-call(bf16[1024,768]{1,0:T(8,128)(2,1)} %get-tuple-element.64.refs_0_.o_ref, f32[1024,768]{1,0:T(8,128)} %get-tuple-element.65.refs_1_.x_ref, ...), custom_call_target="tpu_custom_call" | custom-call | flops 10871635968 | bytes 31457280 | tf_op jit(solution)/shard_map/post/pallas_call | solution.py:291
  143.9 26.8 %ff_back.2 = (bf16[1024,768]{1,0:T(8,128)(2,1)}, bf16[1024,3072]{1,0:T(8,128)(2,1)}, f32[1024,768]{1,0:T(8,128)}, bf16[1024,768]{1,0:T(8,128)(2,1)}, bf16[1024,768]{1,0:T(8,128)(2,1)}, /*index=5*/f32[8,3072]{1,0:T(8,128)}) custom-call(bf16[1024,768]{1,0:T(8,128)(2,1)} %pad_maximum_fusion.3.gx_ref, bf16[1024,3072]{1,0:T(8,128)(2,1)} %get-tuple-element.69.slope_ref, ...), custom_call_target="tpu_custom_call" | custom-call | flops 10871635968 | bytes 25165824 | tf_op jit(solution)/shard_map/ff_back/pallas_call | solution.py:361
  170.8 34.9 %attn_bwd.2 = (bf16[1024,768]{1,0:T(8,128)(2,1)}, bf16[1024,768]{1,0:T(8,128)(2,1)}, bf16[1024,768]{1,0:T(8,128)(2,1)}) custom-call(s32[2]{0:T(128)} %pad_add_fusion.meta_ref, bf16[1024,2304]{1,0:T(8,128)(2,1)} %get-tuple-element.63.q_ref.k_ref.v_ref, bf16[1024,2304]{1,0:T(8,128)(2,1)} %get-tuple-element.63.q_ref.k_ref.v_ref, ...), custom_call_target="tpu_custom_call" | custom-call | flops 16106127360 | bytes 12582912 | tf_op jit(solution)/shard_map/attn_bwd/pallas_call | solution.py:156
  205.7 10.9 %qkv_back.3 = (f32[1024,768]{1,0:T(8,128)}, f32[8,3072]{1,0:T(8,128)}) custom-call(bf16[1024,768]{1,0:T(8,128)(2,1)} %get-tuple-element.73.dq_ref, bf16[1024,768]{1,0:T(8,128)(2,1)} %get-tuple-element.74.dk_ref, bf16[1024,768]{1,0:T(8,128)(2,1)} %get-tuple-element.75.dv_ref, bf16[768,2304]{1,0:T(8,128)(2,1)} %get-tuple-element.129.refs_12_.wqkv_ref, ...), custom_call_target="tpu_custom_call" | custom-call | flops 3623878656 | bytes 15728640 | tf_op jit(solution)/shard_map/qkv_back/pallas_call | solution.py:393
  216.6 26.9 %ff_back.3 = (bf16[1024,768]{1,0:T(8,128)(2,1)}, bf16[1024,3072]{1,0:T(8,128)(2,1)}, f32[1024,768]{1,0:T(8,128)}, bf16[1024,768]{1,0:T(8,128)(2,1)}, bf16[1024,768]{1,0:T(8,128)(2,1)}, /*index=5*/f32[8,3072]{1,0:T(8,128)}) custom-call(f32[1024,768]{1,0:T(8,128)} %get-tuple-element.77.gx_ref, bf16[1024,3072]{1,0:T(8,128)(2,1)} %get-tuple-element.78.slope_ref, ...), custom_call_target="tpu_custom_call" | custom-call | flops 10871635968 | bytes 25165824 | tf_op jit(solution)/shard_map/ff_back/pallas_call | solution.py:361
  243.5 35.0 %attn_bwd.3 = (bf16[1024,768]{1,0:T(8,128)(2,1)}, bf16[1024,768]{1,0:T(8,128)(2,1)}, bf16[1024,768]{1,0:T(8,128)(2,1)}) custom-call(s32[2]{0:T(128)} %pad_add_fusion.meta_ref, bf16[1024,2304]{1,0:T(8,128)(2,1)} %get-tuple-element.61.q_ref.k_ref.v_ref, bf16[1024,2304]{1,0:T(8,128)(2,1)} %get-tuple-element.61.q_ref.k_ref.v_ref, ...), custom_call_target="tpu_custom_call" | custom-call | flops 16106127360 | bytes 12582912 | tf_op jit(solution)/shard_map/attn_bwd/pallas_call | solution.py:156
  278.6 7.1 %qkv_back.4 = (f32[512,768]{1,0:T(8,128)}, f32[8,3072]{1,0:T(8,128)}) custom-call(bf16[1024,768]{1,0:T(8,128)(2,1)} %get-tuple-element.82.dq_ref, bf16[1024,768]{1,0:T(8,128)(2,1)} %get-tuple-element.83.dk_ref, bf16[1024,768]{1,0:T(8,128)(2,1)} %get-tuple-element.84.dv_ref, bf16[768,2304]{1,0:T(8,128)(2,1)} %get-tuple-element.130.wqkv_ref, ...), custom_call_target="tpu_custom_call" | custom-call | flops 1811939328 | bytes 7864320 | tf_op jit(solution)/shard_map/qkv_back/pallas_call | solution.py:393
  285.7 7.2 %qkv_back.5 = (bf16[512,768]{1,0:T(8,128)(2,1)}, f32[8,3072]{1,0:T(8,128)}) custom-call(bf16[1024,768]{1,0:T(8,128)(2,1)} %get-tuple-element.82.dq_ref, bf16[1024,768]{1,0:T(8,128)(2,1)} %get-tuple-element.83.dk_ref, bf16[1024,768]{1,0:T(8,128)(2,1)} %get-tuple-element.84.dv_ref, bf16[768,2304]{1,0:T(8,128)(2,1)} %get-tuple-element.130.wqkv_ref, ...), custom_call_target="tpu_custom_call" | custom-call | flops 1811939328 | bytes 7864320 | tf_op jit(solution)/shard_map/qkv_back/pallas_call | solution.py:393
  314.6 8.6 %convolution_convert_fusion.1 = bf16[768,3072]{1,0:T(8,128)(2,1)S(1)} fusion(bf16[1024,768]{1,0:T(8,128)(2,1)S(1)} %copy-done.39, bf16[1024,3072]{1,0:T(8,128)(2,1)} %get-tuple-element.102), kind=kOutput, calls=%fused_computation.1 | convolution fusion | flops 4834197504 | bytes 12582912 | tf_op jit(solution)/shard_map/dot_general | solution.py:29
  325.1 8.2 %convolution_convert_fusion = bf16[768,3072]{1,0:T(8,128)(2,1)S(1)} fusion(bf16[1024,768]{1,0:T(8,128)(2,1)S(1)} %copy-done.38, bf16[1024,3072]{1,0:T(8,128)(2,1)} %get-tuple-element.104), kind=kOutput, calls=%fused_computation | convolution fusion | flops 4834197504 | bytes 12582912 | tf_op jit(solution)/shard_map/dot_general | solution.py:29
  335.2 8.5 %convolution_convert_fusion.2 = bf16[3072,768]{1,0:T(8,128)(2,1)S(1)} fusion(bf16[1024,3072]{1,0:T(8,128)(2,1)} %get-tuple-element.99, bf16[1024,768]{1,0:T(8,128)(2,1)S(1)} %copy-done.41), kind=kOutput, calls=%fused_computation.2 | convolution fusion | flops 4834197504 | bytes 12582912 | tf_op jit(solution)/shard_map/dot_general | solution.py:29
  352.7 5.5 convolution_convert_fusion.3
  384.8 11.6 %collective-permute-done.3 = bf16[512,768]{1,0:T(8,128)(2,1)S(1)} collective-permute-done((bf16[512,768]{1,0:T(8,128)(2,1)S(1)}, bf16[512,768]{1,0:T(8,128)(2,1)S(1)}, u32[]{:S(2)}, u32[]{:S(2)}) %collective-permute-start.3) | collective-permute-done | bytes 786464 | tf_op jit(solution)/shard_map/ppermute | solution.py:411
  396.6 14.3 %collective-permute-done.1 = bf16[512,768]{1,0:T(8,128)(2,1)S(1)} collective-permute-done((bf16[512,768]{1,0:T(8,128)(2,1)S(1)}, bf16[512,768]{1,0:T(8,128)(2,1)S(1)}, u32[]{:S(2)}, u32[]{:S(2)}) %collective-permute-start.1) | collective-permute-done | bytes 786464 | tf_op jit(solution)/shard_map/ppermute | solution.py:411
  420.0 5.1 collective-permute-done.25
  469.5 10.5 %collective-permute-done.10 = bf16[2,2,2,72,768]{4,3,0,1,2:T(8,128)(2,1)S(1)} collective-permute-done((bf16[2,2,2,72,768]{4,3,0,1,2:T(8,128)(2,1)}, bf16[2,2,2,72,768]{4,3,0,1,2:T(8,128)(2,1)S(1)}, u32[]{:S(2)}, u32[]{:S(2)}) %collective-permute-start.10) | collective-permute-done | bytes 884768 | tf_op jit(solution)/shard_map/ppermute | solution.py:439
  485.4 56.6 %collective-permute-done.11 = bf16[2,2,72,768]{3,2,0,1:T(8,128)(2,1)S(1)} collective-permute-done((bf16[2,2,72,768]{3,2,0,1:T(8,128)(2,1)S(1)}, bf16[2,2,72,768]{3,2,0,1:T(8,128)(2,1)S(1)}, u32[]{:S(2)}, u32[]{:S(2)}) %collective-permute-start.11) | collective-permute-done | bytes 442400 | tf_op jit(solution)/shard_map/ppermute | solution.py:443
  551.2 4.7 collective-permute-done.17
  558.2 6.1 collective-permute-done.13
  564.8 6.3 collective-permute-done.18
  578.0 9.8 %collective-permute-done.41 = bf16[2,2,24,3072]{3,2,0,1:T(8,128)(2,1)S(1)} collective-permute-done((bf16[2,2,24,3072]{3,2,0,1:T(8,128)(2,1)S(1)}, bf16[2,2,24,3072]{3,2,0,1:T(8,128)(2,1)S(1)}, u32[]{:S(2)}, u32[]{:S(2)}) %collective-permute-start.41) | collective-permute-done | bytes 589856 | tf_op jit(solution)/shard_map/ppermute | solution.py:439
  589.4 4.7 collective-permute-done.46
  601.5 7.5 %collective-permute-done.47 = bf16[2,24,3072]{2,1,0:T(8,128)(2,1)S(1)} collective-permute-done((bf16[2,24,3072]{2,1,0:T(8,128)(2,1)S(1)}, bf16[2,24,3072]{2,1,0:T(8,128)(2,1)S(1)}, u32[]{:S(2)}, u32[]{:S(2)}) %collective-permute-start.47) | collective-permute-done | bytes 294944 | tf_op jit(solution)/shard_map/ppermute | solution.py:443
  610.8 6.5 %collective-permute-done.32 = bf16[2,96,768]{2,1,0:T(8,128)(2,1)S(1)} collective-permute-done((bf16[2,96,768]{2,1,0:T(8,128)(2,1)S(1)}, bf16[2,96,768]{2,1,0:T(8,128)(2,1)S(1)}, u32[]{:S(2)}, u32[]{:S(2)}) %collective-permute-start.32) | collective-permute-done | bytes 294944 | tf_op jit(solution)/shard_map/ppermute | solution.py:443
  623.3 7.8 %collective-permute-done.33 = bf16[96,768]{1,0:T(8,128)(2,1)S(1)} collective-permute-done((bf16[96,768]{1,0:T(8,128)(2,1)S(1)}, bf16[96,768]{1,0:T(8,128)(2,1)S(1)}, u32[]{:S(2)}, u32[]{:S(2)}) %collective-permute-start.33) | collective-permute-done | bytes 147488 | tf_op jit(solution)/shard_map/ppermute | solution.py:443
  (346 shorter events, 181.0 us)
Async XLA Ops:
  3.4 38.0 %collective-permute-start = (bf16[512,768]{1,0:T(8,128)(2,1)}, bf16[512,768]{1,0:T(8,128)(2,1)}, u32[]{:S(2)}, u32[]{:S(2)}) collective-permute-start(bf16[512,768]{1,0:T(8,128)(2,1)} %get-tuple-element.150), channel_id=1, source_target_pairs={{0,1},{1,0},{2,3},{3,2},{4,5},{5,4},{6,7},{7,6},{8,9},{9,8},{10,11... | collective-permute-start | bytes 2359304 | tf_op jit(solution)/shard_map/ppermute | solution.py:411
  7.8 133.6 %collective-permute-start.2 = (bf16[512,768]{1,0:T(8,128)(2,1)}, bf16[512,768]{1,0:T(8,128)(2,1)}, u32[]{:S(2)}, u32[]{:S(2)}) collective-permute-start(bf16[512,768]{1,0:T(8,128)(2,1)} %get-tuple-element.146), channel_id=1, source_target_pairs={{0,1},{1,0},{2,3},{3,2},{4,5},{5,4},{6,7},{7,6},{8,9},{9,8},{10,11... | collective-permute-start | bytes 2359304 | tf_op jit(solution)/shard_map/ppermute | solution.py:411
  314.5 44.6 %collective-permute-start.4 = (f32[2,2,2,2,1,576]{5,3,2,1,0,4:T(2,128)S(1)}, f32[2,2,2,2,1,576]{5,3,2,1,0,4:T(2,128)S(1)}, u32[]{:S(2)}, u32[]{:S(2)}) collective-permute-start(f32[2,2,2,2,1,576]{5,3,2,1,0,4:T(2,128)S(1)} %dynamic-slice_bitcast_fusion.34), channel_id=1, source_target_pairs={{0,2},{2,0},{4,6},{6,4},{8,10},{10,8},{12,14},{14,12},{16,18},{18,... | collective-permute-start | bytes 110600 | tf_op jit(solution)/shard_map/ppermute | solution.py:443
  323.9 136.6 %collective-permute-start.39 = (bf16[2,2,2,2,24,3072]{5,4,0,1,3,2:T(8,128)(2,1)S(1)}, bf16[2,2,2,2,24,3072]{5,4,0,1,3,2:T(8,128)(2,1)S(1)}, u32[]{:S(2)}, u32[]{:S(2)}) collective-permute-start(bf16[2,2,2,2,24,3072]{5,4,0,1,3,2:T(8,128)(2,1)S(1)} %bitcast.379), channel_id=1, source_target_pairs={{0,2},{2,0},{4,6},{6,4},{8,10},{10,8},{12,14},{14,12},{16,18},{18,... | collective-permute-start | bytes 7077896 | tf_op jit(solution)/shard_map/ppermute | solution.py:443
  334.0 128.9 %collective-permute-start.44 = (bf16[2,2,2,2,24,3072]{5,4,0,1,3,2:T(8,128)(2,1)S(1)}, bf16[2,2,2,2,24,3072]{5,4,0,1,3,2:T(8,128)(2,1)S(1)}, u32[]{:S(2)}, u32[]{:S(2)}) collective-permute-start(bf16[2,2,2,2,24,3072]{5,4,0,1,3,2:T(8,128)(2,1)S(1)} %bitcast.380), channel_id=1, source_target_pairs={{0,2},{2,0},{4,6},{6,4},{8,10},{10,8},{12,14},{14,12},{16,18},{18,... | collective-permute-start | bytes 7077896 | tf_op jit(solution)/shard_map/ppermute | solution.py:443
  351.0 32.5 %collective-permute-start.24 = (bf16[2,2,2,2,24,768]{5,4,0,1,3,2:T(8,128)(2,1)}, bf16[2,2,2,2,24,768]{5,4,0,1,3,2:T(8,128)(2,1)}, u32[]{:S(2)}, u32[]{:S(2)}) collective-permute-start(bf16[2,2,2,2,24,768]{5,4,0,1,3,2:T(8,128)(2,1)} %bitcast.370), channel_id=1, source_target_pairs={{0,2},{2,0},{4,6},{6,4},{8,10},{10,8},{12,14},{14,12},{16,18},{18,... | collective-permute-start | bytes 1769480 | tf_op jit(solution)/shard_map/ppermute | solution.py:443
  367.7 13.7 %collective-permute-start.19 = (bf16[2,2,2,2,24,768]{5,4,0,1,3,2:T(8,128)(2,1)}, bf16[2,2,2,2,24,768]{5,4,0,1,3,2:T(8,128)(2,1)}, u32[]{:S(2)}, u32[]{:S(2)}) collective-permute-start(bf16[2,2,2,2,24,768]{5,4,0,1,3,2:T(8,128)(2,1)} %bitcast.371), channel_id=1, source_target_pairs={{0,2},{2,0},{4,6},{6,4},{8,10},{10,8},{12,14},{14,12},{16,18},{18,... | collective-permute-start | bytes 1769480 | tf_op jit(solution)/shard_map/ppermute | solution.py:443
  376.0 20.5 %collective-permute-start.3 = (bf16[512,768]{1,0:T(8,128)(2,1)S(1)}, bf16[512,768]{1,0:T(8,128)(2,1)S(1)}, u32[]{:S(2)}, u32[]{:S(2)}) collective-permute-start(bf16[512,768]{1,0:T(8,128)(2,1)S(1)} %copy-done.31), channel_id=1, source_target_pairs={{0,1},{1,0},{2,3},{3,2},{4,5},{5,4},{6,7},{7,6},{8,9},{9,8},{10,11... | collective-permute-start | bytes 2359304 | tf_op jit(solution)/shard_map/ppermute | solution.py:411
  381.4 29.6 %collective-permute-start.1 = (bf16[512,768]{1,0:T(8,128)(2,1)S(1)}, bf16[512,768]{1,0:T(8,128)(2,1)S(1)}, u32[]{:S(2)}, u32[]{:S(2)}) collective-permute-start(bf16[512,768]{1,0:T(8,128)(2,1)S(1)} %copy-done.21), channel_id=1, source_target_pairs={{0,1},{1,0},{2,3},{3,2},{4,5},{5,4},{6,7},{7,6},{8,9},{9,8},{10,11... | collective-permute-start | bytes 2359304 | tf_op jit(solution)/shard_map/ppermute | solution.py:411
  383.5 71.8 %collective-permute-start.9 = (bf16[2,2,2,2,72,768]{5,4,0,1,2,3:T(8,128)(2,1)S(1)}, bf16[2,2,2,2,72,768]{5,4,0,1,2,3:T(8,128)(2,1)S(1)}, u32[]{:S(2)}, u32[]{:S(2)}) collective-permute-start(bf16[2,2,2,2,72,768]{5,4,0,1,2,3:T(8,128)(2,1)S(1)} %bitcast.382), channel_id=1, source_target_pairs={{0,2},{2,0},{4,6},{6,4},{8,10},{10,8},{12,14},{14,12},{16,18},{18,... | collective-permute-start | bytes 5308424 | tf_op jit(solution)/shard_map/ppermute | solution.py:443
  396.5 60.8 %collective-permute-start.14 = (bf16[2,2,2,2,72,768]{5,4,0,1,3,2:T(8,128)(2,1)S(1)}, bf16[2,2,2,2,72,768]{5,4,0,1,3,2:T(8,128)(2,1)}, u32[]{:S(2)}, u32[]{:S(2)}) collective-permute-start(bf16[2,2,2,2,72,768]{5,4,0,1,3,2:T(8,128)(2,1)S(1)} %bitcast.381), channel_id=1, source_target_pairs={{0,2},{2,0},{4,6},{6,4},{8,10},{10,8},{12,14},{14,12},{16,18},{18,... | collective-permute-start | bytes 5308424 | tf_op jit(solution)/shard_map/ppermute | solution.py:443
  455.4 11.6 %collective-permute-start.34 = (bf16[2,2,2,2,96,768]{5,4,0,1,2,3:T(8,128)(2,1)S(1)}, bf16[2,2,2,2,96,768]{5,4,0,1,2,3:T(8,128)(2,1)S(1)}, u32[]{:S(2)}, u32[]{:S(2)}) collective-permute-start(bf16[2,2,2,2,96,768]{5,4,0,1,2,3:T(8,128)(2,1)S(1)} %bitcast.378), channel_id=1, source_target_pairs={{0,2},{2,0},{4,6},{6,4},{8,10},{10,8},{12,14},{14,12},{16,18},{18,... | collective-permute-start | bytes 7077896 | tf_op jit(solution)/shard_map/ppermute | solution.py:443
  457.3 22.7 %collective-permute-start.10 = (bf16[2,2,2,72,768]{4,3,0,1,2:T(8,128)(2,1)}, bf16[2,2,2,72,768]{4,3,0,1,2:T(8,128)(2,1)S(1)}, u32[]{:S(2)}, u32[]{:S(2)}) collective-permute-start(bf16[2,2,2,72,768]{4,3,0,1,2:T(8,128)(2,1)} %dynamic-slice_bitcast_fusion.5), channel_id=1, source_target_pairs={{0,1},{1,0},{2,3},{3,2},{4,5},{5,4},{6,7},{7,6},{8,9},{9,8},{10,11... | collective-permute-start | bytes 2654216 | tf_op jit(solution)/shard_map/ppermute | solution.py:439
  460.5 22.8 %collective-permute-start.15 = (bf16[2,2,2,72,768]{4,3,0,1,2:T(8,128)(2,1)}, bf16[2,2,2,72,768]{4,3,0,1,2:T(8,128)(2,1)S(1)}, u32[]{:S(2)}, u32[]{:S(2)}) collective-permute-start(bf16[2,2,2,72,768]{4,3,0,1,2:T(8,128)(2,1)} %dynamic-slice_bitcast_fusion.4), channel_id=1, source_target_pairs={{0,4},{2,6},{4,0},{6,2},{8,12},{10,14},{12,8},{14,10},{16,20},{18,... | collective-permute-start | bytes 2654216 | tf_op jit(solution)/shard_map/ppermute | solution.py:443
  463.0 108.9 %collective-permute-start.40 = (bf16[2,2,2,24,3072]{4,3,0,1,2:T(8,128)(2,1)S(1)}, bf16[2,2,2,24,3072]{4,3,0,1,2:T(8,128)(2,1)S(1)}, u32[]{:S(2)}, u32[]{:S(2)}) collective-permute-start(bf16[2,2,2,24,3072]{4,3,0,1,2:T(8,128)(2,1)S(1)} %dynamic-slice_bitcast_fusion.1), channel_id=1, source_target_pairs={{0,4},{2,6},{4,0},{6,2},{8,12},{10,14},{12,8},{14,10},{16,20},{18,... | collective-permute-start | bytes 3538952 | tf_op jit(solution)/shard_map/ppermute | solution.py:443
  464.6 109.0 %collective-permute-start.45 = (bf16[2,2,2,24,3072]{4,3,0,1,2:T(8,128)(2,1)S(1)}, bf16[2,2,2,24,3072]{4,3,0,1,2:T(8,128)(2,1)S(1)}, u32[]{:S(2)}, u32[]{:S(2)}) collective-permute-start(bf16[2,2,2,24,3072]{4,3,0,1,2:T(8,128)(2,1)S(1)} %dynamic-slice_bitcast_fusion), channel_id=1, source_target_pairs={{0,4},{2,6},{4,0},{6,2},{8,12},{10,14},{12,8},{14,10},{16,20},{18,... | collective-permute-start | bytes 3538952 | tf_op jit(solution)/shard_map/ppermute | solution.py:443
  467.0 108.0 %collective-permute-start.30 = (bf16[2,2,2,96,768]{4,3,0,1,2:T(8,128)(2,1)S(1)}, bf16[2,2,2,96,768]{4,3,0,1,2:T(8,128)(2,1)S(1)}, u32[]{:S(2)}, u32[]{:S(2)}) collective-permute-start(bf16[2,2,2,96,768]{4,3,0,1,2:T(8,128)(2,1)S(1)} %dynamic-slice_bitcast_fusion.3), channel_id=1, source_target_pairs={{0,1},{1,0},{2,3},{3,2},{4,5},{5,4},{6,7},{7,6},{8,9},{9,8},{10,11... | collective-permute-start | bytes 3538952 | tf_op jit(solution)/shard_map/ppermute | solution.py:439
  480.3 61.8 %collective-permute-start.11 = (bf16[2,2,72,768]{3,2,0,1:T(8,128)(2,1)S(1)}, bf16[2,2,72,768]{3,2,0,1:T(8,128)(2,1)S(1)}, u32[]{:S(2)}, u32[]{:S(2)}) collective-permute-start(bf16[2,2,72,768]{3,2,0,1:T(8,128)(2,1)S(1)} %dynamic-slice_bitcast_fusion.15), channel_id=1, source_target_pairs={{0,4},{2,6},{4,0},{6,2},{8,12},{10,14},{12,8},{14,10},{16,20},{18,... | collective-permute-start | bytes 1327112 | tf_op jit(solution)/shard_map/ppermute | solution.py:443
  483.5 60.4 %collective-permute-start.16 = (bf16[2,2,72,768]{3,2,0,1:T(8,128)(2,1)S(1)}, bf16[2,2,72,768]{3,2,0,1:T(8,128)(2,1)S(1)}, u32[]{:S(2)}, u32[]{:S(2)}) collective-permute-start(bf16[2,2,72,768]{3,2,0,1:T(8,128)(2,1)S(1)} %dynamic-slice_bitcast_fusion.14), channel_id=1, source_target_pairs={{0,1},{1,0},{2,3},{3,2},{4,5},{5,4},{6,7},{7,6},{8,9},{9,8},{10,11... | collective-permute-start | bytes 1327112 | tf_op jit(solution)/shard_map/ppermute | solution.py:439
  542.0 35.0 %collective-permute-start.35 = (bf16[2,2,2,96,768]{4,3,0,1,2:T(8,128)(2,1)S(1)}, bf16[2,2,2,96,768]{4,3,0,1,2:T(8,128)(2,1)S(1)}, u32[]{:S(2)}, u32[]{:S(2)}) collective-permute-start(bf16[2,2,2,96,768]{4,3,0,1,2:T(8,128)(2,1)S(1)} %dynamic-slice_bitcast_fusion.2), channel_id=1, source_target_pairs={{0,1},{1,0},{2,3},{3,2},{4,5},{5,4},{6,7},{7,6},{8,9},{9,8},{10,11... | collective-permute-start | bytes 3538952 | tf_op jit(solution)/shard_map/ppermute | solution.py:439
  572.4 15.4 %collective-permute-start.41 = (bf16[2,2,24,3072]{3,2,0,1:T(8,128)(2,1)S(1)}, bf16[2,2,24,3072]{3,2,0,1:T(8,128)(2,1)S(1)}, u32[]{:S(2)}, u32[]{:S(2)}) collective-permute-start(bf16[2,2,24,3072]{3,2,0,1:T(8,128)(2,1)S(1)} %dynamic-slice_bitcast_fusion.11), channel_id=1, source_target_pairs={{0,1},{1,0},{2,3},{3,2},{4,5},{5,4},{6,7},{7,6},{8,9},{9,8},{10,11... | collective-permute-start | bytes 1769480 | tf_op jit(solution)/shard_map/ppermute | solution.py:439
  574.0 20.1 %collective-permute-start.46 = (bf16[2,2,24,3072]{3,2,0,1:T(8,128)(2,1)S(1)}, bf16[2,2,24,3072]{3,2,0,1:T(8,128)(2,1)S(1)}, u32[]{:S(2)}, u32[]{:S(2)}) collective-permute-start(bf16[2,2,24,3072]{3,2,0,1:T(8,128)(2,1)S(1)} %dynamic-slice_bitcast_fusion.10), channel_id=1, source_target_pairs={{0,1},{1,0},{2,3},{3,2},{4,5},{5,4},{6,7},{7,6},{8,9},{9,8},{10,11... | collective-permute-start | bytes 1769480 | tf_op jit(solution)/shard_map/ppermute | solution.py:439
  575.4 20.4 %collective-permute-start.31 = (bf16[2,2,96,768]{3,2,0,1:T(8,128)(2,1)S(1)}, bf16[2,2,96,768]{3,2,0,1:T(8,128)(2,1)S(1)}, u32[]{:S(2)}, u32[]{:S(2)}) collective-permute-start(bf16[2,2,96,768]{3,2,0,1:T(8,128)(2,1)S(1)} %dynamic-slice_bitcast_fusion.13), channel_id=1, source_target_pairs={{0,4},{2,6},{4,0},{6,2},{8,12},{10,14},{12,8},{14,10},{16,20},{18,... | collective-permute-start | bytes 1769480 | tf_op jit(solution)/shard_map/ppermute | solution.py:443
  577.4 19.3 %collective-permute-start.36 = (bf16[2,2,96,768]{3,2,0,1:T(8,128)(2,1)S(1)}, bf16[2,2,96,768]{3,2,0,1:T(8,128)(2,1)S(1)}, u32[]{:S(2)}, u32[]{:S(2)}) collective-permute-start(bf16[2,2,96,768]{3,2,0,1:T(8,128)(2,1)S(1)} %dynamic-slice_bitcast_fusion.12), channel_id=1, source_target_pairs={{0,4},{2,6},{4,0},{6,2},{8,12},{10,14},{12,8},{14,10},{16,20},{18,... | collective-permute-start | bytes 1769480 | tf_op jit(solution)/shard_map/ppermute | solution.py:443
  588.0 11.5 %collective-permute-start.42 = (bf16[2,24,3072]{2,1,0:T(8,128)(2,1)S(1)}, bf16[2,24,3072]{2,1,0:T(8,128)(2,1)S(1)}, u32[]{:S(2)}, u32[]{:S(2)}) collective-permute-start(bf16[2,24,3072]{2,1,0:T(8,128)(2,1)S(1)} %dynamic-slice_bitcast_fusion.17), channel_id=1, source_target_pairs={{0,8},{2,10},{4,12},{6,14},{8,0},{10,2},{12,4},{14,6},{16,24},{18,... | collective-permute-start | bytes 884744 | tf_op jit(solution)/shard_map/ppermute | solution.py:443
  594.3 14.7 %collective-permute-start.47 = (bf16[2,24,3072]{2,1,0:T(8,128)(2,1)S(1)}, bf16[2,24,3072]{2,1,0:T(8,128)(2,1)S(1)}, u32[]{:S(2)}, u32[]{:S(2)}) collective-permute-start(bf16[2,24,3072]{2,1,0:T(8,128)(2,1)S(1)} %dynamic-slice_bitcast_fusion.16), channel_id=1, source_target_pairs={{0,8},{2,10},{4,12},{6,14},{8,0},{10,2},{12,4},{14,6},{16,24},{18,... | collective-permute-start | bytes 884744 | tf_op jit(solution)/shard_map/ppermute | solution.py:443
  596.0 21.3 %collective-permute-start.32 = (bf16[2,96,768]{2,1,0:T(8,128)(2,1)S(1)}, bf16[2,96,768]{2,1,0:T(8,128)(2,1)S(1)}, u32[]{:S(2)}, u32[]{:S(2)}) collective-permute-start(bf16[2,96,768]{2,1,0:T(8,128)(2,1)S(1)} %dynamic-slice_bitcast_fusion.19), channel_id=1, source_target_pairs={{0,8},{2,10},{4,12},{6,14},{8,0},{10,2},{12,4},{14,6},{16,24},{18,... | collective-permute-start | bytes 884744 | tf_op jit(solution)/shard_map/ppermute | solution.py:443
  596.9 23.9 %collective-permute-start.37 = (bf16[2,96,768]{2,1,0:T(8,128)(2,1)S(1)}, bf16[2,96,768]{2,1,0:T(8,128)(2,1)S(1)}, u32[]{:S(2)}, u32[]{:S(2)}) collective-permute-start(bf16[2,96,768]{2,1,0:T(8,128)(2,1)S(1)} %dynamic-slice_bitcast_fusion.18), channel_id=1, source_target_pairs={{0,8},{2,10},{4,12},{6,14},{8,0},{10,2},{12,4},{14,6},{16,24},{18,... | collective-permute-start | bytes 884744 | tf_op jit(solution)/shard_map/ppermute | solution.py:443
  599.6 22.7 %collective-permute-start.43 = (bf16[24,3072]{1,0:T(8,128)(2,1)S(1)}, bf16[24,3072]{1,0:T(8,128)(2,1)S(1)}, u32[]{:S(2)}, u32[]{:S(2)}) collective-permute-start(bf16[24,3072]{1,0:T(8,128)(2,1)S(1)} %dynamic-slice_bitcast_fusion.25), channel_id=1, source_target_pairs={{0,16},{2,18},{4,20},{6,22},{8,24},{10,26},{12,28},{14,30},{16,0},... | collective-permute-start | bytes 442376 | tf_op jit(solution)/shard_map/ppermute | solution.py:443
  609.1 13.3 %collective-permute-start.48 = (bf16[24,3072]{1,0:T(8,128)(2,1)S(1)}, bf16[24,3072]{1,0:T(8,128)(2,1)S(1)}, u32[]{:S(2)}, u32[]{:S(2)}) collective-permute-start(bf16[24,3072]{1,0:T(8,128)(2,1)S(1)} %dynamic-slice_bitcast_fusion.24), channel_id=1, source_target_pairs={{0,16},{2,18},{4,20},{6,22},{8,24},{10,26},{12,28},{14,30},{16,0},... | collective-permute-start | bytes 442376 | tf_op jit(solution)/shard_map/ppermute | solution.py:443
  617.4 13.7 %collective-permute-start.33 = (bf16[96,768]{1,0:T(8,128)(2,1)S(1)}, bf16[96,768]{1,0:T(8,128)(2,1)S(1)}, u32[]{:S(2)}, u32[]{:S(2)}) collective-permute-start(bf16[96,768]{1,0:T(8,128)(2,1)S(1)} %dynamic-slice_bitcast_fusion.27), channel_id=1, source_target_pairs={{0,16},{2,18},{4,20},{6,22},{8,24},{10,26},{12,28},{14,30},{16,0},... | collective-permute-start | bytes 442376 | tf_op jit(solution)/shard_map/ppermute | solution.py:443
  620.9 11.8 %collective-permute-start.38 = (bf16[96,768]{1,0:T(8,128)(2,1)S(1)}, bf16[96,768]{1,0:T(8,128)(2,1)S(1)}, u32[]{:S(2)}, u32[]{:S(2)}) collective-permute-start(bf16[96,768]{1,0:T(8,128)(2,1)S(1)} %dynamic-slice_bitcast_fusion.26), channel_id=1, source_target_pairs={{0,16},{2,18},{4,20},{6,22},{8,24},{10,26},{12,28},{14,30},{16,0},... | collective-permute-start | bytes 442376 | tf_op jit(solution)/shard_map/ppermute | solution.py:443
  (61 other events, 331.4 us)

commit v2 on v1

--- a/solution.py
+++ b/solution.py
@@ -30,11 +30,12 @@
 
 
 def mask_block(meta_ref, kaug, qone, tokens):
+    side = lax.axis_index("blk")
     rows = lax.broadcasted_iota(jnp.int32, (tokens, 128), 0)
     lanes = lax.broadcasted_iota(jnp.int32, (tokens, 128), 1)
     half = tokens // 2
-    position = jnp.where(rows < half, rows + meta_ref[1], rows - meta_ref[1])
-    masked = jnp.logical_and(lanes == 0, position >= meta_ref[0])
+    position = jnp.where(rows < half, rows + side * half, rows - side * half)
+    masked = jnp.logical_and(lanes == 0, position >= meta_ref[side])
     kaug[...] = jnp.where(masked, NEG, 0.0).astype(BF)
     qone[...] = jnp.where(lanes == 0, 1.0, 0.0).astype(BF)
 
@@ -118,7 +119,7 @@
 
 
 def attn_bwd_kernel(
-    meta_ref, q_ref, k_ref, v_ref, o_ref, low_ref, do_ref, lse_ref, dq_ref, dk_ref, dv_ref, kaug, qone
+    meta_ref, q_ref, k_ref, v_ref, o_ref, low_ref, do_ref, lse_ref, out_ref, kaug, qone
 ):
     tokens = q_ref.shape[0]
 
@@ -144,43 +145,62 @@
         dkh = dot_nn(ds, jnp.where(sel[h], q, zero))
         dqh = dot_nn(kh.T, ds)
         dq, dk, dv = (dqh, dkh, dvh) if h == 0 else (dq + dqh, dk + dkh, dv + dvh)
-    dq_ref[...] = (dq * (1.0 / math.sqrt(HEAD_DIM))).T.astype(BF)
-    dk_ref[...] = (dk * math.log(2.0)).astype(BF)
-    dv_ref[...] = dv.astype(BF)
-
-
-def attn_bwd(proj, mixed, low, g_mixed, lse, meta):
+    out_ref[0] = (dq * (1.0 / math.sqrt(HEAD_DIM))).T.astype(BF)
+    out_ref[1] = (dk * math.log(2.0)).astype(BF)
+    out_ref[2] = dv.astype(BF)
+
+
+def attn_bwd(proj, mixed, low, g_mixed, lse, meta, pairs, into=None, deps=()):
     tokens, width = mixed.shape
-    pairs = width // 128
-    spec = lambda off: pl.BlockSpec((tokens, 128), lambda i, m: (0, off + i))
+    count = width // 128
+    start, stop = pairs
+    spec = lambda off: pl.BlockSpec((tokens, 128), lambda i, m: (0, off + start + i))
+    ops = [meta, proj, proj, proj, mixed, low, g_mixed, lse]
+    specs = [spec(0), spec(count), spec(2 * count), spec(0), spec(0), spec(0)]
+    specs += [pl.BlockSpec((1, 8, tokens), lambda i, m: (start + i, 0, 0))]
+    extra = ([] if into is None else [into]) + list(deps)
     return pl.pallas_call(
-        attn_bwd_kernel,
+        ordered(attn_bwd_kernel, len(ops), extra),
         grid_spec=pltpu.PrefetchScalarGridSpec(
             num_scalar_prefetch=1,
-            grid=(pairs,),
-            in_specs=[spec(0), spec(pairs), spec(2 * pairs), spec(0), spec(0), spec(0)]
-            + [pl.BlockSpec((1, 8, tokens), lambda i, m: (i, 0, 0))],
-            out_specs=[spec(0)] * 3,
+            grid=(stop - start,),
+            in_specs=specs + anywhere(extra),
+            out_specs=pl.BlockSpec((3, tokens, 128), lambda i, m: (0, 0, start + i)),
             scratch_shapes=[pltpu.VMEM((tokens, 128), BF), pltpu.VMEM((tokens, 128), BF)],
         ),
-        out_shape=[jax.ShapeDtypeStruct((tokens, width), BF)] * 3,
+        out_shape=jax.ShapeDtypeStruct((3, tokens, width), BF),
+        input_output_aliases={} if into is None else {len(ops): 0},
         compiler_params=pltpu.CompilerParams(
             vmem_limit_bytes=56 << 20, dimension_semantics=("arbitrary",)
         ),
         cost_estimate=pl.CostEstimate(
-            flops=10 * tokens * tokens * width * 2,
-            bytes_accessed=tokens * width * 16,
-            transcendentals=pairs * 2 * tokens * tokens,
+            flops=20 * tokens * tokens * 128 * (stop - start),
+            bytes_accessed=tokens * 128 * (stop - start) * 18,
+            transcendentals=2 * (stop - start) * tokens * tokens,
         ),
         name="attn_bwd",
-    )(meta, proj, proj, proj, mixed, low, g_mixed, lse)
+    )(*ops, *extra)
 
 
 VMEM = pltpu.CompilerParams(vmem_limit_bytes=58 << 20, dimension_semantics=("arbitrary",))
 
 
-def whole(arr):
-    return pl.BlockSpec(arr.shape, lambda *_: (0,) * arr.ndim, pipeline_mode=pl.Buffered(1))
+def ordered(kernel, n_in, deps):
+    if not deps:
+        return kernel
+    return lambda *refs: kernel(*refs[:n_in], *refs[n_in + len(deps) :])
+
+
+def anywhere(arrays):
+    return [pl.BlockSpec(memory_space=pl.ANY)] * len(arrays)
+
+
+def layer(arr, d, n=0):
+    lead = arr.ndim - 2
+    index = (d, n)[:lead] + (0, 0)
+    return pl.BlockSpec(
+        (None,) * lead + arr.shape[lead:], lambda *_: index, pipeline_mode=pl.Buffered(1)
+    )
 
 
 def tile(rows, width, first=0):
@@ -208,6 +228,17 @@
         cols = slice(j * width, (j + 1) * width)
         part = dot_nn(n1, wqkv_ref[:, cols]) + bias_ref[:, cols]
         proj_ref[:, cols] = (part * factor).astype(BF)
+
+
+def attn_in(params, d):
+    arrays = [params["gains"], params["shifts"], params["wqkv"], params["bias"]]
+    return arrays, [layer(arrays[0], d, 0), layer(arrays[1], d, 0), layer(arrays[2], d), layer(arrays[3], d)]
+
+
+def ff_in(params, d):
+    names = ("wout", "bout", "gains", "shifts", "wup", "bup", "wdown", "bdown")
+    arrays = [params[n] for n in names]
+    return arrays, [layer(a, d, 1) for a in arrays]
 
 
 def enter_kernel(x_ref, gain_ref, shift_ref, wqkv_ref, bias_ref, *refs):
@@ -219,12 +250,13 @@
     project(n1, wqkv_ref, bias_ref, proj_ref, width)
 
 
-def enter(x, gain, shift, wqkv, bias, into, tokens, first):
+def enter(x, params, d, into, tokens, first):
     rows, width = x.shape
     block = 256
     at = first // block
-    ops = [x, gain, shift, wqkv, bias]
-    specs = [tile(block, width)] + [whole(a) for a in ops[1:]]
+    arrays, specs = attn_in(params, d)
+    ops = [x] + arrays
+    specs = [tile(block, width)] + specs
     alias = {}
     if into is not None:
         ops += list(into)
@@ -243,16 +275,31 @@
     )(*ops)
 
 
-def post_kernel(last, parts, *refs):
+def halves(tokens, block, width):
+    turn = tokens // block // 2
+    own = pl.BlockSpec((block, width), lambda i, *_: (jnp.minimum(i, turn - 1), 0))
+    other = pl.BlockSpec((block, width), lambda i, *_: (jnp.maximum(i - turn, 0), 0))
+    return [own, other]
+
+
+def joined(refs):
+    if len(refs) == 1:
+        return refs[0][...].astype(F32)
+    early = pl.program_id(0) < pl.num_programs(0) // 2
+    return jnp.where(early, refs[0][...].astype(F32), refs[1][...].astype(F32))
+
+
+def post_kernel(last, parts, n_x, *refs):
     it = iter(refs)
-    mixed_ref, x_ref = next(it), next(it)
+    mixed_ref = next(it)
+    x_refs = [next(it) for _ in range(n_x)]
     wout_ref, bout_ref, gain_ref, shift_ref = next(it), next(it), next(it), next(it)
     wup_ref, bup_ref, wdown_ref, bdown_ref = next(it), next(it), next(it), next(it)
     if not last:
         gain1_ref, shift1_ref, wqkv_ref, bias_ref = next(it), next(it), next(it), next(it)
     resid_ref, n2_ref, active_ref, slope_ref = next(it), next(it), next(it), next(it)
-    width = x_ref.shape[1]
-    resid = x_ref[...].astype(F32) + dot_nn(mixed_ref[...], wout_ref[...]) + bout_ref[...]
+    width = mixed_ref.shape[1]
+    resid = joined(x_refs) + dot_nn(mixed_ref[...], wout_ref[...]) + bout_ref[...]
     resid_ref[...] = resid
     xhat, _ = normalize(resid)
     n2 = (xhat * gain_ref[...] + shift_ref[...]).astype(BF)
@@ -279,19 +326,23 @@
         project(n1, wqkv_ref, bias_ref, proj_ref, width)
 
 
-def post(mixed, x, weights, following):
-    tokens, width = x.shape
+def post(mixed, xs, params, d, last):
+    tokens, width = mixed.shape
     block = 256
-    ff = weights[4].shape[1]
-    last = following is None
-    ops = [mixed, x] + list(weights) + ([] if last else list(following))
+    ff = params["wup"].shape[2]
+    arrays, specs = ff_in(params, d)
+    if not last:
+        more, more_specs = attn_in(params, d + 1)
+        arrays, specs = arrays + more, specs + more_specs
+    ops = [mixed] + list(xs) + arrays
+    x_specs = [tile(block, width)] if len(xs) == 1 else halves(tokens, block, width)
     outs = [(width, F32), (width, BF), (ff, BF), (ff, BF)]
     outs += [(width, BF)] if last else [(width, F32), (width, BF), (3 * width, BF)]
     flops = 2 * tokens * width * (width + 2 * ff + (0 if last else 3 * width))
     return pl.pallas_call(
-        functools.partial(post_kernel, last, 4),
+        functools.partial(post_kernel, last, 4, len(xs)),
         grid=(tokens // block,),
-        in_specs=[tile(block, width)] * 2 + [whole(a) for a in ops[2:]],
+        in_specs=[tile(block, width)] + x_specs + specs,
         out_specs=[tile(block, w) for w, _ in outs],
         out_shape=[sds(tokens, w, t) for w, t in outs],
         compiler_params=VMEM,
@@ -323,11 +374,13 @@
     return jnp.sum(x, 0, keepdims=True)
 
 
-def ff_back_kernel(parts, gx_ref, slope_ref, resid_ref, wdown_ref, wup_ref, wout_ref, gain_ref, *outs):
-    gy_ref, gu_ref, gres_ref, ga_ref, gmix_ref, vec_ref = outs
+def ff_back_kernel(parts, n_x, *refs):
+    gx_refs = refs[:n_x]
+    slope_ref, resid_ref, wdown_ref, wup_ref, wout_ref, gain_ref = refs[n_x : n_x + 6]
+    gy_ref, gu_ref, gres_ref, ga_ref, gmix_ref, vec_ref = refs[n_x + 6 :]
     fresh = pl.program_id(0) == 0
-    width = gx_ref.shape[1]
-    gx = gx_ref[...].astype(F32)
+    width = resid_ref.shape[1]
+    gx = joined(gx_refs)
     gy = gx.astype(BF)
     gy_ref[...] = gy
     hidden = wup_ref.shape[1] // parts
@@ -337,7 +390,6 @@
         g_act = dot_nt(gy, wdown_ref[cols, :])
         gu = (g_act * slope_ref[:, cols].astype(F32)).astype(BF)
         gu_ref[:, cols] = gu
-        add_row(vec_ref, 0, j * hidden, colsum(gu.astype(F32)), fresh)
         part = dot_nt(gu, wup_ref[:, cols])
         g_n2 = part if g_n2 is None else g_n2 + part
     xhat, rstd = normalize(resid_ref[...])
@@ -346,65 +398,535 @@
     ga = g_resid.astype(BF)
     ga_ref[...] = ga
     gmix_ref[...] = dot_nt(ga, wout_ref[...]).astype(BF)
-    add_row(vec_ref, 1, 0, colsum(g_n2 * xhat), fresh)
-    add_row(vec_ref, 1, width, colsum(g_n2), fresh)
-    add_row(vec_ref, 1, 2 * width, colsum(gy.astype(F32)), fresh)
-    add_row(vec_ref, 1, 3 * width, colsum(ga.astype(F32)), fresh)
-
-
-def ff_back(gx, slope, resid, wdown, wup, wout, gain):
+    add_row(vec_ref, 0, 0, colsum(g_n2 * xhat), fresh)
+    add_row(vec_ref, 0, width, colsum(g_n2), fresh)
+
+
+def ff_back(gxs, slope, resid, params, d, deps=()):
     tokens, width = resid.shape
     ff = slope.shape[1]
-    block = 256
+    block = 512
     outs = [(width, BF), (ff, BF), (width, F32), (width, BF), (width, BF)]
     assert ff == 4 * width
+    x_specs = [tile(block, width)] if len(gxs) == 1 else halves(tokens, block, width)
+    arrays = [params[n] for n in ("wdown", "wup", "wout", "gains")]
     return pl.pallas_call(
-        functools.partial(ff_back_kernel, 4),
+        ordered(functools.partial(ff_back_kernel, 4, len(gxs)), len(gxs) + 6, deps),
         grid=(tokens // block,),
-        in_specs=[tile(block, width), tile(block, ff), tile(block, width)]
-        + [whole(a) for a in (wdown, wup, wout, gain)],
-        out_specs=[tile(block, w) for w, _ in outs] + [pl.BlockSpec((8, ff), lambda i: (0, 0))],
-        out_shape=[sds(tokens, w, t) for w, t in outs] + [sds(8, ff, F32)],
+        in_specs=x_specs
+        + [tile(block, ff), tile(block, width)]
+        + [layer(a, d, 1) for a in arrays]
+        + anywhere(deps),
+        out_specs=[tile(block, w) for w, _ in outs] + [pl.BlockSpec((8, 2 * width), lambda i: (0, 0))],
+        out_shape=[sds(tokens, w, t) for w, t in outs] + [sds(8, 2 * width, F32)],
         compiler_params=VMEM,
         cost_estimate=cost(2 * tokens * width * (2 * ff + width), tokens * ff * 8),
         name="ff_back",
-    )(gx, slope, resid, wdown, wup, wout, gain)
-
-
-def qkv_back_kernel(dq_ref, dk_ref, dv_ref, wqkv_ref, x_ref, gres_ref, gain_ref, *refs):
+    )(*gxs, slope, resid, *arrays, *deps)
+
+
+def qkv_back_kernel(grads_ref, wqkv_ref, x_ref, gres_ref, gain_ref, *refs):
     gx_ref, vec_ref = refs[-2:]
     fresh = pl.program_id(0) == 0
     width = x_ref.shape[1]
-    grads = [dq_ref[...], dk_ref[...], dv_ref[...]]
+    grads = [grads_ref[n] for n in range(3)]
     g_norm = dot_nt(jnp.concatenate(grads, 1), wqkv_ref[...])
     xhat, rstd = normalize(x_ref[...].astype(F32))
     gx = gres_ref[...] + norm_back(g_norm, xhat, rstd, gain_ref[...])
     gx_ref[...] = gx.astype(gx_ref.dtype)
     add_row(vec_ref, 0, 0, colsum(g_norm * xhat), fresh)
     add_row(vec_ref, 0, width, colsum(g_norm), fresh)
-    add_row(vec_ref, 0, 2 * width, colsum(grads[0].astype(F32)), fresh)
-    add_row(vec_ref, 0, 3 * width, colsum(grads[2].astype(F32)), fresh)
-
-
-def qkv_back(grads, wqkv, x, x_first, g_resid, gain, first, rows, dtype):
+
+
+def qkv_back(grads, x, g_resid, params, d, first, rows, dtype, deps=()):
     width = x.shape[1]
     block = 256
     at = first // block
     return pl.pallas_call(
-        qkv_back_kernel,
+        ordered(qkv_back_kernel, 5, deps),
         grid=(rows // block,),
-        in_specs=[tile(block, width, at)] * 3
-        + [whole(wqkv), tile(block, width, x_first // block), tile(block, width, at), whole(gain)],
-        out_specs=[tile(block, width), pl.BlockSpec((8, 4 * width), lambda i: (0, 0))],
-        out_shape=[sds(rows, width, dtype), sds(8, 4 * width, F32)],
+        in_specs=[
+            pl.BlockSpec((3, block, width), lambda i: (0, at + i, 0)),
+            layer(params["wqkv"], d),
+            tile(block, width),
+            tile(block, width, at),
+            layer(params["gains"], d, 0),
+            *anywhere(deps),
+        ],
+        out_specs=[tile(block, width), pl.BlockSpec((8, 2 * width), lambda i: (0, 0))],
+        out_shape=[sds(rows, width, dtype), sds(8, 2 * width, F32)],
         compiler_params=VMEM,
         cost_estimate=cost(6 * rows * width * width, rows * width * 20),
         name="qkv_back",
-    )(*grads, wqkv, x, g_resid, gain)
+    )(grads, params["wqkv"], x, g_resid, params["gains"], *deps)
 
 
 def plain_grad(lefts, right):
     return jnp.concatenate([dot_tn(left, right) for left in lefts], 0).astype(BF)
+
+
+def deal(left_ref, right_ref, rows, start, refs, at):
+    total = left_ref.shape[1]
+
+    def store(mine):
+        result = dot_tn(left_ref[...], right_ref[...])
+        place = (lambda o: o) if mine is None else chunk_of
+        owner = start // rows
+        base = 0 if refs[0].shape[0] == place(31) + 1 else place(owner)
+        while owner * rows < start + total:
+            low = max(owner * rows, start)
+            high = min((owner + 1) * rows, start + total)
+            ref = refs[0] if mine is None or (owner >> 1) & 1 == mine else refs[1]
+            to = at + low - owner * rows
+            ref[place(owner) - base, to : to + high - low, :] = result[
+                low - start : high - start
+            ].astype(BF)
+            owner += 1
+
+    if len(refs) == 1:
+        store(None)
+        return
+    core = lax.axis_index("dp") & 1
+    for mine in range(2):
+        pl.when(core == mine)(functools.partial(store, mine))
+
+
+def chunk_of(owner):
+    return (owner >> 2) * 2 + (owner & 1)
+
+
+def grad_kernel(rows, by_left, n_out, left_ref, right_ref, *refs):
+    sum_ref = refs[-1]
+    deal(left_ref, right_ref, rows, 0, refs[-1 - n_out : -1], 0)
+
+    @pl.when(jnp.logical_or(by_left, pl.program_id(0) == 0))
+    def _():
+        sum_ref[...] = jnp.broadcast_to(colsum(left_ref[...].astype(F32)), sum_ref.shape)
+
+
+def grad_call(left, right, into, total, rows, offset, by_left, n_out=2, deps=()):
+    tokens, wide = left.shape
+    block = 768
+    places = 32 // n_out
+    deep = right.shape[1]
+    if by_left:
+        steps = wide // block
+        lspec = pl.BlockSpec((tokens, block), lambda i: (0, i))
+        rspec = pl.BlockSpec((tokens, block), lambda i: (0, 0))
+        out = pl.BlockSpec((places // steps, rows, block), lambda i: (i, offset // rows, 0))
+        sums = pl.BlockSpec((8, block), lambda i: (0, i))
+    else:
+        steps = deep // block
+        lspec = pl.BlockSpec((tokens, block), lambda i: (0, 0))
+        rspec = pl.BlockSpec((tokens, block), lambda i: (0, i))
+        out = pl.BlockSpec((places, rows, block), lambda i: (0, offset // rows + i, 0))
+        sums = pl.BlockSpec((8, block), lambda i: (0, 0))
+    extra = list(into or ()) + list(deps)
+    shape = jax.ShapeDtypeStruct((places, total, block), BF)
+    return pl.pallas_call(
+        functools.partial(grad_kernel, rows, by_left, n_out),
+        grid=(steps,),
+        in_specs=[lspec, rspec] + anywhere(extra),
+        out_specs=[out] * n_out + [sums],
+        out_shape=[shape] * n_out + [sds(8, wide, F32)],
+        input_output_aliases={2 + n: n for n in range(len(into or ()))},
+        compiler_params=VMEM,
+        cost_estimate=cost(2 * tokens * wide * deep, 2 * (tokens + 16) * (wide + deep)),
+        name="grad",
+    )(left, right, *extra)
+
+
+def qkv_grad_kernel(rows, n_out, left_ref, right_ref, *refs):
+    sum_ref = refs[-1]
+    step = pl.program_id(0)
+    for n in range(3):
+
+        @pl.when(step == n)
+        def _():
+            deal(left_ref, right_ref, rows, n * left_ref.shape[1], refs[-1 - n_out : -1], 0)
+
+    sum_ref[...] = jnp.broadcast_to(colsum(left_ref[...].astype(F32)), sum_ref.shape)
+
+
+def qkv_grad(grads, n1, into, total, n_out=2, deps=()):
+    _, tokens, width = grads.shape
+    rows = 3 * width // 32
+    places = 32 // n_out
+    extra = list(into or ()) + list(deps)
+    shape = jax.ShapeDtypeStruct((places, total, width), BF)
+    out = pl.BlockSpec((places, rows, width), lambda i: (0, total // rows - 1, 0))
+    return pl.pallas_call(
+        functools.partial(qkv_grad_kernel, rows, n_out),
+        grid=(3,),
+        in_specs=[
+            pl.BlockSpec((None, tokens, width), lambda i: (i, 0, 0)),
+            pl.BlockSpec((tokens, width), lambda i: (0, 0)),
+        ]
+        + anywhere(extra),
+        out_specs=[out] * n_out + [pl.BlockSpec((8, width), lambda i: (0, i))],
+        out_shape=[shape] * n_out + [sds(8, 3 * width, F32)],
+        input_output_aliases={2 + n: n for n in range(len(into or ()))},
+        compiler_params=VMEM,
+        cost_estimate=cost(6 * tokens * width * width, 16 * tokens * width),
+        name="qkv_grad",
+    )(grads, n1, *extra)
+
+
+ROWS = 512
+
+
+def ff_all_kernel(n_x, n_out, firsts, d, *refs):
+    it = iter(refs)
+    gx_refs = [next(it) for _ in range(n_x)]
+    slope_ref, resid_ref, gain_ref, active_ref = next(it), next(it), next(it), next(it)
+    sources = [next(it) for _ in range(5)]
+    refs = list(it)
+    gres_ref, gmix_ref, vec_ref = refs[-16 - n_out : -13 - n_out]
+    bufs = refs[-13 - n_out : -13]
+    wdown, wup, wout, n2, mixed, gy_all, gu_all, ga_all, down, up, out, arrive, leave = refs[-13:]
+    step = pl.program_id(0)
+    tokens, width = gy_all.shape
+    parts = wup.shape[1] // width
+    blocks = tokens // ROWS
+    thin = width // 32
+    core = lax.axis_index("dp") & 1
+
+    def load(n):
+        j = n // 2
+        rows = pl.ds(j * width, width)
+        if j < parts and n % 2 == 0:
+            pair = sources[0].at[d, rows], wdown.at[rows]
+        elif j < parts:
+            pair = sources[1].at[d, :, rows], wup.at[:, rows]
+        else:
+            late = n - 2 * parts
+            pair = (sources[2].at[d], sources[3], sources[4])[late], (wout, n2, mixed)[late]
+        return pltpu.make_async_copy(*pair, arrive.at[n])
+
+    def arrived(n):
+        pl.when(step == 0)(lambda: load(n).wait())
+
+    @pl.when(step == 0)
+    def _():
+        for n in range(2 * parts + 3):
+            load(n).start()
+
+    def stores(kind, j):
+        slot = j % 2
+        if kind == "up":
+            held, row, count, tall, place = up, firsts + 4 * thin, 8, 4 * thin, 8 * j
+        else:
+            held = down if kind == "down" else out
+            row, count, tall, place = firsts + (j if kind == "down" else 8) * thin, 32, thin, 0
+        sem = {"down": 0, "up": 4, "out": 8}[kind] + 2 * slot
+        rows = pl.ds(row, tall)
+        if n_out == 1:
+            dst = bufs[0].at[pl.ds(place, count), rows]
+            return [pltpu.make_async_copy(held.at[slot], dst, leave.at[sem])]
+        part = count // 2
+        found = []
+        for n, buf in enumerate(bufs):
+            src = held.at[slot, pl.ds((core if n == 0 else 1 - core) * part, part)]
+            dst = buf.at[pl.ds(place // 2, part), rows]
+            found.append(pltpu.make_async_copy(src, dst, leave.at[sem + n]))
+        return found
+
+    def put(held, slot, result):
+        count, tall = held.shape[1], held.shape[2]
+        for owner in range(count):
+            at = owner if n_out == 1 else ((owner >> 1) & 1) * (count // 2) + chunk_of(owner)
+            held[slot, at] = result[owner * tall : (owner + 1) * tall].astype(BF)
+
+    @pl.when(step < blocks)
+    def _():
+        rows = pl.ds(pl.multiple_of(step * ROWS, ROWS), ROWS)
+        fresh = step == 0
+        gx = joined_rows(gx_refs, step)
+        gy = gx.astype(BF)
+        gy_all[rows, :] = gy
+        g_n2 = None
+        for j in range(parts):
+            cols = slice(j * width, (j + 1) * width)
+            arrived(2 * j)
+            g_act = dot_nt(gy, wdown[cols, :])
+            gu = (g_act * slope_ref[:, cols].astype(F32)).astype(BF)
+            gu_all[rows, cols] = gu
+            arrived(2 * j + 1)
+            part = dot_nt(gu, wup[:, cols])
+            g_n2 = part if g_n2 is None else g_n2 + part
+        xhat, rstd = normalize(resid_ref[...])
+        g_resid = gx + norm_back(g_n2, xhat, rstd, gain_ref[...])
+        gres_ref[...] = g_resid
+        ga = g_resid.astype(BF)
+        ga_all[rows, :] = ga
+        arrived(2 * parts)
+        gmix_ref[...] = dot_nt(ga, wout[...]).astype(BF)
+        add_row(vec_ref, 0, 0, colsum(g_n2 * xhat), fresh)
+        add_row(vec_ref, 0, width, colsum(g_n2), fresh)
+        add_row(vec_ref, 0, 2 * width, colsum(gy.astype(F32)), fresh)
+        add_row(vec_ref, 0, 3 * width, colsum(ga.astype(F32)), fresh)
+
+    arrived(2 * parts + 1)
+    arrived(2 * parts + 2)
+    for j in range(parts):
+
+        @pl.when(step == blocks + j)
+        def _():
+            if j >= 2:
+                for copy in stores("down", j - 2):
+                    copy.wait()
+            put(down, j % 2, dot_tn(gy_all[...], active_ref[...]))
+            for copy in stores("down", j):
+                copy.start()
+
+        @pl.when(step == blocks + parts + j)
+        def _():
+            if j >= 2:
+                for copy in stores("up", j - 2):
+                    copy.wait()
+            cols = slice(j * width, (j + 1) * width)
+            left = gu_all[:, cols]
+            put(up, j % 2, dot_tn(left, n2[...]))
+            vec_ref[1:2, cols] = colsum(left.astype(F32))
+            for copy in stores("up", j):
+                copy.start()
+
+    @pl.when(step == blocks + 2 * parts)
+    def _():
+        put(out, 0, dot_tn(ga_all[...], mixed[...]))
+        for copy in stores("out", 0):
+            copy.start()
+        for kind, first, count in (("down", parts - 2, 2), ("up", parts - 2, 2), ("out", 0, 1)):
+            for j in range(first, first + count):
+                for copy in stores(kind, j):
+                    copy.wait()
+
+
+def joined_rows(refs, step):
+    if len(refs) == 1:
+        return refs[0][...].astype(F32)
+    return jnp.where(step == 0, refs[0][...].astype(F32), refs[1][...].astype(F32))
+
+
+def ff_all(gxs, slope, resid, active, n2, mixed, params, d, into, total, n_out):
+    tokens, width = resid.shape
+    ff = slope.shape[1]
+    parts, blocks = ff // width, tokens // ROWS
+    thin = width // 32
+    early = lambda i: jnp.minimum(i, blocks - 1)
+    row = lambda w: pl.BlockSpec((ROWS, w), lambda i: (early(i), 0))
+    if len(gxs) == 1:
+        x_specs = [row(width)]
+    else:
+        x_specs = [pl.BlockSpec((ROWS, width), lambda i: (0, 0), pipeline_mode=pl.Buffered(1))] * 2
+    weights = [params[n] for n in ("wdown", "wup", "wout")]
+    ops = [*gxs, slope, resid, params["gains"], active, *weights, n2, mixed]
+    specs = x_specs + [
+        row(ff),
+        row(width),
+        layer(params["gains"], d, 1),
+        pl.BlockSpec((tokens, width), lambda i: (0, jnp.clip(i - blocks, 0, parts - 1))),
+    ]
+    extra = list(into or ())
+    specs += anywhere(ops[len(specs) :]) + anywhere(extra)
+    shape = jax.ShapeDtypeStruct((32 // n_out, total, width), BF)
+    vec = pl.BlockSpec((8, ff), lambda i: (0, 0))
+    vm = pltpu.VMEM
+    scratch = [vm((ff, width), BF), vm((width, ff), BF), vm((width, width), BF)]
+    scratch += [vm((tokens, width), BF)] * 3 + [vm((tokens, ff), BF), vm((tokens, width), BF)]
+    scratch += [vm((2, 32, thin, width), BF), vm((2, 8, 4 * thin, width), BF), vm((1, 32, thin, width), BF)]
+    scratch += [pltpu.SemaphoreType.DMA((2 * parts + 3,)), pltpu.SemaphoreType.DMA((12,))]
+    flops = 2 * tokens * width * (4 * ff + 2 * width)
+    return pl.pallas_call(
+        functools.partial(ff_all_kernel, len(gxs), n_out, 0, d),
+        grid=(blocks + 2 * parts + 1,),
+        in_specs=specs,
+        out_specs=[row(width), row(width), vec] + [pl.BlockSpec(memory_space=pl.ANY)] * n_out,
+        out_shape=[sds(tokens, width, F32), sds(tokens, width, BF), sds(8, ff, F32)] + [shape] * n_out,
+        input_output_aliases={len(ops) + n: 3 + n for n in range(len(extra))},
+        scratch_shapes=scratch,
+        compiler_params=pltpu.CompilerParams(
+            vmem_limit_bytes=63 << 20, dimension_semantics=("arbitrary",)
+        ),
+        cost_estimate=cost(flops, 50 << 20),
+        name="ff_all",
+    )(*ops, *extra)
+
+
+def plus(*parts):
+    total = parts[0].astype(F32)
+    for part in parts[1:]:
+        total = total + part.astype(F32)
+    return total
+
+
+def place_xy():
+    return (lax.axis_index("dp") >> 1) & 1, lax.axis_index("blk")
+
+
+def stage1_kernel(tall, has_vec, keep, recv, *refs):
+    kp, sp, kq, sq = refs[-4:]
+    x, y = place_xy()
+    both = lambda a, b, rows: plus(keep[0, a, b, rows], recv[0, a, b, rows]).astype(BF)
+    up, low = slice(0, tall), slice(tall, keep.shape[3])
+    stop = keep.shape[3] - tall
+    for n in range(2):
+        kp[0, n] = both(x, n, up)
+        sp[0, n] = both(1 - x, n, up)
+        kq[0, n, :stop] = both(n, y, low)
+        sq[0, n, :stop] = both(n, 1 - y, low)
+    if has_vec:
+        vk, vr = refs[:2]
+        for n in range(2):
+            kq[0, n, stop:] = plus(vk[0, n, y], vr[0, n, y]).astype(BF)
+            sq[0, n, stop:] = plus(vk[0, n, 1 - y], vr[0, n, 1 - y]).astype(BF)
+
+
+def stage2_kernel(kp, rp, kq, rq, kp2, sp2, kq2, sq2):
+    x, y = place_xy()
+    kp2[0] = plus(kp[0, y], rp[0, y]).astype(BF)
+    sp2[0] = plus(kp[0, 1 - y], rp[0, 1 - y]).astype(BF)
+    kq2[0] = plus(kq[0, x], rq[0, x]).astype(BF)
+    sq2[0] = plus(kq[0, 1 - x], rq[0, 1 - x]).astype(BF)
+
+
+def stage3_kernel(kp, rp, kq, rq, own, *sends):
+    tall = kp.shape[1]
+    z = lax.axis_index("dp") >> 2
+    for n, ref in enumerate((own,) + sends):
+        at = z ^ n
+        ref[:tall, :] = plus(kp[at], rp[at]).astype(ref.dtype)
+        ref[tall:, :] = plus(kq[at], rq[at]).astype(ref.dtype)
+
+
+def stage_call(kernel, name, ops, outs, deps):
+    nbytes = sum(math.prod(a.shape) * 2 for a in ops) + sum(math.prod(s) * 2 for s in outs)
+    spec = lambda shape: pl.BlockSpec((1,) + shape[1:], lambda i: (i,) + (0,) * (len(shape) - 1))
+    return pl.pallas_call(
+        ordered(kernel, len(ops), deps),
+        grid=(ops[0].shape[0],),
+        in_specs=[spec(a.shape) for a in ops] + anywhere(deps),
+        out_specs=[spec(s) for s in outs],
+        out_shape=[jax.ShapeDtypeStruct(s, BF) for s in outs],
+        compiler_params=VMEM,
+        cost_estimate=cost(nbytes, nbytes),
+        name=name,
+    )(*ops, *deps)
+
+
+def xor_permute(x, dp, mask):
+    return lax.ppermute(x, "dp", [(i, i ^ mask) for i in range(dp)])
+
+
+class Group:
+    def __init__(self, keep, send, tall, dp):
+        self.tall, self.dp = tall, dp
+        self.keep, self.recv = keep, xor_permute(send, dp, 1)
+
+    def stage1(self, vec=None, deps=()):
+        _, total, width = self.keep.shape
+        tall = self.tall
+        cut = lambda a: a.reshape(4, 2, 2, a.shape[1], width)
+        ops = [cut(self.keep), cut(self.recv)]
+        low = total - tall
+        if vec is not None:
+            ops += [cut(v) for v in vec]
+            low += vec[0].shape[1]
+        p, q = (4, 2, tall, width), (4, 2, low, width)
+        kernel = functools.partial(stage1_kernel, tall, vec is not None)
+        self.kp, sp, self.kq, sq = stage_call(kernel, "stage1", ops, [p, p, q, q], deps)
+        self.rp, self.rq = xor_permute(sp, self.dp, 2), swap_halves(sq)
+        return [self.kp]
+
+    def stage2(self, deps=()):
+        p, q = [(4,) + a.shape[2:] for a in (self.kp, self.kq)]
+        ops = [self.kp, self.rp, self.kq, self.rq]
+        self.kp, sp, self.kq, sq = stage_call(stage2_kernel, "stage2", ops, [p, p, q, q], deps)
+        self.rp, self.rq = swap_halves(sp), xor_permute(sq, self.dp, 2)
+        return [self.kp]
+
+    def stage3(self, deps=()):
+        ops = [self.kp, self.rp, self.kq, self.rq]
+        total, width = self.kp.shape[1] + self.kq.shape[1], self.kp.shape[2]
+        nbytes = total * width * 24
+        pieces = pl.pallas_call(
+            ordered(stage3_kernel, 4, deps),
+            grid=(1,),
+            in_specs=[pl.BlockSpec(a.shape, lambda i: (0, 0, 0)) for a in ops] + anywhere(deps),
+            out_specs=[pl.BlockSpec((total, width), lambda i: (0, 0))] * 4,
+            out_shape=[sds(total, width, F32)] + [sds(total, width, BF)] * 3,
+            compiler_params=VMEM,
+            cost_estimate=cost(nbytes, nbytes),
+            name="stage3",
+        )(*ops, *deps)
+        moved = [xor_permute(pieces[n], self.dp, n << 2) for n in range(1, 4)]
+        self.pieces = [pieces[0]] + moved
+        return [pieces[0]]
+
+
+def final_kernel(layout, counts, *refs):
+    groups = []
+    for count in counts:
+        groups.append(refs[:count])
+        refs = refs[count:]
+    outs = dict(zip(layout["outs"], refs))
+    width = groups[0][0].shape[1]
+
+    def rows(group, start, count):
+        return plus(*(ref[start : start + count, :] for ref in groups[group]))
+
+    for d in range(LAYERS):
+        place = layout["rows"][d]
+        for name in ("qkv", "out", "up"):
+            outs[name][d] = rows(*place[name])
+        down = rows(*place["down"])
+        thin = outs["down"].shape[1]
+        for j in range(down.shape[0] // thin):
+            outs["down"][d, :, j * width : (j + 1) * width] = down[j * thin : (j + 1) * thin]
+    vec = rows(*layout["vec"])[0:1]
+    at = 0
+    for d in range(LAYERS):
+        for name, n in layout["vectors"]:
+            ref = outs[name]
+            size = ref.shape[-1]
+            value = vec[:, at : at + size]
+            if n is None:
+                ref[d : d + 1, :] = value
+            else:
+                ref[d, n : n + 1, :] = value
+            at += size
+
+
+VECTORS = (
+    ("gains", 0),
+    ("gains", 1),
+    ("shifts", 0),
+    ("shifts", 1),
+    ("bq", None),
+    ("bv", None),
+    ("bout", None),
+    ("bdown", None),
+    ("bup", None),
+)
+
+
+def finish(layout, groups, shapes):
+    ops = [a for g in groups for a in g]
+    names = list(shapes)
+    layout = dict(layout, outs=names, vectors=VECTORS)
+    total = sum(math.prod(a.shape) for a in ops) * 2
+    return dict(
+        zip(
+            names,
+            pl.pallas_call(
+                functools.partial(final_kernel, layout, [len(g) for g in groups]),
+                out_shape=[jax.ShapeDtypeStruct(shapes[n], F32) for n in names],
+                compiler_params=pltpu.CompilerParams(vmem_limit_bytes=58 << 20),
+                cost_estimate=cost(total, total),
+                name="finish",
+            )(*ops),
+        )
+    )
 
 
 def swap_halves(x):
@@ -449,6 +971,34 @@
         return arr
 
 
+class PlainSums:
+    def __init__(self, mesh):
+        self.halving = Halving(mesh)
+        self.held = {}
+
+    def add(self, name, d, lefts, right, blk_first):
+        self.held[name, d] = self.halving.run(plain_grad(lefts, right), blk_first)
+
+    def results(self, vec):
+        vec = self.halving.run(vec, False, wide=True)[0]
+        out = {
+            n: jnp.stack([self.held[n, d].T for d in range(LAYERS)])
+            for n in ("qkv", "out", "up", "down")
+        }
+        thin = vec.shape[0] // (12 * LAYERS)
+        at = 0
+        found = {}
+        for d in range(LAYERS):
+            for name, n in VECTORS:
+                size = 4 * thin if name == "bup" else thin
+                found.setdefault((name, d), []).append(vec[at : at + size])
+                at += size
+        for name in dict(VECTORS):
+            rows = [jnp.stack(found[name, d]) for d in range(LAYERS)]
+            out[name] = jnp.stack(rows if len(rows[0]) == 2 else [r[0] for r in rows])
+        return out
+
+
 def shards(
     mesh,
     hidden_in,
@@ -468,12 +1018,12 @@
 ):
     cells, half, width = hidden_in.shape
     tokens = cells * half
-    halving = Halving(mesh)
-    assert cells == halving.blk
-    owners = halving.dp * halving.blk
+    dp, blk = mesh.shape["dp"], mesh.shape["blk"]
+    owners = dp * blk
+    assert cells == blk == 2
     side = lax.axis_index("blk")
-    meta = jnp.stack([lax.dynamic_index_in_dim(cell_lengths, side, 0, False), side * half])
-    meta = meta.astype(jnp.int32)
+    meta = cell_lengths
+    grouped = dp == 16 and width == 768 and b_up.shape[1] == 4 * width
 
     def split_cell(both):
         own = lax.dynamic_index_in_dim(both, side, 0, False)
@@ -483,98 +1033,165 @@
     def return_cell(own, back):
         return jnp.where(side == 0, jnp.stack([own, back]), jnp.stack([back, own]))
 
-    row = lambda v: v[None, :]
-    biases = [
-        row(jnp.concatenate([b_query[d], jnp.zeros_like(b_query[d]), b_value[d]]))
-        for d in range(LAYERS)
-    ]
-    first = [(row(ln_gains[d, 0]), row(ln_biases[d, 0]), w_qkv[d], biases[d]) for d in range(LAYERS)]
+    rows = lambda v: v[..., None, :]
+    params = {
+        "gains": rows(ln_gains),
+        "shifts": rows(ln_biases),
+        "wqkv": w_qkv,
+        "bias": rows(jnp.concatenate([b_query, jnp.zeros_like(b_query), b_value], 1)),
+        "wout": w_out,
+        "bout": rows(b_out),
+        "wup": w_up,
+        "bup": rows(b_up),
+        "wdown": w_down,
+        "bdown": rows(b_down),
+    }
     own, other = split_cell(hidden_in)
-    entered = enter(own, *first[0], None, tokens, 0)
-    n1, proj = enter(other, *first[0], entered, tokens, half)
-    carried = jnp.concatenate([own, other], 0)
+    entered = enter(own, params, 0, None, tokens, 0)
+    n1, proj = enter(other, params, 0, entered, tokens, half)
+    xs = (own, other)
     saved = []
     for d in range(LAYERS):
         mixed, low, lse = attn_fwd(proj, meta)
-        weights = (
-            w_out[d],
-            row(b_out[d]),
-            row(ln_gains[d, 1]),
-            row(ln_biases[d, 1]),
-            w_up[d],
-            row(b_up[d]),
-            w_down[d],
-            row(b_down[d]),
+        last = d + 1 == LAYERS
+        outs = post(mixed, xs, params, d, last)
+        saved.append((xs, n1, proj, mixed, low, lse) + tuple(outs[:4]))
+        if not last:
+            x, n1, proj = outs[4:]
+            xs = (x,)
+    out16 = outs[4]
+    returned = swap_halves(out16[half:])
+    hidden_out = return_cell(out16[:half], returned)
+
+    gxs = split_cell(cotangent)
+    backward = backward_grouped if grouped else backward_plain
+    gx, out = backward(mesh, params, saved, gxs, meta, [returned])
+    grad_in = return_cell(gx[0], gx[1].astype(F32))
+    order = ("gains", "shifts", "qkv", "bq", "bv", "out", "bout", "up", "bup", "down", "bdown")
+    return (hidden_out, grad_in) + tuple(out[n] for n in order)
+
+
+def vector_rows(owners, width, ln1, ln2, sums):
+    flat = []
+    for d in range(LAYERS):
+        for v in (
+            ln1[d][:width],
+            ln2[d][:width],
+            ln1[d][width:],
+            ln2[d][width:],
+            sums["qkv", d][:width],
+            sums["qkv", d][2 * width :],
+            sums["out", d],
+            sums["down", d],
+            sums["up", d],
+        ):
+            flat.append(v.reshape(owners, -1))
+    return jnp.concatenate(flat, 1)
+
+
+def backward_plain(mesh, params, saved, gxs, meta, early):
+    sums = PlainSums(mesh)
+    ln1, ln2, cols = {}, {}, {}
+    for d in reversed(range(LAYERS)):
+        xs, n1, proj, mixed, low, lse, resid, n2, active, slope = saved[d]
+        tokens, width = resid.shape
+        gy, gu, g_resid, ga, g_mixed, vec2 = ff_back(gxs, slope, resid, params, d)
+        sums.add("down", d, [gy], active, False)
+        sums.add("up", d, [gu], n2, True)
+        sums.add("out", d, [ga], mixed, False)
+        grads = attn_bwd(proj, mixed, low, g_mixed, lse, meta, (0, width // 128))
+        sums.add("qkv", d, [grads[n] for n in range(3)], n1, True)
+        total = lambda a: jnp.sum(a.astype(F32), 0)
+        cols.update({("down", d): total(gy), ("up", d): total(gu), ("out", d): total(ga)})
+        cols["qkv", d] = jnp.concatenate([total(grads[n]) for n in range(3)])
+        ln2[d] = vec2[0]
+        if d > 0:
+            gx, vec1 = qkv_back(grads, xs[0], g_resid, params, d, 0, tokens, F32)
+            gxs = (gx,)
+            ln1[d] = vec1[0]
+        else:
+            half = tokens // 2
+            theirs, vec_a = qkv_back(grads, xs[1], g_resid, params, d, half, half, BF)
+            mine, vec_b = qkv_back(grads, xs[0], g_resid, params, d, 0, half, F32)
+            ln1[d] = vec_a[0] + vec_b[0]
+    owners = mesh.shape["dp"] * mesh.shape["blk"]
+    out = sums.results(vector_rows(owners, width, ln1, ln2, cols))
+    return (mine, swap_halves(theirs)), out
+
+
+def backward_grouped(mesh, params, saved, gxs, meta, early):
+    dp = mesh.shape["dp"]
+    ln1, ln2, cols = {}, {}, {}
+    tokens, width = saved[0][6].shape
+    half, t, pairs = tokens // 2, width // 32, width // 128
+
+    def ff_grads(gxs, d, into, total, n_out):
+        mixed, resid, n2, active, slope = saved[d][3], *saved[d][6:]
+        g_resid, g_mixed, vec, *bufs = ff_all(
+            gxs, slope, resid, active, n2, mixed, params, d, into, total, n_out
         )
-        last = d + 1 == LAYERS
-        outs = post(mixed, carried, weights, None if last else first[d + 1])
-        saved.append((carried, n1, proj, mixed, low, lse) + tuple(outs[:4]))
-        if not last:
-            carried, n1, proj = outs[4:]
-    out16 = outs[4]
-    hidden_out = return_cell(out16[:half], swap_halves(out16[half:]))
-
-    gx = jnp.concatenate(split_cell(cotangent), 0)
-    sums = {}
-    vectors = {}
-    for d in reversed(range(LAYERS)):
-        layer_in, n1, proj, mixed, low, lse, resid, n2, active, slope = saved[d]
-        gy, gu, g_resid, ga, g_mixed, vec2 = ff_back(
-            gx, slope, resid, w_down[d], w_up[d], w_out[d], row(ln_gains[d, 1])
-        )
-        sums["down", d] = halving.run(plain_grad([gy], active), False)
-        sums["up", d] = halving.run(plain_grad([gu], n2), True)
-        sums["out", d] = halving.run(plain_grad([ga], mixed), False)
-        grads = attn_bwd(proj, mixed, low, g_mixed, lse, meta)
-        sums["qkv", d] = halving.run(plain_grad(grads, n1), d == 0)
-        gain1 = row(ln_gains[d, 0])
-        if d > 0:
-            gx, vec1 = qkv_back(grads, w_qkv[d], layer_in, 0, g_resid, gain1, 0, tokens, F32)
-        else:
-            theirs, vec_a = qkv_back(
-                grads, w_qkv[d], layer_in, half, g_resid, gain1, half, half, BF
-            )
-            back = swap_halves(theirs)
-            mine, vec_b = qkv_back(grads, w_qkv[d], layer_in, 0, g_resid, gain1, 0, half, F32)
-            vec1 = vec_a + vec_b
-        at = lambda v, r, n: v[r, n * width : (n + 1) * width]
-        vectors[d] = [
-            at(vec1, 0, 0),
-            at(vec2, 1, 0),
-            at(vec1, 0, 1),
-            at(vec2, 1, 1),
-            at(vec1, 0, 2),
-            at(vec1, 0, 3),
-            at(vec2, 1, 3),
-            at(vec2, 1, 2),
-            vec2[0],
-        ]
-    grad_in = return_cell(mine, back.astype(F32))
-
-    flat = [v.reshape(owners, -1) for d in range(LAYERS) for v in vectors[d]]
-    widths = [f.shape[1] for f in flat]
-    flat = halving.run(jnp.concatenate(flat, 1), False, wide=True)[0]
-    pieces = jnp.split(flat, [sum(widths[: i + 1]) for i in range(len(widths) - 1)])
-    per = [pieces[:9], pieces[9:]]
-    pick = lambda i: jnp.stack([per[0][i], per[1][i]])
-    gains = jnp.stack([jnp.stack([per[d][0], per[d][1]]) for d in range(LAYERS)])
-    shifts = jnp.stack([jnp.stack([per[d][2], per[d][3]]) for d in range(LAYERS)])
-    mat = lambda name: jnp.stack([sums[name, d].T for d in range(LAYERS)])
-    return (
-        hidden_out,
-        grad_in,
-        gains,
-        shifts,
-        mat("qkv"),
-        pick(4),
-        pick(5),
-        mat("out"),
-        pick(6),
-        mat("up"),
-        pick(8),
-        mat("down"),
-        pick(7),
-    )
+        ln2[d] = vec[0, : 2 * width]
+        cols["down", d], cols["out", d] = vec[0, 2 * width : 3 * width], vec[0, 3 * width :]
+        cols["up", d] = vec[1]
+        return g_resid, g_mixed, bufs
+
+    xs, n1, proj, mixed, low, lse, resid, n2, active, slope = saved[1]
+    g_resid, g_mixed, bufs = ff_grads(gxs, 1, None, 9 * t, 1)
+    layer1 = lax.psum_scatter(bufs[0], ("dp", "blk"), scatter_dimension=0, tiled=True)[0]
+    grads = attn_bwd(proj, mixed, low, g_mixed, lse, meta, (0, pairs), None, bufs + early)
+    *bufs, sums = qkv_grad(grads, n1, None, 12 * t)
+    cols["qkv", 1] = sums[0]
+    gx, vec = qkv_back(grads, xs[0], g_resid, params, 1, 0, tokens, F32, bufs)
+    ln1[1] = vec[0]
+    xs, n1, proj, mixed, low, lse, resid, n2, active, slope = saved[0]
+    g_resid, g_mixed, bufs = ff_grads((gx,), 0, bufs, 12 * t, 2)
+    ff0 = Group(*bufs, 6 * t, dp)
+    grads = attn_bwd(proj, mixed, low, g_mixed, lse, meta, (0, 2), None, [ff0.keep])
+    dep = ff0.stage1(deps=[grads])
+    grads = attn_bwd(proj, mixed, low, g_mixed, lse, meta, (2, pairs), grads, dep)
+    *bufs, sums = qkv_grad(grads, n1, None, 3 * t)
+    cols["qkv", 0] = sums[0]
+    at0 = Group(*bufs, 48, dp)
+    theirs, vec_a = qkv_back(grads, xs[1], g_resid, params, 0, half, half, BF, [at0.keep])
+    back = swap_halves(theirs)
+    dep = ff0.stage2(deps=[theirs])
+    mine, vec_b = qkv_back(grads, xs[0], g_resid, params, 0, 0, half, F32, dep)
+    ln1[0] = vec_a[0] + vec_b[0]
+    vec = vector_rows(32, width, ln1, ln2, cols)
+    vec = jnp.pad(vec, ((0, 0), (0, width - vec.shape[1]))).astype(BF)
+    vec = jnp.pad(vec[:, None], ((0, 0), (0, 7), (0, 0))).reshape(8, 2, 2, 8, width)
+    core = lax.axis_index("dp") & 1
+    deal_core = lambda core: lax.dynamic_index_in_dim(vec, core, 1, False).reshape(16, 8, width)
+    kept, sent = deal_core(core), deal_core(1 - core)
+    vec = [kept, xor_permute(sent, dp, 1)]
+    dep = at0.stage1(vec, deps=[back])
+    dep = ff0.stage3(deps=dep)
+    dep = at0.stage2(deps=dep)
+    at0.stage3(deps=ff0.pieces[1:])
+    layout = {
+        "rows": [
+            {"down": (1, 0, 4 * t), "up": (1, 4 * t, 4 * t), "out": (1, 8 * t, t), "qkv": (2, 0, 3 * t)},
+            {"down": (0, 0, 4 * t), "up": (0, 4 * t, 4 * t), "out": (0, 8 * t, t), "qkv": (1, 9 * t, 3 * t)},
+        ],
+        "vec": (2, 3 * t, 8),
+    }
+    shapes = {
+        "qkv": (LAYERS, 3 * t, width),
+        "out": (LAYERS, t, width),
+        "up": (LAYERS, 4 * t, width),
+        "down": (LAYERS, t, 4 * width),
+        "gains": (LAYERS, 2, t),
+        "shifts": (LAYERS, 2, t),
+        "bq": (LAYERS, t),
+        "bv": (LAYERS, t),
+        "bout": (LAYERS, t),
+        "bdown": (LAYERS, t),
+        "bup": (LAYERS, 4 * t),
+    }
+    out = finish(layout, [[layer1], ff0.pieces, at0.pieces], shapes)
+    for name in ("qkv", "out", "up", "down"):
+        out[name] = jnp.swapaxes(out[name], 1, 2)
+    return (mine, back), out
 
 
 def solution(mesh):

time: 637 us -> 475 us (0.75)
  waiting for transfers between devices: 190 us -> 62.7 us
  Pallas kernels: 253 us -> 335 us
  matrix products: 49.7 us -> 0 us
  local copies, waits for them, and re-layouts: 50.7 us -> 18.2 us
  starting transfers between devices: 59.1 us -> 28.2 us
  other arithmetic: 29.4 us -> 7.45 us
  between operations: 2.05 us -> 14.7 us
    ppermute x45 -> x13, waiting for transfers between devices: 164 us -> 34.9 us  [xor_permute(): return lax.ppermute(x, 'dp', [(i, i ^ mask) for i in range(dp)])]
    pallas_call x9 -> x19, Pallas kernels: 199 us -> 282 us  [the longest x2 87.5 us: ff_all(): pl.pallas_call(functools.partial(ff_all_kernel, len(gxs), n_out, 0, d), g...]
    dot_general x12 -> x0, matrix products: 49.7 us -> none  [dot_tn(): lax.dot_general(a, b, (((0,), (0,)), ((), ())), preferred_element_type=F32)]
    ppermute x45 -> x13, starting transfers between devices: 54 us -> 17.1 us  [xor_permute(): return lax.ppermute(x, 'dp', [(i, i ^ mask) for i in range(dp)])]
    squeeze x41 -> x1, local copies, waits for them, and re-layouts: 24.4 us -> 0.98 us  [split_cell(): other = lax.dynamic_index_in_dim(both, 1 - side, 0, False)]
    convert_element_type x32 -> x0, other arithmetic: 11.4 us -> none  [run(): arr = arr.astype(BF)]
    dynamic_slice x17 -> x1, local copies, waits for them, and re-layouts: 7.17 us -> 0.71 us  [backward_grouped(): lax.dynamic_index_in_dim(vec, core, 1, False).reshape(16, 8, width)]
    ppermute x4 -> x8, waiting for transfers between devices: 26 us -> 27.7 us  [swap_halves(): return lax.ppermute(x, 'blk', [(0, 1), (1, 0)])]
  transfers between devices with their start and end apart: 49 -> 22, of which waited for: 28 -> 9; matrix products, arithmetic and copies ran while one was open for 16% -> 4% of each run, Pallas kernels for 16% -> 71%
where the time goes in v2:
time: 475 us; the launch traced here: 466 us
  Pallas kernels  335 us (71%)
  waiting for transfers between devices  62.7 us (13%)
  starting transfers between devices  28.2 us (6%)
  local copies, waits for them, and re-layouts  18.2 us (4%)
  between operations  14.7 us (3%)
  other arithmetic  7.45 us (2%)
    pallas_call x2, Pallas kernels, ff_all(): pl.pallas_call(functools.partial(ff_all_kernel, len(gxs), n_out, 0, d), g...  87.5 us
    pallas_call x3, Pallas kernels, attn_bwd(): pl.pallas_call(ordered(attn_bwd_kernel, len(ops), extra), grid_spec=pltpu...  72.9 us
    pallas_call x2, Pallas kernels, post(): pl.pallas_call(functools.partial(post_kernel, last, 4, len(xs)), grid=(to...  49.8 us
    pallas_call x2, Pallas kernels, attn_fwd(): pl.pallas_call(functools.partial(attn_fwd_kernel, tokens // 2, 2), grid_s...  41.8 us
    ppermute x13, waiting for transfers between devices, xor_permute(): return lax.ppermute(x, 'dp', [(i, i ^ mask) for i in range(dp)])  34.9 us
    ppermute x8, waiting for transfers between devices, swap_halves(): return lax.ppermute(x, 'blk', [(0, 1), (1, 0)])  27.7 us
    pallas_call x3, Pallas kernels, qkv_back(): pl.pallas_call(ordered(qkv_back_kernel, 5, deps), grid=(rows // block,),...  23.2 us
    pallas_call x4, Pallas kernels, stage_call(): pl.pallas_call(ordered(kernel, len(ops), deps), grid=(ops[0].shape[0],),...  21.3 us
  transfers between devices with their start and end apart: 22, of which 9 were waited for; matrix products, arithmetic and copies ran while one was open for 4% of the time, Pallas kernels for 71%

profile of v2, /device:TPU:0, one launch (start us, length us, event | category | flops | bytes accessed | tf_op | source)
XLA Modules:
  0.0 466.4 jit_solution(15298796510842591993)
XLA Ops:
  9.8 3.0 collective-permute-start
  17.5 5.8 %enter.2 = (bf16[1024,768]{1,0:T(8,128)(2,1)}, bf16[1024,2304]{1,0:T(8,128)(2,1)}) custom-call(bf16[512,768]{1,0:T(8,128)(2,1)} %get-tuple-element.189.x_ref.refs_1_.refs_2_, f32[2,2,1,768]{3,2,1,0:T(1,128)} %broadcast_in_dim.24.gain_ref.refs_5_.refs_11_.refs_4_.refs_3_, f32[2,2,1,768]{3,2,1,0:T(1,128)} %broadcast_in_dim.25.shift_ref.refs_6_.refs_12_.refs_5_, ...), custom_call_target="tpu_custom_call" | custom-call | flops 1811939328 | bytes 7471104 | tf_op jit(solution)/shard_map/enter/pallas_call | solution.py:265
  23.3 7.8 %collective-permute-done.x_ref.refs_2_ = bf16[512,768]{1,0:T(8,128)(2,1)S(1)} collective-permute-done((bf16[512,768]{1,0:T(8,128)(2,1)S(1)}, bf16[512,768]{1,0:T(8,128)(2,1)S(1)}, u32[]{:S(2)}, u32[]{:S(2)}) %collective-permute-start) | collective-permute-done | bytes 786464 | tf_op jit(solution)/shard_map/ppermute | solution.py:933
  32.0 5.8 %enter.3 = (bf16[1024,768]{1,0:T(8,128)(2,1)}, bf16[1024,2304]{1,0:T(8,128)(2,1)}) custom-call(bf16[512,768]{1,0:T(8,128)(2,1)} %copy-done, f32[2,2,1,768]{3,2,1,0:T(1,128)} %broadcast_in_dim.24.gain_ref.refs_5_.refs_11_.refs_4_.refs_3_, ...), custom_call_target="tpu_custom_call", output_to_operand_aliasing={{0}: (5, {}), {1}: (6, {})} | custom-call | flops 1811939328 | bytes 7471104 | tf_op jit(solution)/shard_map/enter/pallas_call | solution.py:265
  37.9 20.8 %attn_fwd.2 = (bf16[1024,768]{1,0:T(8,128)(2,1)}, bf16[1024,768]{1,0:T(8,128)(2,1)}, f32[6,8,1024]{2,1,0:T(8,128)}) custom-call(s32[2]{0:T(128)} %refs_0_.5, bf16[1024,2304]{1,0:T(8,128)(2,1)} %get-tuple-element.93.q_ref.k_ref.v_ref.refs_1_.refs_2_.refs_3_, bf16[1024,2304]{1,0:T(8,128)(2,1)} %get-tuple-element.93.q_ref.k_ref.v_ref.refs_1_.refs_2_.refs_3_, ...), custom_call_target="tpu_custom_call" | custom-call | flops 9663676416 | bytes 6291456 | tf_op jit(solution)/shard_map/attn_fwd/pallas_call | solution.py:95
  58.7 28.1 %post.2 = (f32[1024,768]{1,0:T(8,128)}, bf16[1024,768]{1,0:T(8,128)(2,1)}, bf16[1024,3072]{1,0:T(8,128)(2,1)}, bf16[1024,3072]{1,0:T(8,128)(2,1)}, f32[1024,768]...) custom-call(bf16[1024,768]{1,0:T(8,128)(2,1)} %get-tuple-element.94.refs_0_.refs_9_.refs_4_, ...), custom_call_target="tpu_custom_call" | custom-call | flops 14495514624 | bytes 31457280 | tf_op jit(solution)/shard_map/post/pallas_call | solution.py:342
  86.8 21.0 %attn_fwd.3 = (bf16[1024,768]{1,0:T(8,128)(2,1)}, bf16[1024,768]{1,0:T(8,128)(2,1)}, f32[6,8,1024]{2,1,0:T(8,128)}) custom-call(s32[2]{0:T(128)} %refs_0_.5, bf16[1024,2304]{1,0:T(8,128)(2,1)} %get-tuple-element.95.q_ref.k_ref.v_ref.refs_1_.refs_2_.refs_3_, bf16[1024,2304]{1,0:T(8,128)(2,1)} %get-tuple-element.95.q_ref.k_ref.v_ref.refs_1_.refs_2_.refs_3_, ...), custom_call_target="tpu_custom_call" | custom-call | flops 9663676416 | bytes 6291456 | tf_op jit(solution)/shard_map/attn_fwd/pallas_call | solution.py:95
  107.8 21.7 %post.3 = (f32[1024,768]{1,0:T(8,128)}, bf16[1024,768]{1,0:T(8,128)(2,1)}, bf16[1024,3072]{1,0:T(8,128)(2,1)}, bf16[1024,3072]{1,0:T(8,128)(2,1)}, bf16[1024,768]{1,0:T(8,128)(2,1)}) custom-call(bf16[1024,768]{1,0:T(8,128)(2,1)} %get-tuple-element.96.refs_0_.refs_10_.refs_4_, f32[1024,768]{1,0:T(8,128)} %get-tuple-element.97.refs_1_.refs_2_, ...), custom_call_target="tpu_custom_call" | custom-call | flops 10871635968 | bytes 31457280 | tf_op jit(solution)/shard_map/post/pallas_call | solution.py:342
  134.8 43.4 %ff_all.2 = (f32[1024,768]{1,0:T(8,128)}, bf16[1024,768]{1,0:T(8,128)(2,1)}, f32[8,3072]{1,0:T(8,128)}, bf16[32,216,768]{2,1,0:T(8,128)(2,1)}) custom-call(bf16[512,768]{1,0:T(8,128)(2,1)} %get-tuple-element.186.refs_0_, bf16[512,768]{1,0:T(8,128)(2,1)} %copy-done.27, bf16[1024,3072]{1,0:T(8,128)(2,1)} %get-tuple-element.101.refs_2_, ...), custom_call_target="tpu_custom_call" | custom-call | flops 21743271936 | bytes 52428800 | tf_op jit(solution)/shard_map/ff_all/pallas_call | solution.py:740
  178.3 34.7 %attn_bwd.3.left_ref.refs_0_ = bf16[3,1024,768]{2,1,0:T(8,128)(2,1)} custom-call(s32[2]{0:T(128)} %refs_0_.5, bf16[1024,2304]{1,0:T(8,128)(2,1)} %get-tuple-element.95.q_ref.k_ref.v_ref.refs_1_.refs_2_.refs_3_, bf16[1024,2304]{1,0:T(8,128)(2,1)} %get-tuple-element.95.q_ref.k_ref.v_ref.refs_1_.refs_2_.refs_3_, ...), custom_call_target="tpu_custom_call" | custom-call | flops 16106127360 | bytes 14155776 | tf_op jit(solution)/shard_map/attn_bwd/pallas_call | solution.py:162
  213.1 9.2 %qkv_grad.2 = (bf16[16,288,768]{2,1,0:T(8,128)(2,1)}, bf16[16,288,768]{2,1,0:T(8,128)(2,1)}, f32[8,2304]{1,0:T(8,128)}) custom-call(bf16[3,1024,768]{2,1,0:T(8,128)(2,1)} %attn_bwd.3.left_ref.refs_0_, bf16[1024,768]{1,0:T(8,128)(2,1)} %get-tuple-element.109.right_ref), custom_call_target="tpu_custom_call" | custom-call | flops 3623878656 | bytes 12582912 | tf_op jit(solution)/shard_map/qkv_grad/pallas_call | solution.py:558
  222.3 10.2 %qkv_back.3 = (f32[1024,768]{1,0:T(8,128)}, f32[8,1536]{1,0:T(8,128)}) custom-call(bf16[3,1024,768]{2,1,0:T(8,128)(2,1)} %attn_bwd.3.left_ref.refs_0_, bf16[2,768,2304]{2,1,0:T(8,128)(2,1)} %refs_1_.5, f32[1024,768]{1,0:T(8,128)} %get-tuple-element.97.refs_1_.refs_2_, f32[1024,768]{1,0:T(8,128)} %get-tuple-element.108.refs_3_, ...), custom_call_target="tpu_custom_call" | custom-call | flops 3623878656 | bytes 15728640 | tf_op jit(solution)/shard_map/qkv_back/pallas_call | solution.py:445
  232.5 44.0 %ff_all.3 = (f32[1024,768]{1,0:T(8,128)}, bf16[1024,768]{1,0:T(8,128)(2,1)}, f32[8,3072]{1,0:T(8,128)}, bf16[16,288,768]{2,1,0:T(8,128)(2,1)}, bf16[16,288,768]{2,1,0:T(8,128)(2,1)}) custom-call(f32[1024,768]{1,0:T(8,128)} %get-tuple-element.112.refs_0_, ...), custom_call_target="tpu_custom_call", output_to_operand_aliasing={{3}: (10, {}), {4}: (11, {})} | custom-call | flops 21743271936 | bytes 52428800 | tf_op jit(solution)/shard_map/ff_all/pallas_call | solution.py:740
  278.5 14.0 %attn_bwd.4.refs_2_.refs_8_ = bf16[3,1024,768]{2,1,0:T(8,128)(2,1)} custom-call(s32[2]{0:T(128)} %refs_0_.5, bf16[1024,2304]{1,0:T(8,128)(2,1)} %get-tuple-element.93.q_ref.k_ref.v_ref.refs_1_.refs_2_.refs_3_, bf16[1024,2304]{1,0:T(8,128)(2,1)} %get-tuple-element.93.q_ref.k_ref.v_ref.refs_1_.refs_2_.refs_3_, ...), custom_call_target="tpu_custom_call" | custom-call | flops 5368709120 | bytes 4718592 | tf_op jit(solution)/shard_map/attn_bwd/pallas_call | solution.py:162
  292.6 8.5 %stage1.2 = (bf16[4,2,144,768]{3,2,1,0:T(8,128)(2,1)}, bf16[4,2,144,768]{3,2,1,0:T(8,128)(2,1)}, bf16[4,2,144,768]{3,2,1,0:T(8,128)(2,1)}, bf16[4,2,144,768]{3,2,1,0:T(8,128)(2,1)}) custom-call(bf16[4,2,2,288,768]{4,3,2,1,0:T(8,128)(2,1)} %bitcast.30, bf16[4,2,2,288,768]{4,3,2,1,0:T(8,128)(2,1)} %bitcast.7.refs_1_, bf16[3,1024,768]{2,1,0:T(8,128)(2,1)} %attn_bwd.4.refs_2_.refs_8_), custom_call_target="tpu_custom_call" | custom-call | flops 21233664 | bytes 21233664 | tf_op jit(solution)/shard_map/stage1/pallas_call | solution.py:805
  302.8 24.2 %attn_bwd.5.left_ref.refs_0_ = bf16[3,1024,768]{2,1,0:T(8,128)(2,1)} custom-call(s32[2]{0:T(128)} %refs_0_.5, bf16[1024,2304]{1,0:T(8,128)(2,1)} %get-tuple-element.93.q_ref.k_ref.v_ref.refs_1_.refs_2_.refs_3_, bf16[1024,2304]{1,0:T(8,128)(2,1)} %get-tuple-element.93.q_ref.k_ref.v_ref.refs_1_.refs_2_.refs_3_, ...), custom_call_target="tpu_custom_call", output_to_operand_aliasing={{}: (8, {})} | custom-call | flops 10737418240 | bytes 9437184 | tf_op jit(solution)/shard_map/attn_bwd/pallas_call | solution.py:162
  327.0 9.0 %qkv_grad.3 = (bf16[16,72,768]{2,1,0:T(8,128)(2,1)}, bf16[16,72,768]{2,1,0:T(8,128)(2,1)}, f32[8,2304]{1,0:T(8,128)}) custom-call(bf16[3,1024,768]{2,1,0:T(8,128)(2,1)} %attn_bwd.5.left_ref.refs_0_, bf16[1024,768]{1,0:T(8,128)(2,1)} %get-tuple-element.126.right_ref), custom_call_target="tpu_custom_call" | custom-call | flops 3623878656 | bytes 12582912 | tf_op jit(solution)/shard_map/qkv_grad/pallas_call | solution.py:558
  337.7 6.4 %qkv_back.4 = (bf16[512,768]{1,0:T(8,128)(2,1)}, f32[8,1536]{1,0:T(8,128)}) custom-call(bf16[3,1024,768]{2,1,0:T(8,128)(2,1)} %attn_bwd.5.left_ref.refs_0_, bf16[2,768,2304]{2,1,0:T(8,128)(2,1)} %refs_1_.5, bf16[512,768]{1,0:T(8,128)(2,1)} %copy-done, f32[1024,768]{1,0:T(8,128)} %get-tuple-element.122.refs_3_, ...), custom_call_target="tpu_custom_call" | custom-call | flops 1811939328 | bytes 7864320 | tf_op jit(solution)/shard_map/qkv_back/pallas_call | solution.py:445
  346.1 5.2 %stage2.2 = (bf16[4,144,768]{2,1,0:T(8,128)(2,1)}, bf16[4,144,768]{2,1,0:T(8,128)(2,1)}, bf16[4,144,768]{2,1,0:T(8,128)(2,1)}, bf16[4,144,768]{2,1,0:T(8,128)(2,1)}) custom-call(bf16[4,2,144,768]{3,2,1,0:T(8,128)(2,1)} %get-tuple-element.121.refs_9_.refs_0_, bf16[4,2,144,768]{3,2,1,0:T(8,128)(2,1)} %collective-permute-done.4.refs_1_, ...), custom_call_target="tpu_custom_call" | custom-call | flops 10616832 | bytes 10616832 | tf_op jit(solution)/shard_map/stage2/pallas_call | solution.py:805
  351.2 6.5 %qkv_back.5 = (f32[512,768]{1,0:T(8,128)}, f32[8,1536]{1,0:T(8,128)}) custom-call(bf16[3,1024,768]{2,1,0:T(8,128)(2,1)} %attn_bwd.5.left_ref.refs_0_, bf16[2,768,2304]{2,1,0:T(8,128)(2,1)} %refs_1_.5, bf16[512,768]{1,0:T(8,128)(2,1)} %get-tuple-element.189.x_ref.refs_1_.refs_2_, f32[1024,768]{1,0:T(8,128)} %get-tuple-element.122.refs_3_, ...), custom_call_target="tpu_custom_call" | custom-call | flops 1811939328 | bytes 7864320 | tf_op jit(solution)/shard_map/qkv_back/pallas_call | solution.py:445
  360.5 4.2 collective-permute-done.6.refs_4_
  366.3 4.0 stage1.3
  372.5 11.3 %collective-permute-done.7.refs_1_ = bf16[4,144,768]{2,1,0:T(8,128)(2,1)} collective-permute-done((bf16[4,144,768]{2,1,0:T(8,128)(2,1)}, bf16[4,144,768]{2,1,0:T(8,128)(2,1)}, u32[]{:S(2)}, u32[]{:S(2)}) %collective-permute-start.7) | collective-permute-done | bytes 884768 | tf_op jit(solution)/shard_map/ppermute | solution.py:933
  383.8 3.6 stage3.2
  387.5 4.4 collective-permute-done.15.refs_3_
  394.7 3.6 stage2.3
  407.7 5.1 %collective-permute-done.17.refs_3_ = bf16[4,32,768]{2,1,0:T(8,128)(2,1)S(1)} collective-permute-done((bf16[4,32,768]{2,1,0:T(8,128)(2,1)S(1)}, bf16[4,32,768]{2,1,0:T(8,128)(2,1)S(1)}, u32[]{:S(2)}, u32[]{:S(2)}) %collective-permute-start.17) | collective-permute-done | bytes 196640 | tf_op jit(solution)/shard_map/ppermute | solution.py:818
  412.9 6.4 %collective-permute-done.11.refs_4_.refs_2_ = bf16[288,768]{1,0:T(8,128)(2,1)S(1)} collective-permute-done((bf16[288,768]{1,0:T(8,128)(2,1)}, bf16[288,768]{1,0:T(8,128)(2,1)S(1)}, u32[]{:S(2)}, u32[]{:S(2)}) %collective-permute-start.11) | collective-permute-done | bytes 442400 | tf_op jit(solution)/shard_map/ppermute | solution.py:818
  419.3 15.4 %collective-permute-done.12.refs_5_.refs_3_ = bf16[288,768]{1,0:T(8,128)(2,1)S(1)} collective-permute-done((bf16[288,768]{1,0:T(8,128)(2,1)}, bf16[288,768]{1,0:T(8,128)(2,1)S(1)}, u32[]{:S(2)}, u32[]{:S(2)}) %collective-permute-start.12) | collective-permute-done | bytes 442400 | tf_op jit(solution)/shard_map/ppermute | solution.py:818
  437.7 7.4 %collective-permute-start.18 = (bf16[80,768]{1,0:T(8,128)(2,1)}, bf16[80,768]{1,0:T(8,128)(2,1)S(1)}, u32[]{:S(2)}, u32[]{:S(2)}) collective-permute-start(bf16[80,768]{1,0:T(8,128)(2,1)} %get-tuple-element.155), channel_id=1, source_target_pairs={{0,8},{2,10},{4,12},{6,14},{8,0},{10,2},{12,4},{14,6},{16,24},{18,... | collective-permute-start | bytes 368648 | tf_op jit(solution)/shard_map/ppermute | solution.py:818
  449.4 6.0 %collective-permute-done.19.refs_7_ = bf16[80,768]{1,0:T(8,128)(2,1)S(1)} collective-permute-done((bf16[80,768]{1,0:T(8,128)(2,1)}, bf16[80,768]{1,0:T(8,128)(2,1)S(1)}, u32[]{:S(2)}, u32[]{:S(2)}) %collective-permute-start.19) | collective-permute-done | bytes 122912 | tf_op jit(solution)/shard_map/ppermute | solution.py:818
  456.1 3.2 finish.1
  (148 shorter events, 47.5 us)
Async XLA Ops:
  7.2 448.2 %reduce-scatter.2.cloned.1.call-start = ((), (), s32[]{:S(2)}) async-start(), calls=%async_computation.1 | async-start | bytes 10948608 | tf_op jit(solution)/shard_map/reduce_scatter | solution.py:1140
  9.8 21.4 %collective-permute-start = (bf16[512,768]{1,0:T(8,128)(2,1)S(1)}, bf16[512,768]{1,0:T(8,128)(2,1)S(1)}, u32[]{:S(2)}, u32[]{:S(2)}) collective-permute-start(bf16[512,768]{1,0:T(8,128)(2,1)S(1)} %get-tuple-element.190), channel_id=1, source_target_pairs={{0,1},{1,0},{2,3},{3,2},{4,5},{5,4},{6,7},{7,6},{8,9},{9,8},{10,11... | collective-permute-start | bytes 2359304 | tf_op jit(solution)/shard_map/ppermute | solution.py:933
  13.8 120.2 %collective-permute-start.2 = (bf16[512,768]{1,0:T(8,128)(2,1)S(1)}, bf16[512,768]{1,0:T(8,128)(2,1)S(1)}, u32[]{:S(2)}, u32[]{:S(2)}) collective-permute-start(bf16[512,768]{1,0:T(8,128)(2,1)S(1)} %get-tuple-element.185), channel_id=1, source_target_pairs={{0,1},{1,0},{2,3},{3,2},{4,5},{5,4},{6,7},{7,6},{8,9},{9,8},{10,11... | collective-permute-start | bytes 2359304 | tf_op jit(solution)/shard_map/ppermute | solution.py:933
  131.9 46.4 %collective-permute-start.1 = (bf16[512,768]{1,0:T(8,128)(2,1)}, bf16[512,768]{1,0:T(8,128)(2,1)}, u32[]{:S(2)}, u32[]{:S(2)}) collective-permute-start(bf16[512,768]{1,0:T(8,128)(2,1)} %get-tuple-element.188), channel_id=1, source_target_pairs={{0,1},{1,0},{2,3},{3,2},{4,5},{5,4},{6,7},{7,6},{8,9},{9,8},{10,11... | collective-permute-start | bytes 2359304 | tf_op jit(solution)/shard_map/ppermute | solution.py:933
  232.5 44.1 %copy-start.17 = (f32[8,3072]{1,0:T(8,128)S(1)}, f32[8,3072]{1,0:T(8,128)}, u32[]{:S(2)}) copy-start(f32[8,3072]{1,0:T(8,128)} %get-tuple-element.140) | copy-start | bytes 294916
  276.5 16.1 %collective-permute-start.3 = (bf16[16,288,768]{2,1,0:T(8,128)(2,1)}, bf16[16,288,768]{2,1,0:T(8,128)(2,1)}, u32[]{:S(2)}, u32[]{:S(2)}) collective-permute-start(bf16[16,288,768]{2,1,0:T(8,128)(2,1)} %get-tuple-element.120), channel_id=1, source_target_pairs={{0,2},{2,0},{4,6},{6,4},{8,10},{10,8},{12,14},{14,12},{16,18},{18,... | collective-permute-start | bytes 21233672 | tf_op jit(solution)/shard_map/ppermute | solution.py:818
  301.1 45.0 %collective-permute-start.4 = (bf16[4,2,144,768]{3,2,1,0:T(8,128)(2,1)}, bf16[4,2,144,768]{3,2,1,0:T(8,128)(2,1)}, u32[]{:S(2)}, u32[]{:S(2)}) collective-permute-start(bf16[4,2,144,768]{3,2,1,0:T(8,128)(2,1)} %get-tuple-element.123), channel_id=1, source_target_pairs={{0,4},{2,6},{4,0},{6,2},{8,12},{10,14},{12,8},{14,10},{16,20},{18,... | collective-permute-start | bytes 5308424 | tf_op jit(solution)/shard_map/ppermute | solution.py:818
  302.7 43.4 %collective-permute-start.5 = (bf16[4,2,144,768]{3,2,1,0:T(8,128)(2,1)}, bf16[4,2,144,768]{3,2,1,0:T(8,128)(2,1)}, u32[]{:S(2)}, u32[]{:S(2)}) collective-permute-start(bf16[4,2,144,768]{3,2,1,0:T(8,128)(2,1)} %get-tuple-element.125), channel_id=1, source_target_pairs={{0,1},{1,0},{2,3},{3,2},{4,5},{5,4},{6,7},{7,6},{8,9},{9,8},{10,11... | collective-permute-start | bytes 5308424 | tf_op jit(solution)/shard_map/ppermute | solution.py:933
  327.0 9.1 %copy-start.19 = (f32[8,1536]{1,0:T(8,128)S(1)}, f32[8,1536]{1,0:T(8,128)}, u32[]{:S(2)}) copy-start(f32[8,1536]{1,0:T(8,128)} %get-tuple-element.139) | copy-start | bytes 147460
  327.0 9.4 %copy-start.18 = (f32[8,2304]{1,0:T(8,128)S(1)}, f32[8,2304]{1,0:T(8,128)}, u32[]{:S(2)}) copy-start(f32[8,2304]{1,0:T(8,128)} %get-tuple-element.141) | copy-start | bytes 221188
  335.9 28.8 %collective-permute-start.9 = (bf16[16,72,768]{2,1,0:T(8,128)(2,1)}, bf16[16,72,768]{2,1,0:T(8,128)(2,1)S(1)}, u32[]{:S(2)}, u32[]{:S(2)}) collective-permute-start(bf16[16,72,768]{2,1,0:T(8,128)(2,1)} %get-tuple-element.134), channel_id=1, source_target_pairs={{0,2},{2,0},{4,6},{6,4},{8,10},{10,8},{12,14},{14,12},{16,18},{18,... | collective-permute-start | bytes 5308424 | tf_op jit(solution)/shard_map/ppermute | solution.py:818
  344.1 20.6 %collective-permute-start.6 = (bf16[512,768]{1,0:T(8,128)(2,1)}, bf16[512,768]{1,0:T(8,128)(2,1)S(1)}, u32[]{:S(2)}, u32[]{:S(2)}) collective-permute-start(bf16[512,768]{1,0:T(8,128)(2,1)} %get-tuple-element.128.refs_4_), channel_id=1, source_target_pairs={{0,1},{1,0},{2,3},{3,2},{4,5},{5,4},{6,7},{7,6},{8,9},{9,8},{10,11... | collective-permute-start | bytes 2359304 | tf_op jit(solution)/shard_map/ppermute | solution.py:933
  359.1 24.7 %collective-permute-start.7 = (bf16[4,144,768]{2,1,0:T(8,128)(2,1)}, bf16[4,144,768]{2,1,0:T(8,128)(2,1)}, u32[]{:S(2)}, u32[]{:S(2)}) collective-permute-start(bf16[4,144,768]{2,1,0:T(8,128)(2,1)} %get-tuple-element.131), channel_id=1, source_target_pairs={{0,1},{1,0},{2,3},{3,2},{4,5},{5,4},{6,7},{7,6},{8,9},{9,8},{10,11... | collective-permute-start | bytes 2654216 | tf_op jit(solution)/shard_map/ppermute | solution.py:933
  359.3 24.5 %collective-permute-start.8 = (bf16[4,144,768]{2,1,0:T(8,128)(2,1)}, bf16[4,144,768]{2,1,0:T(8,128)(2,1)}, u32[]{:S(2)}, u32[]{:S(2)}) collective-permute-start(bf16[4,144,768]{2,1,0:T(8,128)(2,1)} %get-tuple-element.133), channel_id=1, source_target_pairs={{0,4},{2,6},{4,0},{6,2},{8,12},{10,14},{12,8},{14,10},{16,20},{18,... | collective-permute-start | bytes 2654216 | tf_op jit(solution)/shard_map/ppermute | solution.py:818
  360.5 4.2 collective-permute-start.10
  370.3 23.6 %collective-permute-start.14 = (bf16[4,2,48,768]{3,2,1,0:T(8,128)(2,1)}, bf16[4,2,48,768]{3,2,1,0:T(8,128)(2,1)S(1)}, u32[]{:S(2)}, u32[]{:S(2)}) collective-permute-start(bf16[4,2,48,768]{3,2,1,0:T(8,128)(2,1)} %get-tuple-element.147), channel_id=1, source_target_pairs={{0,4},{2,6},{4,0},{6,2},{8,12},{10,14},{12,8},{14,10},{16,20},{18,... | collective-permute-start | bytes 1769480 | tf_op jit(solution)/shard_map/ppermute | solution.py:818
  370.6 21.2 %collective-permute-start.15 = (bf16[4,2,32,768]{3,2,1,0:T(8,128)(2,1)}, bf16[4,2,32,768]{3,2,1,0:T(8,128)(2,1)S(1)}, u32[]{:S(2)}, u32[]{:S(2)}) collective-permute-start(bf16[4,2,32,768]{3,2,1,0:T(8,128)(2,1)} %get-tuple-element.149), channel_id=1, source_target_pairs={{0,1},{1,0},{2,3},{3,2},{4,5},{5,4},{6,7},{7,6},{8,9},{9,8},{10,11... | collective-permute-start | bytes 1179656 | tf_op jit(solution)/shard_map/ppermute | solution.py:933
  387.4 16.7 %copy-start.28 = (bf16[288,768]{1,0:T(8,128)(2,1)S(1)}, bf16[288,768]{1,0:T(8,128)(2,1)}, u32[]{:S(2)}) copy-start(bf16[288,768]{1,0:T(8,128)(2,1)} %get-tuple-element.146) | copy-start | bytes 1327108
  398.3 8.9 %copy-start.29 = (bf16[4,32,768]{2,1,0:T(8,128)(2,1)S(1)}, bf16[4,32,768]{2,1,0:T(8,128)(2,1)}, u32[]{:S(2)}) copy-start(bf16[4,32,768]{2,1,0:T(8,128)(2,1)} %get-tuple-element.153) | copy-start | bytes 589828
  398.3 9.4 %copy-start.2 = (bf16[512,768]{1,0:T(8,128)(2,1)S(1)}, bf16[512,768]{1,0:T(8,128)(2,1)}, u32[]{:S(2)}) copy-start(bf16[512,768]{1,0:T(8,128)(2,1)} %copy-done.1) | copy-start | bytes 2359300
  398.3 14.6 %collective-permute-start.16 = (bf16[4,48,768]{2,1,0:T(8,128)(2,1)}, bf16[4,48,768]{2,1,0:T(8,128)(2,1)S(1)}, u32[]{:S(2)}, u32[]{:S(2)}) collective-permute-start(bf16[4,48,768]{2,1,0:T(8,128)(2,1)} %get-tuple-element.151), channel_id=1, source_target_pairs={{0,1},{1,0},{2,3},{3,2},{4,5},{5,4},{6,7},{7,6},{8,9},{9,8},{10,11... | collective-permute-start | bytes 884744 | tf_op jit(solution)/shard_map/ppermute | solution.py:933
  400.0 19.3 %collective-permute-start.11 = (bf16[288,768]{1,0:T(8,128)(2,1)}, bf16[288,768]{1,0:T(8,128)(2,1)S(1)}, u32[]{:S(2)}, u32[]{:S(2)}) collective-permute-start(bf16[288,768]{1,0:T(8,128)(2,1)} %get-tuple-element.144), channel_id=1, source_target_pairs={{0,8},{2,10},{4,12},{6,14},{8,0},{10,2},{12,4},{14,6},{16,24},{18,... | collective-permute-start | bytes 1327112 | tf_op jit(solution)/shard_map/ppermute | solution.py:818
  401.5 33.2 %collective-permute-start.12 = (bf16[288,768]{1,0:T(8,128)(2,1)}, bf16[288,768]{1,0:T(8,128)(2,1)S(1)}, u32[]{:S(2)}, u32[]{:S(2)}) collective-permute-start(bf16[288,768]{1,0:T(8,128)(2,1)} %get-tuple-element.145), channel_id=1, source_target_pairs={{0,16},{2,18},{4,20},{6,22},{8,24},{10,26},{12,28},{14,30},{16,0},... | collective-permute-start | bytes 1327112 | tf_op jit(solution)/shard_map/ppermute | solution.py:818
  404.1 30.6 %collective-permute-start.13 = (bf16[288,768]{1,0:T(8,128)(2,1)S(1)}, bf16[288,768]{1,0:T(8,128)(2,1)S(1)}, u32[]{:S(2)}, u32[]{:S(2)}) collective-permute-start(bf16[288,768]{1,0:T(8,128)(2,1)S(1)} %copy-done.28), channel_id=1, source_target_pairs={{0,24},{2,26},{4,28},{6,30},{8,16},{10,18},{12,20},{14,22},{16,8},... | collective-permute-start | bytes 1327112 | tf_op jit(solution)/shard_map/ppermute | solution.py:818
  407.2 40.3 %copy-start.8 = (f32[512,768]{1,0:T(8,128)S(1)}, f32[512,768]{1,0:T(8,128)}, u32[]{:S(2)}) copy-start(f32[512,768]{1,0:T(8,128)} %get-tuple-element.130) | copy-start | bytes 4718596
  407.2 5.7 %collective-permute-start.17 = (bf16[4,32,768]{2,1,0:T(8,128)(2,1)S(1)}, bf16[4,32,768]{2,1,0:T(8,128)(2,1)S(1)}, u32[]{:S(2)}, u32[]{:S(2)}) collective-permute-start(bf16[4,32,768]{2,1,0:T(8,128)(2,1)S(1)} %copy-done.29), channel_id=1, source_target_pairs={{0,4},{2,6},{4,0},{6,2},{8,12},{10,14},{12,8},{14,10},{16,20},{18,... | collective-permute-start | bytes 589832 | tf_op jit(solution)/shard_map/ppermute | solution.py:818
  412.9 21.8 %copy-start.13 = (bf16[4,32,768]{2,1,0:T(8,128)(2,1)}, bf16[4,32,768]{2,1,0:T(8,128)(2,1)S(1)}, u32[]{:S(2)}) copy-start(bf16[4,32,768]{2,1,0:T(8,128)(2,1)S(1)} %collective-permute-done.17.refs_3_) | copy-start | bytes 589828
  412.9 21.8 %copy-start.11 = (bf16[4,48,768]{2,1,0:T(8,128)(2,1)}, bf16[4,48,768]{2,1,0:T(8,128)(2,1)S(1)}, u32[]{:S(2)}) copy-start(bf16[4,48,768]{2,1,0:T(8,128)(2,1)S(1)} %collective-permute-done.16.refs_1_) | copy-start | bytes 884740
  419.3 15.4 %copy-start.4 = (bf16[288,768]{1,0:T(8,128)(2,1)}, bf16[288,768]{1,0:T(8,128)(2,1)S(1)}, u32[]{:S(2)}) copy-start(bf16[288,768]{1,0:T(8,128)(2,1)S(1)} %collective-permute-done.11.refs_4_.refs_2_) | copy-start | bytes 1327108
  437.7 11.7 %collective-permute-start.18 = (bf16[80,768]{1,0:T(8,128)(2,1)}, bf16[80,768]{1,0:T(8,128)(2,1)S(1)}, u32[]{:S(2)}, u32[]{:S(2)}) collective-permute-start(bf16[80,768]{1,0:T(8,128)(2,1)} %get-tuple-element.155), channel_id=1, source_target_pairs={{0,8},{2,10},{4,12},{6,14},{8,0},{10,2},{12,4},{14,6},{16,24},{18,... | collective-permute-start | bytes 368648 | tf_op jit(solution)/shard_map/ppermute | solution.py:818
  445.1 10.3 %collective-permute-start.19 = (bf16[80,768]{1,0:T(8,128)(2,1)}, bf16[80,768]{1,0:T(8,128)(2,1)S(1)}, u32[]{:S(2)}, u32[]{:S(2)}) collective-permute-start(bf16[80,768]{1,0:T(8,128)(2,1)} %get-tuple-element.156), channel_id=1, source_target_pairs={{0,16},{2,18},{4,20},{6,22},{8,24},{10,26},{12,28},{14,30},{16,0},... | collective-permute-start | bytes 368648 | tf_op jit(solution)/shard_map/ppermute | solution.py:818
  446.1 9.3 %collective-permute-start.20 = (bf16[80,768]{1,0:T(8,128)(2,1)}, bf16[80,768]{1,0:T(8,128)(2,1)S(1)}, u32[]{:S(2)}, u32[]{:S(2)}) collective-permute-start(bf16[80,768]{1,0:T(8,128)(2,1)} %get-tuple-element.157), channel_id=1, source_target_pairs={{0,24},{2,26},{4,28},{6,30},{8,16},{10,18},{12,20},{14,22},{16,8},... | collective-permute-start | bytes 368648 | tf_op jit(solution)/shard_map/ppermute | solution.py:818
  (20 other events, 62.4 us)
Sparse Core Ops, SparseCore 0:
  178.4 144.1 reduce-scatter.1

commit v3 on v2

--- a/solution.py
+++ b/solution.py
@@ -173,11 +173,7 @@
         compiler_params=pltpu.CompilerParams(
             vmem_limit_bytes=56 << 20, dimension_semantics=("arbitrary",)
         ),
-        cost_estimate=pl.CostEstimate(
-            flops=20 * tokens * tokens * 128 * (stop - start),
-            bytes_accessed=tokens * 128 * (stop - start) * 18,
-            transcendentals=2 * (stop - start) * tokens * tokens,
-        ),
+        cost_estimate=cost(1, 1),
         name="attn_bwd",
     )(*ops, *extra)
 
@@ -189,6 +185,10 @@
     if not deps:
         return kernel
     return lambda *refs: kernel(*refs[:n_in], *refs[n_in + len(deps) :])
+
+
+def after(array, deps):
+    return lax.optimization_barrier((array, *deps))[0]
 
 
 def anywhere(arrays):
@@ -233,12 +233,6 @@
 def attn_in(params, d):
     arrays = [params["gains"], params["shifts"], params["wqkv"], params["bias"]]
     return arrays, [layer(arrays[0], d, 0), layer(arrays[1], d, 0), layer(arrays[2], d), layer(arrays[3], d)]
-
-
-def ff_in(params, d):
-    names = ("wout", "bout", "gains", "shifts", "wup", "bup", "wdown", "bdown")
-    arrays = [params[n] for n in names]
-    return arrays, [layer(a, d, 1) for a in arrays]
 
 
 def enter_kernel(x_ref, gain_ref, shift_ref, wqkv_ref, bias_ref, *refs):
@@ -289,62 +283,111 @@
     return jnp.where(early, refs[0][...].astype(F32), refs[1][...].astype(F32))
 
 
-def post_kernel(last, parts, n_x, *refs):
+def post_kernel(d, last, parts, n_x, *refs):
     it = iter(refs)
     mixed_ref = next(it)
     x_refs = [next(it) for _ in range(n_x)]
-    wout_ref, bout_ref, gain_ref, shift_ref = next(it), next(it), next(it), next(it)
-    wup_ref, bup_ref, wdown_ref, bdown_ref = next(it), next(it), next(it), next(it)
+    bout_ref, gain_ref, shift_ref, bup_ref, bdown_ref = [next(it) for _ in range(5)]
     if not last:
-        gain1_ref, shift1_ref, wqkv_ref, bias_ref = next(it), next(it), next(it), next(it)
+        gain1_ref, shift1_ref, bias_ref = next(it), next(it), next(it)
+    sources = [next(it) for _ in range(3 if last else 4)]
     resid_ref, n2_ref, active_ref, slope_ref = next(it), next(it), next(it), next(it)
+    outs = [next(it) for _ in range(2 if last else 3)]
+    wout, wup, wdown = next(it), next(it), next(it)
+    wqkv = None if last else next(it)
+    arrive = next(it)
+    step = pl.program_id(0)
     width = mixed_ref.shape[1]
-    resid = joined(x_refs) + dot_nn(mixed_ref[...], wout_ref[...]) + bout_ref[...]
-    resid_ref[...] = resid
-    xhat, _ = normalize(resid)
-    n2 = (xhat * gain_ref[...] + shift_ref[...]).astype(BF)
-    n2_ref[...] = n2
-    hidden = wup_ref.shape[1] // parts
-    total = resid + bdown_ref[...]
-    for j in range(parts):
-        cols = slice(j * hidden, (j + 1) * hidden)
-        upper = dot_nn(n2, wup_ref[:, cols]) + bup_ref[:, cols]
-        cdf = 0.5 + 0.5 * lax.erf(upper * math.sqrt(0.5))
-        dens = jnp.exp2(upper * upper * (-0.5 * math.log2(math.e))) * (1.0 / math.sqrt(2.0 * math.pi))
-        active = (upper * cdf).astype(BF)
-        active_ref[:, cols] = active
-        slope_ref[:, cols] = (cdf + upper * dens).astype(BF)
-        total = total + dot_nn(active, wdown_ref[cols, :])
-    if last:
-        next(it)[...] = total.astype(BF)
-    else:
-        x_out, n1_ref, proj_ref = next(it), next(it), next(it)
-        x_out[...] = total
-        xhat, _ = normalize(total)
-        n1 = (xhat * gain1_ref[...] + shift1_ref[...]).astype(BF)
-        n1_ref[...] = n1
-        project(n1, wqkv_ref, bias_ref, proj_ref, width)
+    hidden = wup.shape[1] // parts
+
+    def load(n):
+        part = pl.ds((n - 1) // 2 * hidden, hidden)
+        if n == 0:
+            pair = sources[0].at[d], wout
+        elif n > 2 * parts:
+            pair = sources[3].at[d + 1], wqkv
+        elif n % 2:
+            pair = sources[1].at[d, :, part], wup.at[:, part]
+        else:
+            pair = sources[2].at[d, part], wdown.at[part]
+        return pltpu.make_async_copy(*pair, arrive.at[n])
+
+    @pl.when(step == 0)
+    def _():
+        for n in range(2 * parts + (1 if last else 2)):
+            load(n).start()
+
+    def body(wait):
+        wait(0)
+        resid = joined(x_refs) + dot_nn(mixed_ref[...], wout[...]) + bout_ref[...]
+        resid_ref[...] = resid
+        xhat, _ = normalize(resid)
+        n2 = (xhat * gain_ref[...] + shift_ref[...]).astype(BF)
+        n2_ref[...] = n2
+        total = resid + bdown_ref[...]
+        for j in range(parts):
+            cols = slice(j * hidden, (j + 1) * hidden)
+            wait(2 * j + 1)
+            upper = dot_nn(n2, wup[:, cols]) + bup_ref[:, cols]
+            cdf = 0.5 + 0.5 * lax.erf(upper * math.sqrt(0.5))
+            dens = jnp.exp2(upper * upper * (-0.5 * math.log2(math.e))) * (1.0 / math.sqrt(2.0 * math.pi))
+            active = (upper * cdf).astype(BF)
+            active_ref[:, cols] = active
+            slope_ref[:, cols] = (cdf + upper * dens).astype(BF)
+            wait(2 * j + 2)
+            total = total + dot_nn(active, wdown[cols, :])
+        if last:
+            for n, ref in enumerate(outs):
+
+                @pl.when(step // (pl.num_programs(0) // 2) == n)
+                def _():
+                    ref[...] = total.astype(BF)
+        else:
+            x_out, n1_ref, proj_ref = outs
+            x_out[...] = total
+            xhat, _ = normalize(total)
+            n1 = (xhat * gain1_ref[...] + shift1_ref[...]).astype(BF)
+            n1_ref[...] = n1
+            wait(2 * parts + 1)
+            project(n1, wqkv, bias_ref, proj_ref, width)
+
+    pl.when(step == 0)(lambda: body(lambda n: load(n).wait()))
+    pl.when(step > 0)(lambda: body(lambda n: None))
 
 
 def post(mixed, xs, params, d, last):
     tokens, width = mixed.shape
     block = 256
+    parts = 4
     ff = params["wup"].shape[2]
-    arrays, specs = ff_in(params, d)
+    small = [(params[n], d) for n in ("bout", "gains", "shifts", "bup", "bdown")]
+    specs = [layer(a, e, 1) for a, e in small]
+    weights = ["wout", "wup", "wdown"]
     if not last:
-        more, more_specs = attn_in(params, d + 1)
-        arrays, specs = arrays + more, specs + more_specs
+        more = [(params[n], d + 1) for n in ("gains", "shifts", "bias")]
+        specs += [layer(a, e, 0) for a, e in more]
+        small += more
+        weights.append("wqkv")
+    arrays = [a for a, _ in small] + [params[n] for n in weights]
     ops = [mixed] + list(xs) + arrays
     x_specs = [tile(block, width)] if len(xs) == 1 else halves(tokens, block, width)
-    outs = [(width, F32), (width, BF), (ff, BF), (ff, BF)]
-    outs += [(width, BF)] if last else [(width, F32), (width, BF), (3 * width, BF)]
+    outs = [(tokens, width, F32), (tokens, width, BF), (tokens, ff, BF), (tokens, ff, BF)]
+    out_specs = [tile(block, w) for _, w, _ in outs]
+    if last:
+        outs += [(tokens // 2, width, BF)] * 2
+        out_specs += halves(tokens, block, width)
+    else:
+        outs += [(tokens, width, F32), (tokens, width, BF), (tokens, 3 * width, BF)]
+        out_specs += [tile(block, w) for _, w, _ in outs[4:]]
     flops = 2 * tokens * width * (width + 2 * ff + (0 if last else 3 * width))
     return pl.pallas_call(
-        functools.partial(post_kernel, last, 4, len(xs)),
+        functools.partial(post_kernel, d, last, parts, len(xs)),
         grid=(tokens // block,),
-        in_specs=[tile(block, width)] + x_specs + specs,
-        out_specs=[tile(block, w) for w, _ in outs],
-        out_shape=[sds(tokens, w, t) for w, t in outs],
+        in_specs=[tile(block, width)] + x_specs + specs + anywhere(weights),
+        out_specs=out_specs,
+        out_shape=[sds(*o) for o in outs],
+        scratch_shapes=[pltpu.VMEM(params[n].shape[1:], BF) for n in weights]
+        + [pltpu.SemaphoreType.DMA((2 * parts + 2,))],
         compiler_params=VMEM,
         cost_estimate=cost(flops, tokens * ff * 10, 2 * tokens * ff),
         name="post",
@@ -465,111 +508,8 @@
     return jnp.concatenate([dot_tn(left, right) for left in lefts], 0).astype(BF)
 
 
-def deal(left_ref, right_ref, rows, start, refs, at):
-    total = left_ref.shape[1]
-
-    def store(mine):
-        result = dot_tn(left_ref[...], right_ref[...])
-        place = (lambda o: o) if mine is None else chunk_of
-        owner = start // rows
-        base = 0 if refs[0].shape[0] == place(31) + 1 else place(owner)
-        while owner * rows < start + total:
-            low = max(owner * rows, start)
-            high = min((owner + 1) * rows, start + total)
-            ref = refs[0] if mine is None or (owner >> 1) & 1 == mine else refs[1]
-            to = at + low - owner * rows
-            ref[place(owner) - base, to : to + high - low, :] = result[
-                low - start : high - start
-            ].astype(BF)
-            owner += 1
-
-    if len(refs) == 1:
-        store(None)
-        return
-    core = lax.axis_index("dp") & 1
-    for mine in range(2):
-        pl.when(core == mine)(functools.partial(store, mine))
-
-
 def chunk_of(owner):
     return (owner >> 2) * 2 + (owner & 1)
-
-
-def grad_kernel(rows, by_left, n_out, left_ref, right_ref, *refs):
-    sum_ref = refs[-1]
-    deal(left_ref, right_ref, rows, 0, refs[-1 - n_out : -1], 0)
-
-    @pl.when(jnp.logical_or(by_left, pl.program_id(0) == 0))
-    def _():
-        sum_ref[...] = jnp.broadcast_to(colsum(left_ref[...].astype(F32)), sum_ref.shape)
-
-
-def grad_call(left, right, into, total, rows, offset, by_left, n_out=2, deps=()):
-    tokens, wide = left.shape
-    block = 768
-    places = 32 // n_out
-    deep = right.shape[1]
-    if by_left:
-        steps = wide // block
-        lspec = pl.BlockSpec((tokens, block), lambda i: (0, i))
-        rspec = pl.BlockSpec((tokens, block), lambda i: (0, 0))
-        out = pl.BlockSpec((places // steps, rows, block), lambda i: (i, offset // rows, 0))
-        sums = pl.BlockSpec((8, block), lambda i: (0, i))
-    else:
-        steps = deep // block
-        lspec = pl.BlockSpec((tokens, block), lambda i: (0, 0))
-        rspec = pl.BlockSpec((tokens, block), lambda i: (0, i))
-        out = pl.BlockSpec((places, rows, block), lambda i: (0, offset // rows + i, 0))
-        sums = pl.BlockSpec((8, block), lambda i: (0, 0))
-    extra = list(into or ()) + list(deps)
-    shape = jax.ShapeDtypeStruct((places, total, block), BF)
-    return pl.pallas_call(
-        functools.partial(grad_kernel, rows, by_left, n_out),
-        grid=(steps,),
-        in_specs=[lspec, rspec] + anywhere(extra),
-        out_specs=[out] * n_out + [sums],
-        out_shape=[shape] * n_out + [sds(8, wide, F32)],
-        input_output_aliases={2 + n: n for n in range(len(into or ()))},
-        compiler_params=VMEM,
-        cost_estimate=cost(2 * tokens * wide * deep, 2 * (tokens + 16) * (wide + deep)),
-        name="grad",
-    )(left, right, *extra)
-
-
-def qkv_grad_kernel(rows, n_out, left_ref, right_ref, *refs):
-    sum_ref = refs[-1]
-    step = pl.program_id(0)
-    for n in range(3):
-
-        @pl.when(step == n)
-        def _():
-            deal(left_ref, right_ref, rows, n * left_ref.shape[1], refs[-1 - n_out : -1], 0)
-
-    sum_ref[...] = jnp.broadcast_to(colsum(left_ref[...].astype(F32)), sum_ref.shape)
-
-
-def qkv_grad(grads, n1, into, total, n_out=2, deps=()):
-    _, tokens, width = grads.shape
-    rows = 3 * width // 32
-    places = 32 // n_out
-    extra = list(into or ()) + list(deps)
-    shape = jax.ShapeDtypeStruct((places, total, width), BF)
-    out = pl.BlockSpec((places, rows, width), lambda i: (0, total // rows - 1, 0))
-    return pl.pallas_call(
-        functools.partial(qkv_grad_kernel, rows, n_out),
-        grid=(3,),
-        in_specs=[
-            pl.BlockSpec((None, tokens, width), lambda i: (i, 0, 0)),
-            pl.BlockSpec((tokens, width), lambda i: (0, 0)),
-        ]
-        + anywhere(extra),
-        out_specs=[out] * n_out + [pl.BlockSpec((8, width), lambda i: (0, i))],
-        out_shape=[shape] * n_out + [sds(8, 3 * width, F32)],
-        input_output_aliases={2 + n: n for n in range(len(into or ()))},
-        compiler_params=VMEM,
-        cost_estimate=cost(6 * tokens * width * width, 16 * tokens * width),
-        name="qkv_grad",
-    )(grads, n1, *extra)
 
 
 ROWS = 512
@@ -602,9 +542,6 @@
             late = n - 2 * parts
             pair = (sources[2].at[d], sources[3], sources[4])[late], (wout, n2, mixed)[late]
         return pltpu.make_async_copy(*pair, arrive.at[n])
-
-    def arrived(n):
-        pl.when(step == 0)(lambda: load(n).wait())
 
     @pl.when(step == 0)
     def _():
@@ -637,8 +574,7 @@
             at = owner if n_out == 1 else ((owner >> 1) & 1) * (count // 2) + chunk_of(owner)
             held[slot, at] = result[owner * tall : (owner + 1) * tall].astype(BF)
 
-    @pl.when(step < blocks)
-    def _():
+    def body(wait):
         rows = pl.ds(pl.multiple_of(step * ROWS, ROWS), ROWS)
         fresh = step == 0
         gx = joined_rows(gx_refs, step)
@@ -647,11 +583,11 @@
         g_n2 = None
         for j in range(parts):
             cols = slice(j * width, (j + 1) * width)
-            arrived(2 * j)
+            wait(2 * j)
             g_act = dot_nt(gy, wdown[cols, :])
             gu = (g_act * slope_ref[:, cols].astype(F32)).astype(BF)
             gu_all[rows, cols] = gu
-            arrived(2 * j + 1)
+            wait(2 * j + 1)
             part = dot_nt(gu, wup[:, cols])
             g_n2 = part if g_n2 is None else g_n2 + part
         xhat, rstd = normalize(resid_ref[...])
@@ -659,15 +595,21 @@
         gres_ref[...] = g_resid
         ga = g_resid.astype(BF)
         ga_all[rows, :] = ga
-        arrived(2 * parts)
+        wait(2 * parts)
         gmix_ref[...] = dot_nt(ga, wout[...]).astype(BF)
         add_row(vec_ref, 0, 0, colsum(g_n2 * xhat), fresh)
         add_row(vec_ref, 0, width, colsum(g_n2), fresh)
         add_row(vec_ref, 0, 2 * width, colsum(gy.astype(F32)), fresh)
         add_row(vec_ref, 0, 3 * width, colsum(ga.astype(F32)), fresh)
 
-    arrived(2 * parts + 1)
-    arrived(2 * parts + 2)
+    pl.when(step == 0)(lambda: body(lambda n: load(n).wait()))
+    pl.when(jnp.logical_and(step > 0, step < blocks))(lambda: body(lambda n: None))
+
+    @pl.when(step == blocks)
+    def _():
+        load(2 * parts + 1).wait()
+        load(2 * parts + 2).wait()
+
     for j in range(parts):
 
         @pl.when(step == blocks + j)
@@ -753,6 +695,152 @@
     )(*ops, *extra)
 
 
+def vector_piece(square, long, owner):
+    tall = long.shape[0] // 32
+    thin = square.shape[0] // 32
+    piece = long[owner * tall : (owner + 1) * tall]
+    top = piece[:thin] + square[owner * thin : (owner + 1) * thin]
+    piece = jnp.concatenate([top, piece[thin:]], 0)
+    return jnp.concatenate([piece[16 * m : 16 * m + 16] for m in range(tall // 16)], 1)
+
+
+def turned_vectors(found):
+    width = found[0][0].shape[1] // 4
+    rows, ups = [], []
+    for proj_vec, ff_vec in found:
+        p = [proj_vec[0:1, n * width : (n + 1) * width] for n in range(4)]
+        f = [ff_vec[0:1, n * width : (n + 1) * width] for n in range(4)]
+        rows += [p[0], f[0], p[1], f[1], p[2], p[3], f[3], f[2]]
+        ups.append(ff_vec[1:2])
+    square = jnp.concatenate(rows + [jnp.zeros((128 - len(rows), width), F32)], 0)
+    before, after = len(rows), 128 - len(rows) - len(ups)
+    zeros = lambda n: jnp.zeros((n, 4 * width), F32)
+    long = jnp.concatenate([zeros(before)] + ups + [zeros(after)], 0)
+    return square.T, long.T
+
+
+def qkv_all_kernel(d, n_x, row0, *refs):
+    it = iter(refs)
+    g_hbm, n1_hbm, w_hbm, gres_hbm, gain_ref = [next(it) for _ in range(5)]
+    x_hbm = [next(it) for _ in range(n_x)]
+    others = [next(it) for _ in range(3 if n_x == 2 else 0)]
+    n_g = 1 if n_x == 1 else 2
+    outs = [next(it) for _ in range(n_g)]
+    vec_ref, keep, send = next(it), next(it), next(it)
+    g_all, n1, wqkv, gres, x_all, held, arrive, leave = [next(it) for _ in range(8)]
+    gx_held = list(it)
+    _, tokens, width = g_all.shape
+    half = tokens // 2
+    rows = 3 * width // 32
+    core = lax.axis_index("dp") & 1
+    pairs = [(g_hbm.at[0], g_all.at[0]), (n1_hbm, n1), (g_hbm.at[1], g_all.at[1])]
+    pairs += [(g_hbm.at[2], g_all.at[2]), (w_hbm.at[d], wqkv), (gres_hbm, gres)]
+    if n_x == 1:
+        pairs.append((x_hbm[0], x_all))
+    else:
+        pairs += [(x_hbm[n], x_all.at[pl.ds(n * half, half)]) for n in range(2)]
+    loads = [pltpu.make_async_copy(a, b, arrive.at[n]) for n, (a, b) in enumerate(pairs)]
+    for copy in loads:
+        copy.start()
+    loads[0].wait()
+    loads[1].wait()
+    for n in range(3):
+        if n:
+            loads[n + 1].wait()
+        left = g_all[n]
+        result = dot_tn(left, n1[...])
+        if n != 1:
+            at = 2 * width if n == 0 else 3 * width
+            vec_ref[0:1, at : at + width] = colsum(left.astype(F32))
+        owner = n * width // rows
+        while owner * rows < (n + 1) * width:
+            low, high = max(owner * rows, n * width), min((owner + 1) * rows, (n + 1) * width)
+            to = low - owner * rows
+            held[(owner >> 1) & 1, chunk_of(owner), to : to + high - low, :] = result[
+                low - n * width : high - n * width
+            ].astype(BF)
+            owner += 1
+    tall = held.shape[2]
+    stores = [
+        pltpu.make_async_copy(
+            held.at[core if n == 0 else 1 - core], buf.at[:, pl.ds(row0, tall)], leave.at[n]
+        )
+        for n, buf in enumerate((keep, send))
+    ]
+    if not others:
+        for copy in stores:
+            copy.start()
+    for copy in loads[4:]:
+        copy.wait()
+    sums = []
+    for n in (1, 0):
+        part = slice(n * half, (n + 1) * half)
+        g = jnp.concatenate([g_all[m, part, :] for m in range(3)], 1)
+        g_norm = dot_nt(g, wqkv[...])
+        xhat, rstd = normalize(x_all[part, :].astype(F32))
+        gx = gres[part, :] + norm_back(g_norm, xhat, rstd, gain_ref[...])
+        scratch = gx_held[n if n_g == 2 else 0]
+        if n_g == 2:
+            scratch[...] = gx.astype(scratch.dtype)
+            copy = pltpu.make_async_copy(scratch, outs[n], leave.at[2 + n])
+        else:
+            scratch[part, :] = gx
+            span = pl.ds(n * half, half)
+            copy = pltpu.make_async_copy(scratch.at[span], outs[0].at[span], leave.at[2 + n])
+        copy.start()
+        stores.append(copy)
+        sums.append((colsum(g_norm * xhat), colsum(g_norm)))
+    vec_ref[0:1, :width] = sums[0][0] + sums[1][0]
+    vec_ref[0:1, width : 2 * width] = sums[0][1] + sums[1][1]
+    if others:
+        square, long = turned_vectors([(vec_ref, others[0]), (others[1], others[2])])
+        for owner in range(32):
+            piece = vector_piece(square, long, owner).astype(BF)
+            held[(owner >> 1) & 1, chunk_of(owner), rows:, :] = piece
+        for copy in stores[:2]:
+            copy.start()
+    for copy in stores:
+        copy.wait()
+
+
+def qkv_all(grads, n1, xs, g_resid, params, d, total, row0, vecs=()):
+    _, tokens, width = grads.shape
+    half = tokens // 2
+    rows = 3 * width // 32
+    ops = [grads, n1, params["wqkv"], g_resid, params["gains"], *xs, *vecs]
+    hbm = pl.BlockSpec(memory_space=pl.ANY)
+    vec = pl.BlockSpec((8, 4 * width), lambda i: (0, 0))
+    specs = [hbm] * 4 + [layer(params["gains"], d, 0)] + [hbm] * len(xs) + [vec] * len(vecs)
+    vm = pltpu.VMEM
+    if len(xs) == 1:
+        g_outs, g_held = [sds(tokens, width, F32)], [vm((tokens, width), F32)]
+    else:
+        g_outs = [sds(half, width, F32), sds(half, width, BF)]
+        g_held = [vm((half, width), F32), vm((half, width), BF)]
+    buf = jax.ShapeDtypeStruct((16, total, width), BF)
+    return pl.pallas_call(
+        functools.partial(qkv_all_kernel, d, len(xs), row0),
+        grid=(1,),
+        in_specs=specs,
+        out_specs=[hbm] * len(g_outs) + [vec, hbm, hbm],
+        out_shape=g_outs + [sds(8, 4 * width, F32), buf, buf],
+        scratch_shapes=[
+            vm((3, tokens, width), BF),
+            vm((tokens, width), BF),
+            vm((width, 3 * width), BF),
+            vm((tokens, width), F32),
+            vm((tokens, width), xs[0].dtype),
+            vm((2, 16, rows + (16 if vecs else 0), width), BF),
+            pltpu.SemaphoreType.DMA((8,)),
+            pltpu.SemaphoreType.DMA((4,)),
+        ]
+        + g_held,
+        compiler_params=VMEM,
+        cost_estimate=cost(1, 1),
+        name="qkv_all",
+    )(*ops)
+
+
 def plus(*parts):
     total = parts[0].astype(F32)
     for part in parts[1:]:
@@ -764,22 +852,15 @@
     return (lax.axis_index("dp") >> 1) & 1, lax.axis_index("blk")
 
 
-def stage1_kernel(tall, has_vec, keep, recv, *refs):
-    kp, sp, kq, sq = refs[-4:]
+def stage1_kernel(tall, keep, recv, kp, sp, kq, sq):
     x, y = place_xy()
     both = lambda a, b, rows: plus(keep[0, a, b, rows], recv[0, a, b, rows]).astype(BF)
     up, low = slice(0, tall), slice(tall, keep.shape[3])
-    stop = keep.shape[3] - tall
     for n in range(2):
         kp[0, n] = both(x, n, up)
         sp[0, n] = both(1 - x, n, up)
-        kq[0, n, :stop] = both(n, y, low)
-        sq[0, n, :stop] = both(n, 1 - y, low)
-    if has_vec:
-        vk, vr = refs[:2]
-        for n in range(2):
-            kq[0, n, stop:] = plus(vk[0, n, y], vr[0, n, y]).astype(BF)
-            sq[0, n, stop:] = plus(vk[0, n, 1 - y], vr[0, n, 1 - y]).astype(BF)
+        kq[0, n] = both(n, y, low)
+        sq[0, n] = both(n, 1 - y, low)
 
 
 def stage2_kernel(kp, rp, kq, rq, kp2, sp2, kq2, sq2):
@@ -823,17 +904,13 @@
         self.tall, self.dp = tall, dp
         self.keep, self.recv = keep, xor_permute(send, dp, 1)
 
-    def stage1(self, vec=None, deps=()):
+    def stage1(self, deps=()):
         _, total, width = self.keep.shape
         tall = self.tall
-        cut = lambda a: a.reshape(4, 2, 2, a.shape[1], width)
+        cut = lambda a: a.reshape(4, 2, 2, total, width)
         ops = [cut(self.keep), cut(self.recv)]
-        low = total - tall
-        if vec is not None:
-            ops += [cut(v) for v in vec]
-            low += vec[0].shape[1]
-        p, q = (4, 2, tall, width), (4, 2, low, width)
-        kernel = functools.partial(stage1_kernel, tall, vec is not None)
+        p, q = (4, 2, tall, width), (4, 2, total - tall, width)
+        kernel = functools.partial(stage1_kernel, tall)
         self.kp, sp, self.kq, sq = stage_call(kernel, "stage1", ops, [p, p, q, q], deps)
         self.rp, self.rq = xor_permute(sp, self.dp, 2), swap_halves(sq)
         return [self.kp]
@@ -883,18 +960,20 @@
         thin = outs["down"].shape[1]
         for j in range(down.shape[0] // thin):
             outs["down"][d, :, j * width : (j + 1) * width] = down[j * thin : (j + 1) * thin]
-    vec = rows(*layout["vec"])[0:1]
-    at = 0
+    vec = rows(*layout["vec"])
+    lanes = [vec[:, 128 * m : 128 * m + 128] for m in range(width // 128)]
+    lanes.append(jnp.zeros((128 - 16 * len(lanes), 128), F32))
+    turned = jnp.concatenate(lanes, 0).T
+    short = len(VECTORS) - 1
     for d in range(LAYERS):
-        for name, n in layout["vectors"]:
+        for at, (name, n) in enumerate(VECTORS):
             ref = outs[name]
-            size = ref.shape[-1]
-            value = vec[:, at : at + size]
+            row = d * short + at if at < short else LAYERS * short + d
+            value = turned[row : row + 1, : ref.shape[-1]]
             if n is None:
                 ref[d : d + 1, :] = value
             else:
                 ref[d, n : n + 1, :] = value
-            at += size
 
 
 VECTORS = (
@@ -913,7 +992,7 @@
 def finish(layout, groups, shapes):
     ops = [a for g in groups for a in g]
     names = list(shapes)
-    layout = dict(layout, outs=names, vectors=VECTORS)
+    layout = dict(layout, outs=names)
     total = sum(math.prod(a.shape) for a in ops) * 2
     return dict(
         zip(
@@ -1059,9 +1138,8 @@
         if not last:
             x, n1, proj = outs[4:]
             xs = (x,)
-    out16 = outs[4]
-    returned = swap_halves(out16[half:])
-    hidden_out = return_cell(out16[:half], returned)
+    returned = swap_halves(outs[5])
+    hidden_out = return_cell(outs[4], returned)
 
     gxs = split_cell(cotangent)
     backward = backward_grouped if grouped else backward_plain
@@ -1080,7 +1158,7 @@
             ln1[d][width:],
             ln2[d][width:],
             sums["qkv", d][:width],
-            sums["qkv", d][2 * width :],
+            sums["qkv", d][-width:],
             sums["out", d],
             sums["down", d],
             sums["up", d],
@@ -1121,59 +1199,42 @@
 
 def backward_grouped(mesh, params, saved, gxs, meta, early):
     dp = mesh.shape["dp"]
-    ln1, ln2, cols = {}, {}, {}
-    tokens, width = saved[0][6].shape
-    half, t, pairs = tokens // 2, width // 32, width // 128
+    width = saved[0][6].shape[1]
+    t, pairs = width // 32, width // 128
 
     def ff_grads(gxs, d, into, total, n_out):
         mixed, resid, n2, active, slope = saved[d][3], *saved[d][6:]
         g_resid, g_mixed, vec, *bufs = ff_all(
             gxs, slope, resid, active, n2, mixed, params, d, into, total, n_out
         )
-        ln2[d] = vec[0, : 2 * width]
-        cols["down", d], cols["out", d] = vec[0, 2 * width : 3 * width], vec[0, 3 * width :]
-        cols["up", d] = vec[1]
-        return g_resid, g_mixed, bufs
-
-    xs, n1, proj, mixed, low, lse, resid, n2, active, slope = saved[1]
-    g_resid, g_mixed, bufs = ff_grads(gxs, 1, None, 9 * t, 1)
+        return g_resid, g_mixed, vec, bufs
+
+    xs, n1, proj, mixed, low, lse = saved[1][:6]
+    g_resid, g_mixed, ff_vec1, bufs = ff_grads(gxs, 1, None, 9 * t, 1)
     layer1 = lax.psum_scatter(bufs[0], ("dp", "blk"), scatter_dimension=0, tiled=True)[0]
     grads = attn_bwd(proj, mixed, low, g_mixed, lse, meta, (0, pairs), None, bufs + early)
-    *bufs, sums = qkv_grad(grads, n1, None, 12 * t)
-    cols["qkv", 1] = sums[0]
-    gx, vec = qkv_back(grads, xs[0], g_resid, params, 1, 0, tokens, F32, bufs)
-    ln1[1] = vec[0]
-    xs, n1, proj, mixed, low, lse, resid, n2, active, slope = saved[0]
-    g_resid, g_mixed, bufs = ff_grads((gx,), 0, bufs, 12 * t, 2)
+    gx, proj_vec1, *bufs = qkv_all(grads, n1, xs, g_resid, params, 1, 12 * t, 9 * t)
+    xs, n1, proj, mixed, low, lse = saved[0][:6]
+    g_resid, g_mixed, ff_vec0, bufs = ff_grads((gx,), 0, bufs, 12 * t, 2)
     ff0 = Group(*bufs, 6 * t, dp)
     grads = attn_bwd(proj, mixed, low, g_mixed, lse, meta, (0, 2), None, [ff0.keep])
     dep = ff0.stage1(deps=[grads])
     grads = attn_bwd(proj, mixed, low, g_mixed, lse, meta, (2, pairs), grads, dep)
-    *bufs, sums = qkv_grad(grads, n1, None, 3 * t)
-    cols["qkv", 0] = sums[0]
-    at0 = Group(*bufs, 48, dp)
-    theirs, vec_a = qkv_back(grads, xs[1], g_resid, params, 0, half, half, BF, [at0.keep])
-    back = swap_halves(theirs)
+    vecs = (ff_vec0, proj_vec1, ff_vec1)
+    mine, theirs, _, *bufs = qkv_all(grads, n1, xs, g_resid, params, 0, 3 * t + 16, 0, vecs)
     dep = ff0.stage2(deps=[theirs])
-    mine, vec_b = qkv_back(grads, xs[0], g_resid, params, 0, 0, half, F32, dep)
-    ln1[0] = vec_a[0] + vec_b[0]
-    vec = vector_rows(32, width, ln1, ln2, cols)
-    vec = jnp.pad(vec, ((0, 0), (0, width - vec.shape[1]))).astype(BF)
-    vec = jnp.pad(vec[:, None], ((0, 0), (0, 7), (0, 0))).reshape(8, 2, 2, 8, width)
-    core = lax.axis_index("dp") & 1
-    deal_core = lambda core: lax.dynamic_index_in_dim(vec, core, 1, False).reshape(16, 8, width)
-    kept, sent = deal_core(core), deal_core(1 - core)
-    vec = [kept, xor_permute(sent, dp, 1)]
-    dep = at0.stage1(vec, deps=[back])
+    at0 = Group(bufs[0], after(bufs[1], dep), 48, dp)
+    dep = at0.stage1(deps=dep)
     dep = ff0.stage3(deps=dep)
     dep = at0.stage2(deps=dep)
-    at0.stage3(deps=ff0.pieces[1:])
+    dep = at0.stage3()
+    back = swap_halves(after(theirs, dep))
     layout = {
         "rows": [
             {"down": (1, 0, 4 * t), "up": (1, 4 * t, 4 * t), "out": (1, 8 * t, t), "qkv": (2, 0, 3 * t)},
             {"down": (0, 0, 4 * t), "up": (0, 4 * t, 4 * t), "out": (0, 8 * t, t), "qkv": (1, 9 * t, 3 * t)},
         ],
-        "vec": (2, 3 * t, 8),
+        "vec": (2, 3 * t, 16),
     }
     shapes = {
         "qkv": (LAYERS, 3 * t, width),

time: 475 us -> 463 us (0.975)
  waiting for transfers between devices: 62.7 us -> 77 us
  Pallas kernels: 335 us -> 324 us
    ppermute x13 -> x12, waiting for transfers between devices: 34.9 us -> 50.1 us  [xor_permute(): return lax.ppermute(x, 'dp', [(i, i ^ mask) for i in range(dp)])]
    pallas_call x7 -> x4, Pallas kernels: 91.2 us -> 82.2 us  [the longest x2 51.5 us: post(): pl.pallas_call(functools.partial(post_kernel, d, last, parts, len(xs)), g...]
    ppermute x13 -> x12, starting transfers between devices: 17.1 us -> 15.7 us  [xor_permute(): return lax.ppermute(x, 'dp', [(i, i ^ mask) for i in range(dp)])]
  transfers between devices with their start and end apart: 22 -> 21, of which waited for: 9 -> 13; matrix products, arithmetic and copies ran while one was open for 4% -> 2% of each run, Pallas kernels for 71% -> 70%
where the time goes in v3:
time: 463 us; the launch traced here: 458 us
  Pallas kernels  324 us (70%)
  waiting for transfers between devices  77 us (17%)
  starting transfers between devices  23.7 us (5%)
  local copies, waits for them, and re-layouts  15.6 us (3%)
  between operations  14.6 us (3%)
    pallas_call x2, Pallas kernels, ff_all(): pl.pallas_call(functools.partial(ff_all_kernel, len(gxs), n_out, 0, d), g...  84.4 us
    pallas_call x3, Pallas kernels, attn_bwd(): pl.pallas_call(ordered(attn_bwd_kernel, len(ops), extra), grid_spec=pltpu...  73 us
    pallas_call x2, Pallas kernels, post(): pl.pallas_call(functools.partial(post_kernel, d, last, parts, len(xs)), g...  51.5 us
    ppermute x12, waiting for transfers between devices, xor_permute(): return lax.ppermute(x, 'dp', [(i, i ^ mask) for i in range(dp)])  50.1 us
    pallas_call x2, Pallas kernels, attn_fwd(): pl.pallas_call(functools.partial(attn_fwd_kernel, tokens // 2, 2), grid_s...  42.1 us
    pallas_call x2, Pallas kernels, qkv_all(): pl.pallas_call(functools.partial(qkv_all_kernel, d, len(xs), row0), grid=...  30.8 us
    ppermute x8, waiting for transfers between devices, swap_halves(): return lax.ppermute(x, 'blk', [(0, 1), (1, 0)])  26.9 us
    pallas_call x4, Pallas kernels, stage_call(): pl.pallas_call(ordered(kernel, len(ops), deps), grid=(ops[0].shape[0],),...  21.5 us
  transfers between devices with their start and end apart: 21, of which 13 were waited for; matrix products, arithmetic and copies ran while one was open for 2% of the time, Pallas kernels for 70%

profile of v3, /device:TPU:0, one launch (start us, length us, event | category | flops | bytes accessed | tf_op | source)
XLA Modules:
  0.0 457.9 jit_solution(2283236054012107703)
XLA Ops:
  7.2 2.5 dynamic-slice_bitcast_fusion.2
  9.8 3.0 collective-permute-start
  17.5 5.8 %enter.2 = (bf16[1024,768]{1,0:T(8,128)(2,1)}, bf16[1024,2304]{1,0:T(8,128)(2,1)}) custom-call(bf16[512,768]{1,0:T(8,128)(2,1)} %get-tuple-element.169.x_ref.refs_1_.refs_5_, f32[2,2,1,768]{3,2,1,0:T(1,128)} %broadcast_in_dim.21.gain_ref.refs_4_.refs_8_.refs_3_, f32[2,2,1,768]{3,2,1,0:T(1,128)} %broadcast_in_dim.22.shift_ref.refs_5_.refs_9_.refs_4_, ...), custom_call_target="tpu_custom_call" | custom-call | flops 1811939328 | bytes 7471104 | tf_op jit(solution)/shard_map/enter/pallas_call | solution.py:259
  23.3 7.8 %collective-permute-done.x_ref.refs_2_.refs_6_ = bf16[512,768]{1,0:T(8,128)(2,1)S(1)} collective-permute-done((bf16[512,768]{1,0:T(8,128)(2,1)S(1)}, bf16[512,768]{1,0:T(8,128)(2,1)S(1)}, u32[]{:S(2)}, u32[]{:S(2)}) %collective-permute-start) | collective-permute-done | bytes 786464 | tf_op jit(solution)/shard_map/ppermute | solution.py:1012
  32.0 5.8 %enter.3 = (bf16[1024,768]{1,0:T(8,128)(2,1)}, bf16[1024,2304]{1,0:T(8,128)(2,1)}) custom-call(bf16[512,768]{1,0:T(8,128)(2,1)} %copy-done, f32[2,2,1,768]{3,2,1,0:T(1,128)} %broadcast_in_dim.21.gain_ref.refs_4_.refs_8_.refs_3_, f32[2,2,1,768]{3,2,1,0:T(1,128)} %broadcast_in_dim.22.shift_ref.refs_5_.refs_9_.refs_4_, ...), custom_call_target="tpu_custom_call", output_to_operand_aliasing={{0}: (5, {}), {1}: (6, {})} | custom-call | flops 1811939328 | bytes 7471104 | tf_op jit(solution)/shard_map/enter/pallas_call | solution.py:259
  37.9 20.8 %attn_fwd.2 = (bf16[1024,768]{1,0:T(8,128)(2,1)}, bf16[1024,768]{1,0:T(8,128)(2,1)}, f32[6,8,1024]{2,1,0:T(8,128)}) custom-call(s32[2]{0:T(128)} %refs_0_.5, bf16[1024,2304]{1,0:T(8,128)(2,1)} %get-tuple-element.92.q_ref.k_ref.v_ref.refs_1_.refs_2_.refs_3_, bf16[1024,2304]{1,0:T(8,128)(2,1)} %get-tuple-element.92.q_ref.k_ref.v_ref.refs_1_.refs_2_.refs_3_, ...), custom_call_target="tpu_custom_call" | custom-call | flops 9663676416 | bytes 6291456 | tf_op jit(solution)/shard_map/attn_fwd/pallas_call | solution.py:95
  58.7 28.9 %post.2 = (f32[1024,768]{1,0:T(8,128)}, bf16[1024,768]{1,0:T(8,128)(2,1)}, bf16[1024,3072]{1,0:T(8,128)(2,1)}, bf16[1024,3072]{1,0:T(8,128)(2,1)}, f32[1024,768]...) custom-call(bf16[1024,768]{1,0:T(8,128)(2,1)} %get-tuple-element.93.refs_0_.refs_9_.refs_4_, ...), custom_call_target="tpu_custom_call" | custom-call | flops 14495514624 | bytes 31457280 | tf_op jit(solution)/shard_map/post/pallas_call | solution.py:383
  87.6 21.3 %attn_fwd.3 = (bf16[1024,768]{1,0:T(8,128)(2,1)}, bf16[1024,768]{1,0:T(8,128)(2,1)}, f32[6,8,1024]{2,1,0:T(8,128)}) custom-call(s32[2]{0:T(128)} %refs_0_.5, bf16[1024,2304]{1,0:T(8,128)(2,1)} %get-tuple-element.94.q_ref.k_ref.v_ref.refs_1_.refs_2_.refs_3_, bf16[1024,2304]{1,0:T(8,128)(2,1)} %get-tuple-element.94.q_ref.k_ref.v_ref.refs_1_.refs_2_.refs_3_, ...), custom_call_target="tpu_custom_call" | custom-call | flops 9663676416 | bytes 6291456 | tf_op jit(solution)/shard_map/attn_fwd/pallas_call | solution.py:95
  108.9 22.6 %post.3 = (f32[1024,768]{1,0:T(8,128)}, bf16[1024,768]{1,0:T(8,128)(2,1)}, bf16[1024,3072]{1,0:T(8,128)(2,1)}, bf16[1024,3072]{1,0:T(8,128)(2,1)}, bf16[512,768]{1,0:T(8,128)(2,1)}, /*index=5*/bf16[512,768]{1,0:T(8,128)(2,1)}) custom-call(bf16[1024,768]{1,0:T(8,128)(2,1)} %get-tuple-element.95.refs_0_.refs_10_.refs_4_, ...), custom_call_target="tpu_custom_call" | custom-call | flops 10871635968 | bytes 31457280 | tf_op jit(solution)/shard_map/post/pallas_call | solution.py:383
  134.5 40.8 %ff_all.2 = (f32[1024,768]{1,0:T(8,128)}, bf16[1024,768]{1,0:T(8,128)(2,1)}, f32[8,3072]{1,0:T(8,128)}, bf16[32,216,768]{2,1,0:T(8,128)(2,1)}) custom-call(bf16[512,768]{1,0:T(8,128)(2,1)} %get-tuple-element.168.refs_0_, bf16[512,768]{1,0:T(8,128)(2,1)} %copy-done.29, bf16[1024,3072]{1,0:T(8,128)(2,1)} %get-tuple-element.101.refs_2_, ...), custom_call_target="tpu_custom_call" | custom-call | flops 21743271936 | bytes 52428800 | tf_op jit(solution)/shard_map/ff_all/pallas_call | solution.py:682
  176.2 35.0 %attn_bwd.3.refs_0_ = bf16[3,1024,768]{2,1,0:T(8,128)(2,1)} custom-call(s32[2]{0:T(128)} %refs_0_.5, bf16[1024,2304]{1,0:T(8,128)(2,1)} %get-tuple-element.94.q_ref.k_ref.v_ref.refs_1_.refs_2_.refs_3_, bf16[1024,2304]{1,0:T(8,128)(2,1)} %get-tuple-element.94.q_ref.k_ref.v_ref.refs_1_.refs_2_.refs_3_, ...), custom_call_target="tpu_custom_call" | custom-call | flops 1 | bytes 1 | tf_op jit(solution)/shard_map/attn_bwd/pallas_call | solution.py:162
  211.2 14.5 %qkv_all.2 = (f32[1024,768]{1,0:T(8,128)}, f32[8,3072]{1,0:T(8,128)}, bf16[16,288,768]{2,1,0:T(8,128)(2,1)}, bf16[16,288,768]{2,1,0:T(8,128)(2,1)}) custom-call(bf16[3,1024,768]{2,1,0:T(8,128)(2,1)} %attn_bwd.3.refs_0_, bf16[1024,768]{1,0:T(8,128)(2,1)} %get-tuple-element.108.refs_1_, bf16[2,768,2304]{2,1,0:T(8,128)(2,1)} %refs_2_.3, ...), custom_call_target="tpu_custom_call" | custom-call | flops 1 | bytes 1 | tf_op jit(solution)/shard_map/qkv_all/pallas_call | solution.py:821
  225.7 43.6 %ff_all.3 = (f32[1024,768]{1,0:T(8,128)}, bf16[1024,768]{1,0:T(8,128)(2,1)}, f32[8,3072]{1,0:T(8,128)}, bf16[16,288,768]{2,1,0:T(8,128)(2,1)}, bf16[16,288,768]{2,1,0:T(8,128)(2,1)}) custom-call(f32[1024,768]{1,0:T(8,128)} %get-tuple-element.110.refs_0_, ...), custom_call_target="tpu_custom_call", output_to_operand_aliasing={{3}: (10, {}), {4}: (11, {})} | custom-call | flops 21743271936 | bytes 52428800 | tf_op jit(solution)/shard_map/ff_all/pallas_call | solution.py:682
  269.4 13.6 %attn_bwd.4.refs_2_.refs_8_ = bf16[3,1024,768]{2,1,0:T(8,128)(2,1)} custom-call(s32[2]{0:T(128)} %refs_0_.5, bf16[1024,2304]{1,0:T(8,128)(2,1)} %get-tuple-element.92.q_ref.k_ref.v_ref.refs_1_.refs_2_.refs_3_, bf16[1024,2304]{1,0:T(8,128)(2,1)} %get-tuple-element.92.q_ref.k_ref.v_ref.refs_1_.refs_2_.refs_3_, ...), custom_call_target="tpu_custom_call" | custom-call | flops 1 | bytes 1 | tf_op jit(solution)/shard_map/attn_bwd/pallas_call | solution.py:162
  283.0 8.3 %stage1.2 = (bf16[4,2,144,768]{3,2,1,0:T(8,128)(2,1)}, bf16[4,2,144,768]{3,2,1,0:T(8,128)(2,1)}, bf16[4,2,144,768]{3,2,1,0:T(8,128)(2,1)}, bf16[4,2,144,768]{3,2,1,0:T(8,128)(2,1)}) custom-call(bf16[4,2,2,288,768]{4,3,2,1,0:T(8,128)(2,1)} %bitcast.23, bf16[4,2,2,288,768]{4,3,2,1,0:T(8,128)(2,1)} %bitcast.7.refs_1_, bf16[3,1024,768]{2,1,0:T(8,128)(2,1)} %attn_bwd.4.refs_2_.refs_8_), custom_call_target="tpu_custom_call" | custom-call | flops 21233664 | bytes 21233664 | tf_op jit(solution)/shard_map/stage1/pallas_call | solution.py:886
  293.2 24.4 %attn_bwd.5.refs_0_ = bf16[3,1024,768]{2,1,0:T(8,128)(2,1)} custom-call(s32[2]{0:T(128)} %refs_0_.5, bf16[1024,2304]{1,0:T(8,128)(2,1)} %get-tuple-element.92.q_ref.k_ref.v_ref.refs_1_.refs_2_.refs_3_, bf16[1024,2304]{1,0:T(8,128)(2,1)} %get-tuple-element.92.q_ref.k_ref.v_ref.refs_1_.refs_2_.refs_3_, ...), custom_call_target="tpu_custom_call", output_to_operand_aliasing={{}: (8, {})} | custom-call | flops 1 | bytes 1 | tf_op jit(solution)/shard_map/attn_bwd/pallas_call | solution.py:162
  317.7 16.3 %qkv_all.3 = (f32[512,768]{1,0:T(8,128)}, bf16[512,768]{1,0:T(8,128)(2,1)}, f32[8,3072]{1,0:T(8,128)}, bf16[16,88,768]{2,1,0:T(8,128)(2,1)}, bf16[16,88,768]{2,1,0:T(8,128)(2,1)}) custom-call(bf16[3,1024,768]{2,1,0:T(8,128)(2,1)} %attn_bwd.5.refs_0_, bf16[1024,768]{1,0:T(8,128)(2,1)} %get-tuple-element.122.refs_1_, bf16[2,768,2304]{2,1,0:T(8,128)(2,1)} %refs_2_.3, ...), custom_call_target="tpu_custom_call" | custom-call | flops 1 | bytes 1 | tf_op jit(solution)/shard_map/qkv_all/pallas_call | solution.py:821
  337.3 5.4 %stage2.2 = (bf16[4,144,768]{2,1,0:T(8,128)(2,1)}, bf16[4,144,768]{2,1,0:T(8,128)(2,1)}, bf16[4,144,768]{2,1,0:T(8,128)(2,1)}, bf16[4,144,768]{2,1,0:T(8,128)(2,1)}) custom-call(bf16[4,2,144,768]{3,2,1,0:T(8,128)(2,1)} %get-tuple-element.121.refs_9_.refs_0_, bf16[4,2,144,768]{3,2,1,0:T(8,128)(2,1)} %copy-done.4, ...), custom_call_target="tpu_custom_call" | custom-call | flops 10616832 | bytes 10616832 | tf_op jit(solution)/shard_map/stage2/pallas_call | solution.py:886
  344.1 2.9 collective-permute-done.6
  348.4 4.2 stage1.3
  353.9 11.6 %collective-permute-done.10.refs_3_ = bf16[4,144,768]{2,1,0:T(8,128)(2,1)S(1)} collective-permute-done((bf16[4,144,768]{2,1,0:T(8,128)(2,1)}, bf16[4,144,768]{2,1,0:T(8,128)(2,1)S(1)}, u32[]{:S(2)}, u32[]{:S(2)}) %collective-permute-start.10) | collective-permute-done | bytes 884768 | tf_op jit(solution)/shard_map/ppermute | solution.py:899
  367.2 3.6 stage3.2
  370.9 5.2 %collective-permute-done.8.refs_3_ = bf16[4,2,40,768]{3,2,1,0:T(8,128)(2,1)S(1)} collective-permute-done((bf16[4,2,40,768]{3,2,1,0:T(8,128)(2,1)}, bf16[4,2,40,768]{3,2,1,0:T(8,128)(2,1)S(1)}, u32[]{:S(2)}, u32[]{:S(2)}) %collective-permute-start.8) | collective-permute-done | bytes 491552 | tf_op jit(solution)/shard_map/ppermute | solution.py:1012
  378.4 3.6 stage2.3
  383.4 6.6 %collective-permute-done.12.rq = bf16[4,40,768]{2,1,0:T(8,128)(2,1)S(1)} collective-permute-done((bf16[4,40,768]{2,1,0:T(8,128)(2,1)}, bf16[4,40,768]{2,1,0:T(8,128)(2,1)S(1)}, u32[]{:S(2)}, u32[]{:S(2)}) %collective-permute-start.12) | collective-permute-done | bytes 245792 | tf_op jit(solution)/shard_map/ppermute | solution.py:899
  397.5 2.6 collective-permute-start.15
  401.0 11.0 %collective-permute-done.13 = bf16[512,768]{1,0:T(8,128)(2,1)S(1)} collective-permute-done((bf16[512,768]{1,0:T(8,128)(2,1)S(1)}, bf16[512,768]{1,0:T(8,128)(2,1)S(1)}, u32[]{:S(2)}, u32[]{:S(2)}) %collective-permute-start.13) | collective-permute-done | bytes 786464 | tf_op jit(solution)/shard_map/ppermute | solution.py:1012
  411.9 2.6 collective-permute-start.18
  414.7 3.9 collective-permute-start.19
  420.5 15.8 %collective-permute-done.15.refs_3_ = bf16[288,768]{1,0:T(8,128)(2,1)S(1)} collective-permute-done((bf16[288,768]{1,0:T(8,128)(2,1)S(1)}, bf16[288,768]{1,0:T(8,128)(2,1)S(1)}, u32[]{:S(2)}, u32[]{:S(2)}) %collective-permute-start.15) | collective-permute-done | bytes 442400 | tf_op jit(solution)/shard_map/ppermute | solution.py:899
  436.3 10.7 %collective-permute-done.18.refs_7_ = bf16[88,768]{1,0:T(8,128)(2,1)S(1)} collective-permute-done((bf16[88,768]{1,0:T(8,128)(2,1)S(1)}, bf16[88,768]{1,0:T(8,128)(2,1)S(1)}, u32[]{:S(2)}, u32[]{:S(2)}) %collective-permute-start.18) | collective-permute-done | bytes 135200 | tf_op jit(solution)/shard_map/ppermute | solution.py:899
  447.7 3.2 finish.1
  (115 shorter events, 35.5 us)
Async XLA Ops:
  7.2 439.8 %reduce-scatter.2.cloned.1.call-start = ((), (), s32[]{:S(2)}) async-start(), calls=%async_computation.1 | async-start | bytes 10948608 | tf_op jit(solution)/shard_map/reduce_scatter | solution.py:1214
  9.7 7.2 %copy-start.25 = (f32[2,768]{1,0:T(2,128)S(1)}, f32[2,768]{1,0:T(2,128)}, u32[]{:S(2)}) copy-start(f32[2,768]{1,0:T(2,128)} %param.27) | copy-start | bytes 18436
  9.8 21.4 %collective-permute-start = (bf16[512,768]{1,0:T(8,128)(2,1)S(1)}, bf16[512,768]{1,0:T(8,128)(2,1)S(1)}, u32[]{:S(2)}, u32[]{:S(2)}) collective-permute-start(bf16[512,768]{1,0:T(8,128)(2,1)S(1)} %get-tuple-element.170), channel_id=1, source_target_pairs={{0,1},{1,0},{2,3},{3,2},{4,5},{5,4},{6,7},{7,6},{8,9},{9,8},{10,11... | collective-permute-start | bytes 2359304 | tf_op jit(solution)/shard_map/ppermute | solution.py:1012
  13.8 119.8 %collective-permute-start.2 = (bf16[512,768]{1,0:T(8,128)(2,1)S(1)}, bf16[512,768]{1,0:T(8,128)(2,1)S(1)}, u32[]{:S(2)}, u32[]{:S(2)}) collective-permute-start(bf16[512,768]{1,0:T(8,128)(2,1)S(1)} %get-tuple-element.167), channel_id=1, source_target_pairs={{0,1},{1,0},{2,3},{3,2},{4,5},{5,4},{6,7},{7,6},{8,9},{9,8},{10,11... | collective-permute-start | bytes 2359304 | tf_op jit(solution)/shard_map/ppermute | solution.py:1012
  131.4 43.9 %collective-permute-start.1 = (bf16[512,768]{1,0:T(8,128)(2,1)}, bf16[512,768]{1,0:T(8,128)(2,1)S(1)}, u32[]{:S(2)}, u32[]{:S(2)}) collective-permute-start(bf16[512,768]{1,0:T(8,128)(2,1)} %get-tuple-element.98), channel_id=1, source_target_pairs={{0,1},{1,0},{2,3},{3,2},{4,5},{5,4},{6,7},{7,6},{8,9},{9,8},{10,11... | collective-permute-start | bytes 2359304 | tf_op jit(solution)/shard_map/ppermute | solution.py:1012
  269.3 13.7 %collective-permute-start.3 = (bf16[16,288,768]{2,1,0:T(8,128)(2,1)}, bf16[16,288,768]{2,1,0:T(8,128)(2,1)}, u32[]{:S(2)}, u32[]{:S(2)}) collective-permute-start(bf16[16,288,768]{2,1,0:T(8,128)(2,1)} %get-tuple-element.120), channel_id=1, source_target_pairs={{0,2},{2,0},{4,6},{6,4},{8,10},{10,8},{12,14},{14,12},{16,18},{18,... | collective-permute-start | bytes 21233672 | tf_op jit(solution)/shard_map/ppermute | solution.py:899
  291.3 43.6 %collective-permute-start.4 = (bf16[4,2,144,768]{3,2,1,0:T(8,128)(2,1)}, bf16[4,2,144,768]{3,2,1,0:T(8,128)(2,1)S(1)}, u32[]{:S(2)}, u32[]{:S(2)}) collective-permute-start(bf16[4,2,144,768]{3,2,1,0:T(8,128)(2,1)} %get-tuple-element.131), channel_id=1, source_target_pairs={{0,4},{2,6},{4,0},{6,2},{8,12},{10,14},{12,8},{14,10},{16,20},{18,... | collective-permute-start | bytes 5308424 | tf_op jit(solution)/shard_map/ppermute | solution.py:899
  292.8 43.3 %collective-permute-start.5 = (bf16[4,2,144,768]{3,2,1,0:T(8,128)(2,1)}, bf16[4,2,144,768]{3,2,1,0:T(8,128)(2,1)S(1)}, u32[]{:S(2)}, u32[]{:S(2)}) collective-permute-start(bf16[4,2,144,768]{3,2,1,0:T(8,128)(2,1)} %get-tuple-element.133), channel_id=1, source_target_pairs={{0,1},{1,0},{2,3},{3,2},{4,5},{5,4},{6,7},{7,6},{8,9},{9,8},{10,11... | collective-permute-start | bytes 5308424 | tf_op jit(solution)/shard_map/ppermute | solution.py:1012
  342.6 4.3 collective-permute-start.6
  342.7 22.7 %collective-permute-start.10 = (bf16[4,144,768]{2,1,0:T(8,128)(2,1)}, bf16[4,144,768]{2,1,0:T(8,128)(2,1)S(1)}, u32[]{:S(2)}, u32[]{:S(2)}) collective-permute-start(bf16[4,144,768]{2,1,0:T(8,128)(2,1)} %get-tuple-element.142), channel_id=1, source_target_pairs={{0,4},{2,6},{4,0},{6,2},{8,12},{10,14},{12,8},{14,10},{16,20},{18,... | collective-permute-start | bytes 2654216 | tf_op jit(solution)/shard_map/ppermute | solution.py:899
  343.6 22.7 %collective-permute-start.9 = (bf16[4,144,768]{2,1,0:T(8,128)(2,1)}, bf16[4,144,768]{2,1,0:T(8,128)(2,1)S(1)}, u32[]{:S(2)}, u32[]{:S(2)}) collective-permute-start(bf16[4,144,768]{2,1,0:T(8,128)(2,1)} %get-tuple-element.140), channel_id=1, source_target_pairs={{0,1},{1,0},{2,3},{3,2},{4,5},{5,4},{6,7},{7,6},{8,9},{9,8},{10,11... | collective-permute-start | bytes 2654216 | tf_op jit(solution)/shard_map/ppermute | solution.py:1012
  352.6 25.0 %collective-permute-start.7 = (bf16[4,2,48,768]{3,2,1,0:T(8,128)(2,1)}, bf16[4,2,48,768]{3,2,1,0:T(8,128)(2,1)S(1)}, u32[]{:S(2)}, u32[]{:S(2)}) collective-permute-start(bf16[4,2,48,768]{3,2,1,0:T(8,128)(2,1)} %get-tuple-element.137), channel_id=1, source_target_pairs={{0,4},{2,6},{4,0},{6,2},{8,12},{10,14},{12,8},{14,10},{16,20},{18,... | collective-permute-start | bytes 1769480 | tf_op jit(solution)/shard_map/ppermute | solution.py:899
  353.4 22.6 %collective-permute-start.8 = (bf16[4,2,40,768]{3,2,1,0:T(8,128)(2,1)}, bf16[4,2,40,768]{3,2,1,0:T(8,128)(2,1)S(1)}, u32[]{:S(2)}, u32[]{:S(2)}) collective-permute-start(bf16[4,2,40,768]{3,2,1,0:T(8,128)(2,1)} %get-tuple-element.139), channel_id=1, source_target_pairs={{0,1},{1,0},{2,3},{3,2},{4,5},{5,4},{6,7},{7,6},{8,9},{9,8},{10,11... | collective-permute-start | bytes 1474568 | tf_op jit(solution)/shard_map/ppermute | solution.py:1012
  370.9 22.8 %copy-start.11 = (bf16[512,768]{1,0:T(8,128)(2,1)S(1)}, bf16[512,768]{1,0:T(8,128)(2,1)}, u32[]{:S(2)}) copy-start(bf16[512,768]{1,0:T(8,128)(2,1)} %get-tuple-element.149.refs_4_) | copy-start | bytes 2359300
  370.9 25.2 %copy-start.2 = (bf16[512,768]{1,0:T(8,128)(2,1)S(1)}, bf16[512,768]{1,0:T(8,128)(2,1)}, u32[]{:S(2)}) copy-start(bf16[512,768]{1,0:T(8,128)(2,1)} %copy-done.1) | copy-start | bytes 2359300
  370.9 25.2 %copy-start.10 = (bf16[512,768]{1,0:T(8,128)(2,1)S(1)}, bf16[512,768]{1,0:T(8,128)(2,1)}, u32[]{:S(2)}) copy-start(bf16[512,768]{1,0:T(8,128)(2,1)} %get-tuple-element.97) | copy-start | bytes 2359300
  382.0 8.8 %collective-permute-start.11 = (bf16[4,48,768]{2,1,0:T(8,128)(2,1)}, bf16[4,48,768]{2,1,0:T(8,128)(2,1)S(1)}, u32[]{:S(2)}, u32[]{:S(2)}) collective-permute-start(bf16[4,48,768]{2,1,0:T(8,128)(2,1)} %get-tuple-element.145), channel_id=1, source_target_pairs={{0,1},{1,0},{2,3},{3,2},{4,5},{5,4},{6,7},{7,6},{8,9},{9,8},{10,11... | collective-permute-start | bytes 884744 | tf_op jit(solution)/shard_map/ppermute | solution.py:1012
  382.5 7.5 %collective-permute-start.12 = (bf16[4,40,768]{2,1,0:T(8,128)(2,1)}, bf16[4,40,768]{2,1,0:T(8,128)(2,1)S(1)}, u32[]{:S(2)}, u32[]{:S(2)}) collective-permute-start(bf16[4,40,768]{2,1,0:T(8,128)(2,1)} %get-tuple-element.147), channel_id=1, source_target_pairs={{0,4},{2,6},{4,0},{6,2},{8,12},{10,14},{12,8},{14,10},{16,20},{18,... | collective-permute-start | bytes 737288 | tf_op jit(solution)/shard_map/ppermute | solution.py:899
  393.7 6.6 %copy-start.34 = (bf16[88,768]{1,0:T(8,128)(2,1)S(1)}, bf16[88,768]{1,0:T(8,128)(2,1)}, u32[]{:S(2)}) copy-start(bf16[88,768]{1,0:T(8,128)(2,1)} %get-tuple-element.153) | copy-start | bytes 405508
  393.7 18.3 %copy-start.33 = (bf16[88,768]{1,0:T(8,128)(2,1)S(1)}, bf16[88,768]{1,0:T(8,128)(2,1)}, u32[]{:S(2)}) copy-start(bf16[88,768]{1,0:T(8,128)(2,1)} %get-tuple-element.154) | copy-start | bytes 405508
  393.7 18.3 %collective-permute-start.13 = (bf16[512,768]{1,0:T(8,128)(2,1)S(1)}, bf16[512,768]{1,0:T(8,128)(2,1)S(1)}, u32[]{:S(2)}, u32[]{:S(2)}) collective-permute-start(bf16[512,768]{1,0:T(8,128)(2,1)S(1)} %copy-done.11), channel_id=1, source_target_pairs={{0,1},{1,0},{2,3},{3,2},{4,5},{5,4},{6,7},{7,6},{8,9},{9,8},{10,11... | collective-permute-start | bytes 2359304 | tf_op jit(solution)/shard_map/ppermute | solution.py:1012
  394.5 20.2 %collective-permute-start.14 = (bf16[288,768]{1,0:T(8,128)(2,1)}, bf16[288,768]{1,0:T(8,128)(2,1)}, u32[]{:S(2)}, u32[]{:S(2)}) collective-permute-start(bf16[288,768]{1,0:T(8,128)(2,1)} %get-tuple-element.150), channel_id=1, source_target_pairs={{0,8},{2,10},{4,12},{6,14},{8,0},{10,2},{12,4},{14,6},{16,24},{18,... | collective-permute-start | bytes 1327112 | tf_op jit(solution)/shard_map/ppermute | solution.py:899
  396.1 18.6 %copy-start.32 = (bf16[88,768]{1,0:T(8,128)(2,1)S(1)}, bf16[88,768]{1,0:T(8,128)(2,1)}, u32[]{:S(2)}) copy-start(bf16[88,768]{1,0:T(8,128)(2,1)} %get-tuple-element.155) | copy-start | bytes 405508
  396.1 22.5 %copy-start.7 = (f32[512,768]{1,0:T(8,128)S(1)}, f32[512,768]{1,0:T(8,128)}, u32[]{:S(2)}) copy-start(f32[512,768]{1,0:T(8,128)} %get-tuple-element.127) | copy-start | bytes 4718596
  397.5 38.8 %collective-permute-start.15 = (bf16[288,768]{1,0:T(8,128)(2,1)S(1)}, bf16[288,768]{1,0:T(8,128)(2,1)S(1)}, u32[]{:S(2)}, u32[]{:S(2)}) collective-permute-start(bf16[288,768]{1,0:T(8,128)(2,1)S(1)} %copy-done.31), channel_id=1, source_target_pairs={{0,16},{2,18},{4,20},{6,22},{8,24},{10,26},{12,28},{14,30},{16,0},... | collective-permute-start | bytes 1327112 | tf_op jit(solution)/shard_map/ppermute | solution.py:899
  400.1 36.1 %collective-permute-start.16 = (bf16[288,768]{1,0:T(8,128)(2,1)S(1)}, bf16[288,768]{1,0:T(8,128)(2,1)S(1)}, u32[]{:S(2)}, u32[]{:S(2)}) collective-permute-start(bf16[288,768]{1,0:T(8,128)(2,1)S(1)} %copy-done.30), channel_id=1, source_target_pairs={{0,24},{2,26},{4,28},{6,30},{8,16},{10,18},{12,20},{14,22},{16,8},... | collective-permute-start | bytes 1327112 | tf_op jit(solution)/shard_map/ppermute | solution.py:899
  400.3 35.9 %collective-permute-start.17 = (bf16[88,768]{1,0:T(8,128)(2,1)S(1)}, bf16[88,768]{1,0:T(8,128)(2,1)S(1)}, u32[]{:S(2)}, u32[]{:S(2)}) collective-permute-start(bf16[88,768]{1,0:T(8,128)(2,1)S(1)} %copy-done.34), channel_id=1, source_target_pairs={{0,8},{2,10},{4,12},{6,14},{8,0},{10,2},{12,4},{14,6},{16,24},{18,... | collective-permute-start | bytes 405512 | tf_op jit(solution)/shard_map/ppermute | solution.py:899
  411.9 35.0 %collective-permute-start.18 = (bf16[88,768]{1,0:T(8,128)(2,1)S(1)}, bf16[88,768]{1,0:T(8,128)(2,1)S(1)}, u32[]{:S(2)}, u32[]{:S(2)}) collective-permute-start(bf16[88,768]{1,0:T(8,128)(2,1)S(1)} %copy-done.33), channel_id=1, source_target_pairs={{0,16},{2,18},{4,20},{6,22},{8,24},{10,26},{12,28},{14,30},{16,0},... | collective-permute-start | bytes 405512 | tf_op jit(solution)/shard_map/ppermute | solution.py:899
  414.7 32.3 %collective-permute-start.19 = (bf16[88,768]{1,0:T(8,128)(2,1)S(1)}, bf16[88,768]{1,0:T(8,128)(2,1)S(1)}, u32[]{:S(2)}, u32[]{:S(2)}) collective-permute-start(bf16[88,768]{1,0:T(8,128)(2,1)S(1)} %copy-done.32), channel_id=1, source_target_pairs={{0,24},{2,26},{4,28},{6,30},{8,16},{10,18},{12,20},{14,22},{16,8},... | collective-permute-start | bytes 405512 | tf_op jit(solution)/shard_map/ppermute | solution.py:899
  436.2 10.8 %copy-start.14 = (bf16[288,768]{1,0:T(8,128)(2,1)}, bf16[288,768]{1,0:T(8,128)(2,1)S(1)}, u32[]{:S(2)}) copy-start(bf16[288,768]{1,0:T(8,128)(2,1)S(1)} %collective-permute-done.15.refs_3_) | copy-start | bytes 1327108
  436.2 10.8 %copy-start.15 = (bf16[288,768]{1,0:T(8,128)(2,1)}, bf16[288,768]{1,0:T(8,128)(2,1)S(1)}, u32[]{:S(2)}) copy-start(bf16[288,768]{1,0:T(8,128)(2,1)S(1)} %collective-permute-done.16.refs_4_) | copy-start | bytes 1327108
  436.3 10.8 %copy-start.18 = (bf16[88,768]{1,0:T(8,128)(2,1)}, bf16[88,768]{1,0:T(8,128)(2,1)S(1)}, u32[]{:S(2)}) copy-start(bf16[88,768]{1,0:T(8,128)(2,1)S(1)} %collective-permute-done.17.refs_6_) | copy-start | bytes 405508
  (24 other events, 65.3 us)
Sparse Core Ops, SparseCore 0:
  175.4 144.0 reduce-scatter.1

commit v4 on v3

--- a/solution.py
+++ b/solution.py
@@ -179,6 +179,7 @@
 
 
 VMEM = pltpu.CompilerParams(vmem_limit_bytes=58 << 20, dimension_semantics=("arbitrary",))
+SMALL = pltpu.CompilerParams(vmem_limit_bytes=20 << 20)
 
 
 def ordered(kernel, n_in, deps):
@@ -263,7 +264,7 @@
         out_specs=[tile(block, width, at), tile(block, 3 * width, at)],
         out_shape=[sds(tokens, width, BF), sds(tokens, 3 * width, BF)],
         input_output_aliases=alias,
-        compiler_params=VMEM,
+        compiler_params=SMALL,
         cost_estimate=cost(6 * rows * width * width, rows * width * 10 + 6 * width * width),
         name="enter",
     )(*ops)
@@ -889,7 +890,7 @@
         in_specs=[spec(a.shape) for a in ops] + anywhere(deps),
         out_specs=[spec(s) for s in outs],
         out_shape=[jax.ShapeDtypeStruct(s, BF) for s in outs],
-        compiler_params=VMEM,
+        compiler_params=SMALL,
         cost_estimate=cost(nbytes, nbytes),
         name=name,
     )(*ops, *deps)
@@ -932,7 +933,7 @@
             in_specs=[pl.BlockSpec(a.shape, lambda i: (0, 0, 0)) for a in ops] + anywhere(deps),
             out_specs=[pl.BlockSpec((total, width), lambda i: (0, 0))] * 4,
             out_shape=[sds(total, width, F32)] + [sds(total, width, BF)] * 3,
-            compiler_params=VMEM,
+            compiler_params=SMALL,
             cost_estimate=cost(nbytes, nbytes),
             name="stage3",
         )(*ops, *deps)
@@ -1000,7 +1001,7 @@
             pl.pallas_call(
                 functools.partial(final_kernel, layout, [len(g) for g in groups]),
                 out_shape=[jax.ShapeDtypeStruct(shapes[n], F32) for n in names],
-                compiler_params=pltpu.CompilerParams(vmem_limit_bytes=58 << 20),
+                compiler_params=SMALL,
                 cost_estimate=cost(total, total),
                 name="finish",
             )(*ops),
@@ -1226,9 +1227,9 @@
     at0 = Group(bufs[0], after(bufs[1], dep), 48, dp)
     dep = at0.stage1(deps=dep)
     dep = ff0.stage3(deps=dep)
-    dep = at0.stage2(deps=dep)
-    dep = at0.stage3()
     back = swap_halves(after(theirs, dep))
+    at0.stage2(deps=dep + ff0.pieces[1:3] + [back])
+    at0.stage3(deps=ff0.pieces[3:])
     layout = {
         "rows": [
             {"down": (1, 0, 4 * t), "up": (1, 4 * t, 4 * t), "out": (1, 8 * t, t), "qkv": (2, 0, 3 * t)},

time: 463 us -> 439 us (0.948)
  Pallas kernels: 324 us -> 303 us
  waiting for transfers between devices: 77 us -> 61.8 us
  local copies, waits for them, and re-layouts: 15.6 us -> 22.5 us
    ppermute x12, waiting for transfers between devices: 50.1 us -> 32.3 us  [xor_permute(): return lax.ppermute(x, 'dp', [(i, i ^ mask) for i in range(dp)])]
    unnamed x70 -> x78, local copies, waits for them, and re-layouts: 8.49 us -> 18.1 us
    pallas_call x4, Pallas kernels: 21.5 us -> 12.9 us  [stage_call(): pl.pallas_call(ordered(kernel, len(ops), deps), grid=(ops[0].shape[0],),...]
    pallas_call x2, Pallas kernels: 11.6 us -> 5.33 us  [enter(): pl.pallas_call(enter_kernel, grid=(rows // block,), in_specs=specs, out_s...]
  transfers between devices with their start and end apart: 21 -> 21, of which waited for: 13 -> 10; matrix products, arithmetic and copies ran while one was open for 2% -> 1% of each run, Pallas kernels for 70% -> 70%
where the time goes in v4:
time: 439 us; the launch traced here: 433 us
  Pallas kernels  303 us (69%)
  waiting for transfers between devices  61.8 us (14%)
  starting transfers between devices  28 us (6%)
  local copies, waits for them, and re-layouts  22.5 us (5%)
  between operations  14.8 us (3%)
    pallas_call x2, Pallas kernels, ff_all(): pl.pallas_call(functools.partial(ff_all_kernel, len(gxs), n_out, 0, d), g...  84.3 us
    pallas_call x3, Pallas kernels, attn_bwd(): pl.pallas_call(ordered(attn_bwd_kernel, len(ops), extra), grid_spec=pltpu...  73.5 us
    pallas_call x2, Pallas kernels, post(): pl.pallas_call(functools.partial(post_kernel, d, last, parts, len(xs)), g...  51.5 us
    pallas_call x2, Pallas kernels, attn_fwd(): pl.pallas_call(functools.partial(attn_fwd_kernel, tokens // 2, 2), grid_s...  42.1 us
    ppermute x12, waiting for transfers between devices, xor_permute(): return lax.ppermute(x, 'dp', [(i, i ^ mask) for i in range(dp)])  32.3 us
    pallas_call x2, Pallas kernels, qkv_all(): pl.pallas_call(functools.partial(qkv_all_kernel, d, len(xs), row0), grid=...  30.8 us
    ppermute x8, waiting for transfers between devices, swap_halves(): return lax.ppermute(x, 'blk', [(0, 1), (1, 0)])  29.4 us
    ppermute x12, starting transfers between devices, xor_permute(): return lax.ppermute(x, 'dp', [(i, i ^ mask) for i in range(dp)])  18.4 us
  transfers between devices with their start and end apart: 21, of which 10 were waited for; matrix products, arithmetic and copies ran while one was open for 1% of the time, Pallas kernels for 70%

profile of v4, /device:TPU:0, one launch (start us, length us, event | category | flops | bytes accessed | tf_op | source)
XLA Modules:
  0.0 433.5 jit_solution(4990762616855808345)
XLA Ops:
  8.9 3.0 collective-permute-start
  15.0 3.0 copy-done.1
  18.0 2.7 enter.2
  20.7 9.6 %collective-permute-done.x_ref.refs_2_.refs_6_ = bf16[512,768]{1,0:T(8,128)(2,1)S(1)} collective-permute-done((bf16[512,768]{1,0:T(8,128)(2,1)S(1)}, bf16[512,768]{1,0:T(8,128)(2,1)S(1)}, u32[]{:S(2)}, u32[]{:S(2)}) %collective-permute-start) | collective-permute-done | bytes 786464 | tf_op jit(solution)/shard_map/ppermute | solution.py:1013
  30.3 2.7 enter.3
  33.1 2.1 copy-done
  35.2 20.8 %attn_fwd.2 = (bf16[1024,768]{1,0:T(8,128)(2,1)}, bf16[1024,768]{1,0:T(8,128)(2,1)}, f32[6,8,1024]{2,1,0:T(8,128)}) custom-call(s32[2]{0:T(128)} %refs_0_.5, bf16[1024,2304]{1,0:T(8,128)(2,1)} %copy-done, bf16[1024,2304]{1,0:T(8,128)(2,1)} %copy-done, bf16[1024,2304]{1,0:T(8,128)(2,1)} %copy-done), custom_call_target="tpu_custom_call" | custom-call | flops 9663676416 | bytes 6291456 | tf_op jit(solution)/shard_map/attn_fwd/pallas_call | solution.py:95
  56.0 29.0 %post.2 = (f32[1024,768]{1,0:T(8,128)}, bf16[1024,768]{1,0:T(8,128)(2,1)}, bf16[1024,3072]{1,0:T(8,128)(2,1)}, bf16[1024,3072]{1,0:T(8,128)(2,1)}, f32[1024,768]...) custom-call(bf16[1024,768]{1,0:T(8,128)(2,1)} %get-tuple-element.93.refs_0_.refs_9_.refs_4_, ...), custom_call_target="tpu_custom_call" | custom-call | flops 14495514624 | bytes 31457280 | tf_op jit(solution)/shard_map/post/pallas_call | solution.py:384
  85.0 21.2 %attn_fwd.3 = (bf16[1024,768]{1,0:T(8,128)(2,1)}, bf16[1024,768]{1,0:T(8,128)(2,1)}, f32[6,8,1024]{2,1,0:T(8,128)}) custom-call(s32[2]{0:T(128)} %refs_0_.5, bf16[1024,2304]{1,0:T(8,128)(2,1)} %get-tuple-element.94.q_ref.k_ref.v_ref.refs_1_.refs_2_.refs_3_, bf16[1024,2304]{1,0:T(8,128)(2,1)} %get-tuple-element.94.q_ref.k_ref.v_ref.refs_1_.refs_2_.refs_3_, ...), custom_call_target="tpu_custom_call" | custom-call | flops 9663676416 | bytes 6291456 | tf_op jit(solution)/shard_map/attn_fwd/pallas_call | solution.py:95
  106.2 22.6 %post.3 = (f32[1024,768]{1,0:T(8,128)}, bf16[1024,768]{1,0:T(8,128)(2,1)}, bf16[1024,3072]{1,0:T(8,128)(2,1)}, bf16[1024,3072]{1,0:T(8,128)(2,1)}, bf16[512,768]{1,0:T(8,128)(2,1)}, /*index=5*/bf16[512,768]{1,0:T(8,128)(2,1)}) custom-call(bf16[1024,768]{1,0:T(8,128)(2,1)} %get-tuple-element.95.refs_0_.refs_10_.refs_4_, ...), custom_call_target="tpu_custom_call" | custom-call | flops 10871635968 | bytes 31457280 | tf_op jit(solution)/shard_map/post/pallas_call | solution.py:384
  128.8 2.1 collective-permute-start.1
  131.8 40.8 %ff_all.2 = (f32[1024,768]{1,0:T(8,128)}, bf16[1024,768]{1,0:T(8,128)(2,1)}, f32[8,3072]{1,0:T(8,128)}, bf16[32,216,768]{2,1,0:T(8,128)(2,1)}) custom-call(bf16[512,768]{1,0:T(8,128)(2,1)} %get-tuple-element.168.refs_0_, bf16[512,768]{1,0:T(8,128)(2,1)} %copy-done.36, bf16[1024,3072]{1,0:T(8,128)(2,1)} %get-tuple-element.101.refs_2_, ...), custom_call_target="tpu_custom_call" | custom-call | flops 21743271936 | bytes 52428800 | tf_op jit(solution)/shard_map/ff_all/pallas_call | solution.py:683
  173.5 35.0 %attn_bwd.3.refs_0_ = bf16[3,1024,768]{2,1,0:T(8,128)(2,1)} custom-call(s32[2]{0:T(128)} %refs_0_.5, bf16[1024,2304]{1,0:T(8,128)(2,1)} %get-tuple-element.94.q_ref.k_ref.v_ref.refs_1_.refs_2_.refs_3_, bf16[1024,2304]{1,0:T(8,128)(2,1)} %get-tuple-element.94.q_ref.k_ref.v_ref.refs_1_.refs_2_.refs_3_, ...), custom_call_target="tpu_custom_call" | custom-call | flops 1 | bytes 1 | tf_op jit(solution)/shard_map/attn_bwd/pallas_call | solution.py:162
  208.5 14.5 %qkv_all.2 = (f32[1024,768]{1,0:T(8,128)}, f32[8,3072]{1,0:T(8,128)}, bf16[16,288,768]{2,1,0:T(8,128)(2,1)}, bf16[16,288,768]{2,1,0:T(8,128)(2,1)}) custom-call(bf16[3,1024,768]{2,1,0:T(8,128)(2,1)} %attn_bwd.3.refs_0_, bf16[1024,768]{1,0:T(8,128)(2,1)} %get-tuple-element.108.refs_1_, bf16[2,768,2304]{2,1,0:T(8,128)(2,1)} %refs_2_.3, ...), custom_call_target="tpu_custom_call" | custom-call | flops 1 | bytes 1 | tf_op jit(solution)/shard_map/qkv_all/pallas_call | solution.py:822
  222.9 43.6 %ff_all.3 = (f32[1024,768]{1,0:T(8,128)}, bf16[1024,768]{1,0:T(8,128)(2,1)}, f32[8,3072]{1,0:T(8,128)}, bf16[16,288,768]{2,1,0:T(8,128)(2,1)}, bf16[16,288,768]{2,1,0:T(8,128)(2,1)}) custom-call(f32[1024,768]{1,0:T(8,128)} %get-tuple-element.110.refs_0_, ...), custom_call_target="tpu_custom_call", output_to_operand_aliasing={{3}: (10, {}), {4}: (11, {})} | custom-call | flops 21743271936 | bytes 52428800 | tf_op jit(solution)/shard_map/ff_all/pallas_call | solution.py:683
  266.6 14.1 %attn_bwd.4.refs_2_.refs_8_ = bf16[3,1024,768]{2,1,0:T(8,128)(2,1)} custom-call(s32[2]{0:T(128)} %refs_0_.5, bf16[1024,2304]{1,0:T(8,128)(2,1)} %copy-done, bf16[1024,2304]{1,0:T(8,128)(2,1)} %copy-done, bf16[1024,2304]{1,0:T(8,128)(2,1)} %copy-done, bf16[1024,768]{1,0:T(8,128)(2,1)} %get-tuple-element.93.refs_0_.refs_9_.refs_4_, ...), custom_call_target="tpu_custom_call" | custom-call | flops 1 | bytes 1 | tf_op jit(solution)/shard_map/attn_bwd/pallas_call | solution.py:162
  280.8 2.3 copy-done.3
  283.1 5.8 %stage1.2 = (bf16[4,2,144,768]{3,2,1,0:T(8,128)(2,1)S(1)}, bf16[4,2,144,768]{3,2,1,0:T(8,128)(2,1)}, bf16[4,2,144,768]{3,2,1,0:T(8,128)(2,1)S(1)}, bf16[4,2,144,768]{3,2,1,0:T(8,128)(2,1)}) custom-call(bf16[4,2,2,288,768]{4,3,2,1,0:T(8,128)(2,1)S(1)} %bitcast.25, bf16[4,2,2,288,768]{4,3,2,1,0:T(8,128)(2,1)} %bitcast.7.refs_1_, ...), custom_call_target="tpu_custom_call" | custom-call | flops 21233664 | bytes 21233664 | tf_op jit(solution)/shard_map/stage1/pallas_call | solution.py:887
  293.3 24.4 %attn_bwd.5.refs_0_ = bf16[3,1024,768]{2,1,0:T(8,128)(2,1)} custom-call(s32[2]{0:T(128)} %refs_0_.5, bf16[1024,2304]{1,0:T(8,128)(2,1)} %copy-done, bf16[1024,2304]{1,0:T(8,128)(2,1)} %copy-done, bf16[1024,2304]{1,0:T(8,128)(2,1)} %copy-done, bf16[1024,768]{1,0:T(8,128)(2,1)} %get-tuple-element.93.refs_0_.refs_9_.refs_4_, ...), custom_call_target="tpu_custom_call", output_to_operand_aliasing={{}: (8, {})} | custom-call | flops 1 | bytes 1 | tf_op jit(solution)/shard_map/attn_bwd/pallas_call | solution.py:162
  317.8 16.3 %qkv_all.3 = (f32[512,768]{1,0:T(8,128)}, bf16[512,768]{1,0:T(8,128)(2,1)}, f32[8,3072]{1,0:T(8,128)}, bf16[16,88,768]{2,1,0:T(8,128)(2,1)}, bf16[16,88,768]{2,1,0:T(8,128)(2,1)}) custom-call(bf16[3,1024,768]{2,1,0:T(8,128)(2,1)} %attn_bwd.5.refs_0_, bf16[1024,768]{1,0:T(8,128)(2,1)} %copy-done.7, bf16[2,768,2304]{2,1,0:T(8,128)(2,1)} %refs_2_.3, ...), custom_call_target="tpu_custom_call" | custom-call | flops 1 | bytes 1 | tf_op jit(solution)/shard_map/qkv_all/pallas_call | solution.py:822
  337.9 3.0 stage2.2
  342.9 2.4 collective-permute-done.8
  346.9 16.2 %collective-permute-done.6.refs_1_ = bf16[4,144,768]{2,1,0:T(8,128)(2,1)S(1)} collective-permute-done((bf16[4,144,768]{2,1,0:T(8,128)(2,1)S(1)}, bf16[4,144,768]{2,1,0:T(8,128)(2,1)S(1)}, u32[]{:S(2)}, u32[]{:S(2)}) %collective-permute-start.6) | collective-permute-done | bytes 884768 | tf_op jit(solution)/shard_map/ppermute | solution.py:1013
  370.3 2.6 collective-permute-start.11
  372.9 16.1 %collective-permute-done.10.refs_5_.refs_2_ = bf16[288,768]{1,0:T(8,128)(2,1)S(1)} collective-permute-done((bf16[288,768]{1,0:T(8,128)(2,1)}, bf16[288,768]{1,0:T(8,128)(2,1)S(1)}, u32[]{:S(2)}, u32[]{:S(2)}) %collective-permute-start.10) | collective-permute-done | bytes 442400 | tf_op jit(solution)/shard_map/ppermute | solution.py:900
  389.0 2.5 collective-permute-start.12
  391.5 3.5 collective-permute-done.14.refs_3_
  396.1 2.4 stage2.3
  402.9 4.7 %collective-permute-done.16.refs_3_ = bf16[4,40,768]{2,1,0:T(8,128)(2,1)S(1)} collective-permute-done((bf16[4,40,768]{2,1,0:T(8,128)(2,1)S(1)}, bf16[4,40,768]{2,1,0:T(8,128)(2,1)S(1)}, u32[]{:S(2)}, u32[]{:S(2)}) %collective-permute-start.16) | collective-permute-done | bytes 245792 | tf_op jit(solution)/shard_map/ppermute | solution.py:900
  408.4 3.3 collective-permute-start.17
  414.2 1.9 maximum_select_fusion
  416.1 8.0 %collective-permute-done.18.refs_7_ = bf16[88,768]{1,0:T(8,128)(2,1)S(1)} collective-permute-done((bf16[88,768]{1,0:T(8,128)(2,1)S(1)}, bf16[88,768]{1,0:T(8,128)(2,1)S(1)}, u32[]{:S(2)}, u32[]{:S(2)}) %collective-permute-start.18) | collective-permute-done | bytes 135200 | tf_op jit(solution)/shard_map/ppermute | solution.py:900
  (124 shorter events, 36.6 us)
Async XLA Ops:
  7.2 416.9 %reduce-scatter.2.cloned.1.call-start = ((), (), s32[]{:S(2)}) async-start(), calls=%async_computation.1 | async-start | bytes 10948608 | tf_op jit(solution)/shard_map/reduce_scatter | solution.py:1215
  8.9 21.4 %collective-permute-start = (bf16[512,768]{1,0:T(8,128)(2,1)S(1)}, bf16[512,768]{1,0:T(8,128)(2,1)S(1)}, u32[]{:S(2)}, u32[]{:S(2)}) collective-permute-start(bf16[512,768]{1,0:T(8,128)(2,1)S(1)} %get-tuple-element.170), channel_id=1, source_target_pairs={{0,1},{1,0},{2,3},{3,2},{4,5},{5,4},{6,7},{7,6},{8,9},{9,8},{10,11... | collective-permute-start | bytes 2359304 | tf_op jit(solution)/shard_map/ppermute | solution.py:1013
  12.9 117.9 %collective-permute-start.2 = (bf16[512,768]{1,0:T(8,128)(2,1)S(1)}, bf16[512,768]{1,0:T(8,128)(2,1)S(1)}, u32[]{:S(2)}, u32[]{:S(2)}) collective-permute-start(bf16[512,768]{1,0:T(8,128)(2,1)S(1)} %get-tuple-element.167), channel_id=1, source_target_pairs={{0,1},{1,0},{2,3},{3,2},{4,5},{5,4},{6,7},{7,6},{8,9},{9,8},{10,11... | collective-permute-start | bytes 2359304 | tf_op jit(solution)/shard_map/ppermute | solution.py:1013
  13.0 17.3 %copy-start.19 = (f32[2,2,1,768]{3,2,1,0:T(1,128)}, f32[2,2,1,768]{3,2,1,0:T(1,128)S(1)}, u32[]{:S(2)}) copy-start(f32[2,2,1,768]{3,2,1,0:T(1,128)S(1)} %broadcast_in_dim.21.gain_ref.refs_4_.refs_8_.refs_3_) | copy-start | bytes 36868
  13.1 17.3 %copy-start.21 = (f32[2,2,1,768]{3,2,1,0:T(1,128)}, f32[2,2,1,768]{3,2,1,0:T(1,128)S(1)}, u32[]{:S(2)}) copy-start(f32[2,2,1,768]{3,2,1,0:T(1,128)S(1)} %broadcast_in_dim.22.shift_ref.refs_5_.refs_9_.refs_4_) | copy-start | bytes 36868
  13.2 17.2 %copy-start.20 = (f32[2,1,2304]{2,1,0:T(1,128)}, f32[2,1,2304]{2,1,0:T(1,128)S(1)}, u32[]{:S(2)}) copy-start(f32[2,1,2304]{2,1,0:T(1,128)S(1)} %broadcast_in_dim.24.bias_ref.refs_10_) | copy-start | bytes 55300
  18.0 12.3 %copy-start.2 = (bf16[2,768,2304]{2,1,0:T(8,128)(2,1)S(1)}, bf16[2,768,2304]{2,1,0:T(8,128)(2,1)}, u32[]{:S(2)}) copy-start(bf16[2,768,2304]{2,1,0:T(8,128)(2,1)} %refs_2_.3) | copy-start | bytes 21233668
  35.2 20.8 %copy-start.7 = (bf16[1024,768]{1,0:T(8,128)(2,1)}, bf16[1024,768]{1,0:T(8,128)(2,1)S(1)}, u32[]{:S(2)}) copy-start(bf16[1024,768]{1,0:T(8,128)(2,1)S(1)} %get-tuple-element.122.refs_1_) | copy-start | bytes 4718596
  128.8 43.8 %collective-permute-start.1 = (bf16[512,768]{1,0:T(8,128)(2,1)}, bf16[512,768]{1,0:T(8,128)(2,1)S(1)}, u32[]{:S(2)}, u32[]{:S(2)}) collective-permute-start(bf16[512,768]{1,0:T(8,128)(2,1)} %get-tuple-element.98), channel_id=1, source_target_pairs={{0,1},{1,0},{2,3},{3,2},{4,5},{5,4},{6,7},{7,6},{8,9},{9,8},{10,11... | collective-permute-start | bytes 2359304 | tf_op jit(solution)/shard_map/ppermute | solution.py:1013
  266.5 14.2 %collective-permute-start.3 = (bf16[16,288,768]{2,1,0:T(8,128)(2,1)}, bf16[16,288,768]{2,1,0:T(8,128)(2,1)}, u32[]{:S(2)}, u32[]{:S(2)}) collective-permute-start(bf16[16,288,768]{2,1,0:T(8,128)(2,1)} %get-tuple-element.120), channel_id=1, source_target_pairs={{0,2},{2,0},{4,6},{6,4},{8,10},{10,8},{12,14},{14,12},{16,18},{18,... | collective-permute-start | bytes 21233672 | tf_op jit(solution)/shard_map/ppermute | solution.py:900
  266.6 14.2 %slice-start = ((s8[7077888]{0:T(1024)(128)(4,1)}), s8[4194304]{0:T(1024)(128)(4,1)S(1)}, s32[]{:S(2)}) async-start(s8[7077888]{0:T(1024)(128)(4,1)} %bitcast.23), calls=%async_computation.2 | async-start | bytes 8388608
  266.6 14.2 %slice-start.1 = ((s8[7077888]{0:T(1024)(128)(4,1)}), s8[2883584]{0:T(1024)(128)(4,1)S(1)}, s32[]{:S(2)}) async-start(s8[7077888]{0:T(1024)(128)(4,1)} %bitcast.23), calls=%async_computation.3 | async-start | bytes 5767168
  291.4 43.6 %collective-permute-start.4 = (bf16[4,2,144,768]{3,2,1,0:T(8,128)(2,1)}, bf16[4,2,144,768]{3,2,1,0:T(8,128)(2,1)S(1)}, u32[]{:S(2)}, u32[]{:S(2)}) collective-permute-start(bf16[4,2,144,768]{3,2,1,0:T(8,128)(2,1)} %get-tuple-element.129), channel_id=1, source_target_pairs={{0,4},{2,6},{4,0},{6,2},{8,12},{10,14},{12,8},{14,10},{16,20},{18,... | collective-permute-start | bytes 5308424 | tf_op jit(solution)/shard_map/ppermute | solution.py:900
  292.9 43.5 %collective-permute-start.5 = (bf16[4,2,144,768]{3,2,1,0:T(8,128)(2,1)}, bf16[4,2,144,768]{3,2,1,0:T(8,128)(2,1)}, u32[]{:S(2)}, u32[]{:S(2)}) collective-permute-start(bf16[4,2,144,768]{3,2,1,0:T(8,128)(2,1)} %get-tuple-element.131), channel_id=1, source_target_pairs={{0,1},{1,0},{2,3},{3,2},{4,5},{5,4},{6,7},{7,6},{8,9},{9,8},{10,11... | collective-permute-start | bytes 5308424 | tf_op jit(solution)/shard_map/ppermute | solution.py:1013
  317.7 18.7 %copy-start.6 = (bf16[4,2,144,768]{3,2,1,0:T(8,128)(2,1)S(1)}, bf16[4,2,144,768]{3,2,1,0:T(8,128)(2,1)}, u32[]{:S(2)}) copy-start(bf16[4,2,144,768]{3,2,1,0:T(8,128)(2,1)} %copy-done.5) | copy-start | bytes 5308420
  317.7 18.6 %copy-start.13 = (bf16[4,2,144,768]{3,2,1,0:T(8,128)(2,1)S(1)}, bf16[4,2,144,768]{3,2,1,0:T(8,128)(2,1)}, u32[]{:S(2)}) copy-start(bf16[4,2,144,768]{3,2,1,0:T(8,128)(2,1)} %copy-done.12) | copy-start | bytes 5308420
  340.9 4.3 collective-permute-start.8
  341.0 22.1 %collective-permute-start.6 = (bf16[4,144,768]{2,1,0:T(8,128)(2,1)S(1)}, bf16[4,144,768]{2,1,0:T(8,128)(2,1)S(1)}, u32[]{:S(2)}, u32[]{:S(2)}) collective-permute-start(bf16[4,144,768]{2,1,0:T(8,128)(2,1)S(1)} %get-tuple-element.133), channel_id=1, source_target_pairs={{0,1},{1,0},{2,3},{3,2},{4,5},{5,4},{6,7},{7,6},{8,9},{9,8},{10,11... | collective-permute-start | bytes 2654216 | tf_op jit(solution)/shard_map/ppermute | solution.py:1013
  341.6 21.7 %collective-permute-start.7 = (bf16[4,144,768]{2,1,0:T(8,128)(2,1)S(1)}, bf16[4,144,768]{2,1,0:T(8,128)(2,1)S(1)}, u32[]{:S(2)}, u32[]{:S(2)}) collective-permute-start(bf16[4,144,768]{2,1,0:T(8,128)(2,1)S(1)} %get-tuple-element.135), channel_id=1, source_target_pairs={{0,4},{2,6},{4,0},{6,2},{8,12},{10,14},{12,8},{14,10},{16,20},{18,... | collective-permute-start | bytes 2654216 | tf_op jit(solution)/shard_map/ppermute | solution.py:900
  346.9 23.4 %copy-start.16 = (bf16[4,2,40,768]{3,2,1,0:T(8,128)(2,1)}, bf16[4,2,40,768]{3,2,1,0:T(8,128)(2,1)S(1)}, u32[]{:S(2)}) copy-start(bf16[4,2,40,768]{3,2,1,0:T(8,128)(2,1)S(1)} %get-tuple-element.146.refs_2_) | copy-start | bytes 1474564
  365.3 29.7 %collective-permute-start.9 = (bf16[512,768]{1,0:T(8,128)(2,1)}, bf16[512,768]{1,0:T(8,128)(2,1)S(1)}, u32[]{:S(2)}, u32[]{:S(2)}) collective-permute-start(bf16[512,768]{1,0:T(8,128)(2,1)} %get-tuple-element.141.refs_4_), channel_id=1, source_target_pairs={{0,1},{1,0},{2,3},{3,2},{4,5},{5,4},{6,7},{7,6},{8,9},{9,8},{10,11... | collective-permute-start | bytes 2359304 | tf_op jit(solution)/shard_map/ppermute | solution.py:1013
  366.8 28.2 %collective-permute-start.13 = (bf16[4,2,48,768]{3,2,1,0:T(8,128)(2,1)}, bf16[4,2,48,768]{3,2,1,0:T(8,128)(2,1)}, u32[]{:S(2)}, u32[]{:S(2)}) collective-permute-start(bf16[4,2,48,768]{3,2,1,0:T(8,128)(2,1)} %get-tuple-element.145), channel_id=1, source_target_pairs={{0,4},{2,6},{4,0},{6,2},{8,12},{10,14},{12,8},{14,10},{16,20},{18,... | collective-permute-start | bytes 1769480 | tf_op jit(solution)/shard_map/ppermute | solution.py:900
  368.2 26.8 %collective-permute-start.14 = (bf16[4,2,40,768]{3,2,1,0:T(8,128)(2,1)}, bf16[4,2,40,768]{3,2,1,0:T(8,128)(2,1)}, u32[]{:S(2)}, u32[]{:S(2)}) collective-permute-start(bf16[4,2,40,768]{3,2,1,0:T(8,128)(2,1)} %get-tuple-element.147), channel_id=1, source_target_pairs={{0,1},{1,0},{2,3},{3,2},{4,5},{5,4},{6,7},{7,6},{8,9},{9,8},{10,11... | collective-permute-start | bytes 1474568 | tf_op jit(solution)/shard_map/ppermute | solution.py:1013
  368.6 20.3 %collective-permute-start.10 = (bf16[288,768]{1,0:T(8,128)(2,1)}, bf16[288,768]{1,0:T(8,128)(2,1)S(1)}, u32[]{:S(2)}, u32[]{:S(2)}) collective-permute-start(bf16[288,768]{1,0:T(8,128)(2,1)} %get-tuple-element.142), channel_id=1, source_target_pairs={{0,8},{2,10},{4,12},{6,14},{8,0},{10,2},{12,4},{14,6},{16,24},{18,... | collective-permute-start | bytes 1327112 | tf_op jit(solution)/shard_map/ppermute | solution.py:900
  370.3 21.2 %collective-permute-start.11 = (bf16[288,768]{1,0:T(8,128)(2,1)}, bf16[288,768]{1,0:T(8,128)(2,1)S(1)}, u32[]{:S(2)}, u32[]{:S(2)}) collective-permute-start(bf16[288,768]{1,0:T(8,128)(2,1)} %get-tuple-element.143), channel_id=1, source_target_pairs={{0,16},{2,18},{4,20},{6,22},{8,24},{10,26},{12,28},{14,30},{16,0},... | collective-permute-start | bytes 1327112 | tf_op jit(solution)/shard_map/ppermute | solution.py:900
  389.0 13.9 %collective-permute-start.12 = (bf16[288,768]{1,0:T(8,128)(2,1)}, bf16[288,768]{1,0:T(8,128)(2,1)S(1)}, u32[]{:S(2)}, u32[]{:S(2)}) collective-permute-start(bf16[288,768]{1,0:T(8,128)(2,1)} %copy-done.22), channel_id=1, source_target_pairs={{0,24},{2,26},{4,28},{6,30},{8,16},{10,18},{12,20},{14,22},{16,8},... | collective-permute-start | bytes 1327112 | tf_op jit(solution)/shard_map/ppermute | solution.py:900
  398.5 9.1 %collective-permute-start.15 = (bf16[4,48,768]{2,1,0:T(8,128)(2,1)S(1)}, bf16[4,48,768]{2,1,0:T(8,128)(2,1)S(1)}, u32[]{:S(2)}, u32[]{:S(2)}) collective-permute-start(bf16[4,48,768]{2,1,0:T(8,128)(2,1)S(1)} %get-tuple-element.149), channel_id=1, source_target_pairs={{0,1},{1,0},{2,3},{3,2},{4,5},{5,4},{6,7},{7,6},{8,9},{9,8},{10,11... | collective-permute-start | bytes 884744 | tf_op jit(solution)/shard_map/ppermute | solution.py:1013
  401.3 12.9 %copy-start.26 = (f32[512,768]{1,0:T(8,128)S(1)}, f32[512,768]{1,0:T(8,128)}, u32[]{:S(2)}) copy-start(f32[512,768]{1,0:T(8,128)} %get-tuple-element.127) | copy-start | bytes 4718596
  401.3 6.2 %collective-permute-start.16 = (bf16[4,40,768]{2,1,0:T(8,128)(2,1)S(1)}, bf16[4,40,768]{2,1,0:T(8,128)(2,1)S(1)}, u32[]{:S(2)}, u32[]{:S(2)}) collective-permute-start(bf16[4,40,768]{2,1,0:T(8,128)(2,1)S(1)} %get-tuple-element.151), channel_id=1, source_target_pairs={{0,4},{2,6},{4,0},{6,2},{8,12},{10,14},{12,8},{14,10},{16,20},{18,... | collective-permute-start | bytes 737288 | tf_op jit(solution)/shard_map/ppermute | solution.py:900
  408.4 7.7 %collective-permute-start.17 = (bf16[88,768]{1,0:T(8,128)(2,1)S(1)}, bf16[88,768]{1,0:T(8,128)(2,1)S(1)}, u32[]{:S(2)}, u32[]{:S(2)}) collective-permute-start(bf16[88,768]{1,0:T(8,128)(2,1)S(1)} %get-tuple-element.153), channel_id=1, source_target_pairs={{0,8},{2,10},{4,12},{6,14},{8,0},{10,2},{12,4},{14,6},{16,24},{18,... | collective-permute-start | bytes 405512 | tf_op jit(solution)/shard_map/ppermute | solution.py:900
  411.8 12.3 %collective-permute-start.18 = (bf16[88,768]{1,0:T(8,128)(2,1)S(1)}, bf16[88,768]{1,0:T(8,128)(2,1)S(1)}, u32[]{:S(2)}, u32[]{:S(2)}) collective-permute-start(bf16[88,768]{1,0:T(8,128)(2,1)S(1)} %get-tuple-element.154), channel_id=1, source_target_pairs={{0,16},{2,18},{4,20},{6,22},{8,24},{10,26},{12,28},{14,30},{16,0},... | collective-permute-start | bytes 405512 | tf_op jit(solution)/shard_map/ppermute | solution.py:900
  412.8 11.3 %collective-permute-start.19 = (bf16[88,768]{1,0:T(8,128)(2,1)S(1)}, bf16[88,768]{1,0:T(8,128)(2,1)S(1)}, u32[]{:S(2)}, u32[]{:S(2)}) collective-permute-start(bf16[88,768]{1,0:T(8,128)(2,1)S(1)} %get-tuple-element.155), channel_id=1, source_target_pairs={{0,24},{2,26},{4,28},{6,30},{8,16},{10,18},{12,20},{14,22},{16,8},... | collective-permute-start | bytes 405512 | tf_op jit(solution)/shard_map/ppermute | solution.py:900
  (28 other events, 96.9 us)
Sparse Core Ops, SparseCore 0:
  172.7 144.1 reduce-scatter.1

commit v5 on v4

--- a/solution.py
+++ b/solution.py
@@ -54,7 +54,8 @@
     zero = jnp.zeros_like(k)
     sel = [first, jnp.logical_not(first)]
     keys = [jnp.concatenate([jnp.where(sel[h], k, zero), kaug[...]], 1) for h in range(2)]
-    vals = [jnp.where(sel[h], v, zero).T for h in range(2)]
+    ones = jnp.ones((16, tokens), BF)
+    vals = [jnp.concatenate([jnp.where(sel[h], v, zero).T, ones], 0) for h in range(2)]
     qa = jnp.concatenate([q, qone[...]], 1)
     units = [(c, h) for c in range(tokens // chunk) for h in range(2)]
     ready = {}
@@ -75,8 +76,8 @@
         top = jnp.max(st, axis=0, keepdims=True)
         p = jnp.exp2(st - top)
         p = p.astype(BF)
-        total = jnp.sum(p.astype(F32), axis=0, keepdims=True)
-        kept[h] = (dot_nn(vals[h], p), top, total)
+        both = dot_nn(vals[h], p)
+        kept[h] = (both[:128], top, both[128:129])
         if h == 1:
             head = lax.broadcasted_iota(jnp.int32, (128, chunk), 0) < HEAD_DIM
             inv = jnp.where(head, 1.0 / kept[0][2], 1.0 / kept[1][2])
@@ -93,7 +94,7 @@
     pairs = width // 128
     spec = lambda off: pl.BlockSpec((tokens, 128), lambda i, m: (0, off + i))
     return pl.pallas_call(
-        functools.partial(attn_fwd_kernel, tokens // 2, 2),
+        functools.partial(attn_fwd_kernel, tokens // 2, 3),
         grid_spec=pltpu.PrefetchScalarGridSpec(
             num_scalar_prefetch=1,
             grid=(pairs,),

time: 439 us -> 436 us (level)
  transfers between devices with their start and end apart: 21 -> 21, of which waited for: 10 -> 10; matrix products, arithmetic and copies ran while one was open for 1% -> 1% of each run, Pallas kernels for 70% -> 69%
where the time goes in v5:
time: 436 us; the launch traced here: 431 us
  Pallas kernels  301 us (69%)
  waiting for transfers between devices  61.7 us (14%)
  starting transfers between devices  28.1 us (6%)
  local copies, waits for them, and re-layouts  22.5 us (5%)
  between operations  14.8 us (3%)
    pallas_call x2, Pallas kernels, ff_all(): pl.pallas_call(functools.partial(ff_all_kernel, len(gxs), n_out, 0, d), g...  84.3 us
    pallas_call x3, Pallas kernels, attn_bwd(): pl.pallas_call(ordered(attn_bwd_kernel, len(ops), extra), grid_spec=pltpu...  73.5 us
    pallas_call x2, Pallas kernels, post(): pl.pallas_call(functools.partial(post_kernel, d, last, parts, len(xs)), g...  51.5 us
    pallas_call x2, Pallas kernels, attn_fwd(): pl.pallas_call(functools.partial(attn_fwd_kernel, tokens // 2, 3), grid_s...  39.6 us
    ppermute x12, waiting for transfers between devices, xor_permute(): return lax.ppermute(x, 'dp', [(i, i ^ mask) for i in range(dp)])  32.3 us
    pallas_call x2, Pallas kernels, qkv_all(): pl.pallas_call(functools.partial(qkv_all_kernel, d, len(xs), row0), grid=...  30.8 us
    ppermute x8, waiting for transfers between devices, swap_halves(): return lax.ppermute(x, 'blk', [(0, 1), (1, 0)])  29.4 us
    ppermute x12, starting transfers between devices, xor_permute(): return lax.ppermute(x, 'dp', [(i, i ^ mask) for i in range(dp)])  18.4 us
  transfers between devices with their start and end apart: 21, of which 10 were waited for; matrix products, arithmetic and copies ran while one was open for 1% of the time, Pallas kernels for 69%

profile of v5, /device:TPU:0, one launch (start us, length us, event | category | flops | bytes accessed | tf_op | source)
XLA Modules:
  0.0 431.0 jit_solution(13420241868813855653)
XLA Ops:
  8.9 3.0 collective-permute-start
  15.0 3.0 copy-done.1
  18.0 2.7 enter.2
  20.7 9.6 %collective-permute-done.x_ref.refs_2_.refs_6_ = bf16[512,768]{1,0:T(8,128)(2,1)S(1)} collective-permute-done((bf16[512,768]{1,0:T(8,128)(2,1)S(1)}, bf16[512,768]{1,0:T(8,128)(2,1)S(1)}, u32[]{:S(2)}, u32[]{:S(2)}) %collective-permute-start) | collective-permute-done | bytes 786464 | tf_op jit(solution)/shard_map/ppermute | solution.py:1014
  30.3 2.7 enter.3
  33.1 2.1 copy-done
  35.2 19.6 %attn_fwd.2 = (bf16[1024,768]{1,0:T(8,128)(2,1)}, bf16[1024,768]{1,0:T(8,128)(2,1)}, f32[6,8,1024]{2,1,0:T(8,128)}) custom-call(s32[2]{0:T(128)} %refs_0_.5, bf16[1024,2304]{1,0:T(8,128)(2,1)} %copy-done, bf16[1024,2304]{1,0:T(8,128)(2,1)} %copy-done, bf16[1024,2304]{1,0:T(8,128)(2,1)} %copy-done), custom_call_target="tpu_custom_call" | custom-call | flops 9663676416 | bytes 6291456 | tf_op jit(solution)/shard_map/attn_fwd/pallas_call | solution.py:96
  54.8 29.0 %post.2 = (f32[1024,768]{1,0:T(8,128)}, bf16[1024,768]{1,0:T(8,128)(2,1)}, bf16[1024,3072]{1,0:T(8,128)(2,1)}, bf16[1024,3072]{1,0:T(8,128)(2,1)}, f32[1024,768]...) custom-call(bf16[1024,768]{1,0:T(8,128)(2,1)} %get-tuple-element.93.refs_0_.refs_9_.refs_4_, ...), custom_call_target="tpu_custom_call" | custom-call | flops 14495514624 | bytes 31457280 | tf_op jit(solution)/shard_map/post/pallas_call | solution.py:385
  83.7 20.0 %attn_fwd.3 = (bf16[1024,768]{1,0:T(8,128)(2,1)}, bf16[1024,768]{1,0:T(8,128)(2,1)}, f32[6,8,1024]{2,1,0:T(8,128)}) custom-call(s32[2]{0:T(128)} %refs_0_.5, bf16[1024,2304]{1,0:T(8,128)(2,1)} %get-tuple-element.94.q_ref.k_ref.v_ref.refs_1_.refs_2_.refs_3_, bf16[1024,2304]{1,0:T(8,128)(2,1)} %get-tuple-element.94.q_ref.k_ref.v_ref.refs_1_.refs_2_.refs_3_, ...), custom_call_target="tpu_custom_call" | custom-call | flops 9663676416 | bytes 6291456 | tf_op jit(solution)/shard_map/attn_fwd/pallas_call | solution.py:96
  103.7 22.6 %post.3 = (f32[1024,768]{1,0:T(8,128)}, bf16[1024,768]{1,0:T(8,128)(2,1)}, bf16[1024,3072]{1,0:T(8,128)(2,1)}, bf16[1024,3072]{1,0:T(8,128)(2,1)}, bf16[512,768]{1,0:T(8,128)(2,1)}, /*index=5*/bf16[512,768]{1,0:T(8,128)(2,1)}) custom-call(bf16[1024,768]{1,0:T(8,128)(2,1)} %get-tuple-element.95.refs_0_.refs_10_.refs_4_, ...), custom_call_target="tpu_custom_call" | custom-call | flops 10871635968 | bytes 31457280 | tf_op jit(solution)/shard_map/post/pallas_call | solution.py:385
  126.3 2.1 collective-permute-start.1
  129.3 40.8 %ff_all.2 = (f32[1024,768]{1,0:T(8,128)}, bf16[1024,768]{1,0:T(8,128)(2,1)}, f32[8,3072]{1,0:T(8,128)}, bf16[32,216,768]{2,1,0:T(8,128)(2,1)}) custom-call(bf16[512,768]{1,0:T(8,128)(2,1)} %get-tuple-element.168.refs_0_, bf16[512,768]{1,0:T(8,128)(2,1)} %copy-done.36, bf16[1024,3072]{1,0:T(8,128)(2,1)} %get-tuple-element.101.refs_2_, ...), custom_call_target="tpu_custom_call" | custom-call | flops 21743271936 | bytes 52428800 | tf_op jit(solution)/shard_map/ff_all/pallas_call | solution.py:684
  171.0 35.0 %attn_bwd.3.refs_0_ = bf16[3,1024,768]{2,1,0:T(8,128)(2,1)} custom-call(s32[2]{0:T(128)} %refs_0_.5, bf16[1024,2304]{1,0:T(8,128)(2,1)} %get-tuple-element.94.q_ref.k_ref.v_ref.refs_1_.refs_2_.refs_3_, bf16[1024,2304]{1,0:T(8,128)(2,1)} %get-tuple-element.94.q_ref.k_ref.v_ref.refs_1_.refs_2_.refs_3_, ...), custom_call_target="tpu_custom_call" | custom-call | flops 1 | bytes 1 | tf_op jit(solution)/shard_map/attn_bwd/pallas_call | solution.py:163
  206.0 14.5 %qkv_all.2 = (f32[1024,768]{1,0:T(8,128)}, f32[8,3072]{1,0:T(8,128)}, bf16[16,288,768]{2,1,0:T(8,128)(2,1)}, bf16[16,288,768]{2,1,0:T(8,128)(2,1)}) custom-call(bf16[3,1024,768]{2,1,0:T(8,128)(2,1)} %attn_bwd.3.refs_0_, bf16[1024,768]{1,0:T(8,128)(2,1)} %get-tuple-element.108.refs_1_, bf16[2,768,2304]{2,1,0:T(8,128)(2,1)} %refs_2_.3, ...), custom_call_target="tpu_custom_call" | custom-call | flops 1 | bytes 1 | tf_op jit(solution)/shard_map/qkv_all/pallas_call | solution.py:823
  220.5 43.6 %ff_all.3 = (f32[1024,768]{1,0:T(8,128)}, bf16[1024,768]{1,0:T(8,128)(2,1)}, f32[8,3072]{1,0:T(8,128)}, bf16[16,288,768]{2,1,0:T(8,128)(2,1)}, bf16[16,288,768]{2,1,0:T(8,128)(2,1)}) custom-call(f32[1024,768]{1,0:T(8,128)} %get-tuple-element.110.refs_0_, ...), custom_call_target="tpu_custom_call", output_to_operand_aliasing={{3}: (10, {}), {4}: (11, {})} | custom-call | flops 21743271936 | bytes 52428800 | tf_op jit(solution)/shard_map/ff_all/pallas_call | solution.py:684
  264.1 14.1 %attn_bwd.4.refs_2_.refs_8_ = bf16[3,1024,768]{2,1,0:T(8,128)(2,1)} custom-call(s32[2]{0:T(128)} %refs_0_.5, bf16[1024,2304]{1,0:T(8,128)(2,1)} %copy-done, bf16[1024,2304]{1,0:T(8,128)(2,1)} %copy-done, bf16[1024,2304]{1,0:T(8,128)(2,1)} %copy-done, bf16[1024,768]{1,0:T(8,128)(2,1)} %get-tuple-element.93.refs_0_.refs_9_.refs_4_, ...), custom_call_target="tpu_custom_call" | custom-call | flops 1 | bytes 1 | tf_op jit(solution)/shard_map/attn_bwd/pallas_call | solution.py:163
  278.3 2.3 copy-done.3
  280.6 5.8 %stage1.2 = (bf16[4,2,144,768]{3,2,1,0:T(8,128)(2,1)S(1)}, bf16[4,2,144,768]{3,2,1,0:T(8,128)(2,1)}, bf16[4,2,144,768]{3,2,1,0:T(8,128)(2,1)S(1)}, bf16[4,2,144,768]{3,2,1,0:T(8,128)(2,1)}) custom-call(bf16[4,2,2,288,768]{4,3,2,1,0:T(8,128)(2,1)S(1)} %bitcast.25, bf16[4,2,2,288,768]{4,3,2,1,0:T(8,128)(2,1)} %bitcast.7.refs_1_, ...), custom_call_target="tpu_custom_call" | custom-call | flops 21233664 | bytes 21233664 | tf_op jit(solution)/shard_map/stage1/pallas_call | solution.py:888
  290.9 24.4 %attn_bwd.5.refs_0_ = bf16[3,1024,768]{2,1,0:T(8,128)(2,1)} custom-call(s32[2]{0:T(128)} %refs_0_.5, bf16[1024,2304]{1,0:T(8,128)(2,1)} %copy-done, bf16[1024,2304]{1,0:T(8,128)(2,1)} %copy-done, bf16[1024,2304]{1,0:T(8,128)(2,1)} %copy-done, bf16[1024,768]{1,0:T(8,128)(2,1)} %get-tuple-element.93.refs_0_.refs_9_.refs_4_, ...), custom_call_target="tpu_custom_call", output_to_operand_aliasing={{}: (8, {})} | custom-call | flops 1 | bytes 1 | tf_op jit(solution)/shard_map/attn_bwd/pallas_call | solution.py:163
  315.3 16.3 %qkv_all.3 = (f32[512,768]{1,0:T(8,128)}, bf16[512,768]{1,0:T(8,128)(2,1)}, f32[8,3072]{1,0:T(8,128)}, bf16[16,88,768]{2,1,0:T(8,128)(2,1)}, bf16[16,88,768]{2,1,0:T(8,128)(2,1)}) custom-call(bf16[3,1024,768]{2,1,0:T(8,128)(2,1)} %attn_bwd.5.refs_0_, bf16[1024,768]{1,0:T(8,128)(2,1)} %copy-done.7, bf16[2,768,2304]{2,1,0:T(8,128)(2,1)} %refs_2_.3, ...), custom_call_target="tpu_custom_call" | custom-call | flops 1 | bytes 1 | tf_op jit(solution)/shard_map/qkv_all/pallas_call | solution.py:823
  335.4 3.0 stage2.2
  340.4 2.4 collective-permute-done.8
  344.4 16.2 %collective-permute-done.6.refs_1_ = bf16[4,144,768]{2,1,0:T(8,128)(2,1)S(1)} collective-permute-done((bf16[4,144,768]{2,1,0:T(8,128)(2,1)S(1)}, bf16[4,144,768]{2,1,0:T(8,128)(2,1)S(1)}, u32[]{:S(2)}, u32[]{:S(2)}) %collective-permute-start.6) | collective-permute-done | bytes 884768 | tf_op jit(solution)/shard_map/ppermute | solution.py:1014
  367.8 2.7 collective-permute-start.11
  370.4 16.0 %collective-permute-done.10.refs_5_.refs_2_ = bf16[288,768]{1,0:T(8,128)(2,1)S(1)} collective-permute-done((bf16[288,768]{1,0:T(8,128)(2,1)}, bf16[288,768]{1,0:T(8,128)(2,1)S(1)}, u32[]{:S(2)}, u32[]{:S(2)}) %collective-permute-start.10) | collective-permute-done | bytes 442400 | tf_op jit(solution)/shard_map/ppermute | solution.py:901
  386.5 2.5 collective-permute-start.12
  389.0 3.5 collective-permute-done.14.refs_3_
  393.6 2.4 stage2.3
  400.4 4.7 %collective-permute-done.16.refs_3_ = bf16[4,40,768]{2,1,0:T(8,128)(2,1)S(1)} collective-permute-done((bf16[4,40,768]{2,1,0:T(8,128)(2,1)S(1)}, bf16[4,40,768]{2,1,0:T(8,128)(2,1)S(1)}, u32[]{:S(2)}, u32[]{:S(2)}) %collective-permute-start.16) | collective-permute-done | bytes 245792 | tf_op jit(solution)/shard_map/ppermute | solution.py:901
  405.9 3.4 collective-permute-start.17
  411.8 1.9 maximum_select_fusion
  413.6 8.0 %collective-permute-done.18.refs_7_ = bf16[88,768]{1,0:T(8,128)(2,1)S(1)} collective-permute-done((bf16[88,768]{1,0:T(8,128)(2,1)S(1)}, bf16[88,768]{1,0:T(8,128)(2,1)S(1)}, u32[]{:S(2)}, u32[]{:S(2)}) %collective-permute-start.18) | collective-permute-done | bytes 135200 | tf_op jit(solution)/shard_map/ppermute | solution.py:901
  (124 shorter events, 36.6 us)
Async XLA Ops:
  7.2 414.4 %reduce-scatter.2.cloned.1.call-start = ((), (), s32[]{:S(2)}) async-start(), calls=%async_computation.1 | async-start | bytes 10948608 | tf_op jit(solution)/shard_map/reduce_scatter | solution.py:1216
  8.9 21.4 %collective-permute-start = (bf16[512,768]{1,0:T(8,128)(2,1)S(1)}, bf16[512,768]{1,0:T(8,128)(2,1)S(1)}, u32[]{:S(2)}, u32[]{:S(2)}) collective-permute-start(bf16[512,768]{1,0:T(8,128)(2,1)S(1)} %get-tuple-element.170), channel_id=1, source_target_pairs={{0,1},{1,0},{2,3},{3,2},{4,5},{5,4},{6,7},{7,6},{8,9},{9,8},{10,11... | collective-permute-start | bytes 2359304 | tf_op jit(solution)/shard_map/ppermute | solution.py:1014
  12.9 115.5 %collective-permute-start.2 = (bf16[512,768]{1,0:T(8,128)(2,1)S(1)}, bf16[512,768]{1,0:T(8,128)(2,1)S(1)}, u32[]{:S(2)}, u32[]{:S(2)}) collective-permute-start(bf16[512,768]{1,0:T(8,128)(2,1)S(1)} %get-tuple-element.167), channel_id=1, source_target_pairs={{0,1},{1,0},{2,3},{3,2},{4,5},{5,4},{6,7},{7,6},{8,9},{9,8},{10,11... | collective-permute-start | bytes 2359304 | tf_op jit(solution)/shard_map/ppermute | solution.py:1014
  13.0 17.3 %copy-start.19 = (f32[2,2,1,768]{3,2,1,0:T(1,128)}, f32[2,2,1,768]{3,2,1,0:T(1,128)S(1)}, u32[]{:S(2)}) copy-start(f32[2,2,1,768]{3,2,1,0:T(1,128)S(1)} %broadcast_in_dim.21.gain_ref.refs_4_.refs_8_.refs_3_) | copy-start | bytes 36868
  13.1 17.3 %copy-start.21 = (f32[2,2,1,768]{3,2,1,0:T(1,128)}, f32[2,2,1,768]{3,2,1,0:T(1,128)S(1)}, u32[]{:S(2)}) copy-start(f32[2,2,1,768]{3,2,1,0:T(1,128)S(1)} %broadcast_in_dim.22.shift_ref.refs_5_.refs_9_.refs_4_) | copy-start | bytes 36868
  13.2 17.2 %copy-start.20 = (f32[2,1,2304]{2,1,0:T(1,128)}, f32[2,1,2304]{2,1,0:T(1,128)S(1)}, u32[]{:S(2)}) copy-start(f32[2,1,2304]{2,1,0:T(1,128)S(1)} %broadcast_in_dim.24.bias_ref.refs_10_) | copy-start | bytes 55300
  18.0 12.3 %copy-start.2 = (bf16[2,768,2304]{2,1,0:T(8,128)(2,1)S(1)}, bf16[2,768,2304]{2,1,0:T(8,128)(2,1)}, u32[]{:S(2)}) copy-start(bf16[2,768,2304]{2,1,0:T(8,128)(2,1)} %refs_2_.3) | copy-start | bytes 21233668
  35.2 19.6 %copy-start.7 = (bf16[1024,768]{1,0:T(8,128)(2,1)}, bf16[1024,768]{1,0:T(8,128)(2,1)S(1)}, u32[]{:S(2)}) copy-start(bf16[1024,768]{1,0:T(8,128)(2,1)S(1)} %get-tuple-element.122.refs_1_) | copy-start | bytes 4718596
  126.3 43.8 %collective-permute-start.1 = (bf16[512,768]{1,0:T(8,128)(2,1)}, bf16[512,768]{1,0:T(8,128)(2,1)S(1)}, u32[]{:S(2)}, u32[]{:S(2)}) collective-permute-start(bf16[512,768]{1,0:T(8,128)(2,1)} %get-tuple-element.98), channel_id=1, source_target_pairs={{0,1},{1,0},{2,3},{3,2},{4,5},{5,4},{6,7},{7,6},{8,9},{9,8},{10,11... | collective-permute-start | bytes 2359304 | tf_op jit(solution)/shard_map/ppermute | solution.py:1014
  264.0 14.2 %collective-permute-start.3 = (bf16[16,288,768]{2,1,0:T(8,128)(2,1)}, bf16[16,288,768]{2,1,0:T(8,128)(2,1)}, u32[]{:S(2)}, u32[]{:S(2)}) collective-permute-start(bf16[16,288,768]{2,1,0:T(8,128)(2,1)} %get-tuple-element.120), channel_id=1, source_target_pairs={{0,2},{2,0},{4,6},{6,4},{8,10},{10,8},{12,14},{14,12},{16,18},{18,... | collective-permute-start | bytes 21233672 | tf_op jit(solution)/shard_map/ppermute | solution.py:901
  264.1 14.2 %slice-start = ((s8[7077888]{0:T(1024)(128)(4,1)}), s8[4194304]{0:T(1024)(128)(4,1)S(1)}, s32[]{:S(2)}) async-start(s8[7077888]{0:T(1024)(128)(4,1)} %bitcast.23), calls=%async_computation.2 | async-start | bytes 8388608
  264.1 14.2 %slice-start.1 = ((s8[7077888]{0:T(1024)(128)(4,1)}), s8[2883584]{0:T(1024)(128)(4,1)S(1)}, s32[]{:S(2)}) async-start(s8[7077888]{0:T(1024)(128)(4,1)} %bitcast.23), calls=%async_computation.3 | async-start | bytes 5767168
  288.9 43.6 %collective-permute-start.4 = (bf16[4,2,144,768]{3,2,1,0:T(8,128)(2,1)}, bf16[4,2,144,768]{3,2,1,0:T(8,128)(2,1)S(1)}, u32[]{:S(2)}, u32[]{:S(2)}) collective-permute-start(bf16[4,2,144,768]{3,2,1,0:T(8,128)(2,1)} %get-tuple-element.129), channel_id=1, source_target_pairs={{0,4},{2,6},{4,0},{6,2},{8,12},{10,14},{12,8},{14,10},{16,20},{18,... | collective-permute-start | bytes 5308424 | tf_op jit(solution)/shard_map/ppermute | solution.py:901
  290.4 43.5 %collective-permute-start.5 = (bf16[4,2,144,768]{3,2,1,0:T(8,128)(2,1)}, bf16[4,2,144,768]{3,2,1,0:T(8,128)(2,1)}, u32[]{:S(2)}, u32[]{:S(2)}) collective-permute-start(bf16[4,2,144,768]{3,2,1,0:T(8,128)(2,1)} %get-tuple-element.131), channel_id=1, source_target_pairs={{0,1},{1,0},{2,3},{3,2},{4,5},{5,4},{6,7},{7,6},{8,9},{9,8},{10,11... | collective-permute-start | bytes 5308424 | tf_op jit(solution)/shard_map/ppermute | solution.py:1014
  315.2 18.6 %copy-start.6 = (bf16[4,2,144,768]{3,2,1,0:T(8,128)(2,1)S(1)}, bf16[4,2,144,768]{3,2,1,0:T(8,128)(2,1)}, u32[]{:S(2)}) copy-start(bf16[4,2,144,768]{3,2,1,0:T(8,128)(2,1)} %copy-done.5) | copy-start | bytes 5308420
  315.3 18.6 %copy-start.13 = (bf16[4,2,144,768]{3,2,1,0:T(8,128)(2,1)S(1)}, bf16[4,2,144,768]{3,2,1,0:T(8,128)(2,1)}, u32[]{:S(2)}) copy-start(bf16[4,2,144,768]{3,2,1,0:T(8,128)(2,1)} %copy-done.12) | copy-start | bytes 5308420
  338.4 4.3 %collective-permute-start.8 = (bf16[16,88,768]{2,1,0:T(8,128)(2,1)S(1)}, bf16[16,88,768]{2,1,0:T(8,128)(2,1)S(1)}, u32[]{:S(2)}, u32[]{:S(2)}) collective-permute-start(bf16[16,88,768]{2,1,0:T(8,128)(2,1)S(1)} %copy-done.35), channel_id=1, source_target_pairs={{0,2},{2,0},{4,6},{6,4},{8,10},{10,8},{12,14},{14,12},{16,18},{18,... | collective-permute-start | bytes 6488072 | tf_op jit(solution)/shard_map/ppermute | solution.py:901
  338.5 22.1 %collective-permute-start.6 = (bf16[4,144,768]{2,1,0:T(8,128)(2,1)S(1)}, bf16[4,144,768]{2,1,0:T(8,128)(2,1)S(1)}, u32[]{:S(2)}, u32[]{:S(2)}) collective-permute-start(bf16[4,144,768]{2,1,0:T(8,128)(2,1)S(1)} %get-tuple-element.133), channel_id=1, source_target_pairs={{0,1},{1,0},{2,3},{3,2},{4,5},{5,4},{6,7},{7,6},{8,9},{9,8},{10,11... | collective-permute-start | bytes 2654216 | tf_op jit(solution)/shard_map/ppermute | solution.py:1014
  339.1 21.7 %collective-permute-start.7 = (bf16[4,144,768]{2,1,0:T(8,128)(2,1)S(1)}, bf16[4,144,768]{2,1,0:T(8,128)(2,1)S(1)}, u32[]{:S(2)}, u32[]{:S(2)}) collective-permute-start(bf16[4,144,768]{2,1,0:T(8,128)(2,1)S(1)} %get-tuple-element.135), channel_id=1, source_target_pairs={{0,4},{2,6},{4,0},{6,2},{8,12},{10,14},{12,8},{14,10},{16,20},{18,... | collective-permute-start | bytes 2654216 | tf_op jit(solution)/shard_map/ppermute | solution.py:901
  344.4 23.4 %copy-start.16 = (bf16[4,2,40,768]{3,2,1,0:T(8,128)(2,1)}, bf16[4,2,40,768]{3,2,1,0:T(8,128)(2,1)S(1)}, u32[]{:S(2)}) copy-start(bf16[4,2,40,768]{3,2,1,0:T(8,128)(2,1)S(1)} %get-tuple-element.146.refs_2_) | copy-start | bytes 1474564
  362.8 29.7 %collective-permute-start.9 = (bf16[512,768]{1,0:T(8,128)(2,1)}, bf16[512,768]{1,0:T(8,128)(2,1)S(1)}, u32[]{:S(2)}, u32[]{:S(2)}) collective-permute-start(bf16[512,768]{1,0:T(8,128)(2,1)} %get-tuple-element.141.refs_4_), channel_id=1, source_target_pairs={{0,1},{1,0},{2,3},{3,2},{4,5},{5,4},{6,7},{7,6},{8,9},{9,8},{10,11... | collective-permute-start | bytes 2359304 | tf_op jit(solution)/shard_map/ppermute | solution.py:1014
  364.3 28.2 %collective-permute-start.13 = (bf16[4,2,48,768]{3,2,1,0:T(8,128)(2,1)}, bf16[4,2,48,768]{3,2,1,0:T(8,128)(2,1)}, u32[]{:S(2)}, u32[]{:S(2)}) collective-permute-start(bf16[4,2,48,768]{3,2,1,0:T(8,128)(2,1)} %get-tuple-element.145), channel_id=1, source_target_pairs={{0,4},{2,6},{4,0},{6,2},{8,12},{10,14},{12,8},{14,10},{16,20},{18,... | collective-permute-start | bytes 1769480 | tf_op jit(solution)/shard_map/ppermute | solution.py:901
  365.7 26.8 %collective-permute-start.14 = (bf16[4,2,40,768]{3,2,1,0:T(8,128)(2,1)}, bf16[4,2,40,768]{3,2,1,0:T(8,128)(2,1)}, u32[]{:S(2)}, u32[]{:S(2)}) collective-permute-start(bf16[4,2,40,768]{3,2,1,0:T(8,128)(2,1)} %get-tuple-element.147), channel_id=1, source_target_pairs={{0,1},{1,0},{2,3},{3,2},{4,5},{5,4},{6,7},{7,6},{8,9},{9,8},{10,11... | collective-permute-start | bytes 1474568 | tf_op jit(solution)/shard_map/ppermute | solution.py:1014
  366.2 20.3 %collective-permute-start.10 = (bf16[288,768]{1,0:T(8,128)(2,1)}, bf16[288,768]{1,0:T(8,128)(2,1)S(1)}, u32[]{:S(2)}, u32[]{:S(2)}) collective-permute-start(bf16[288,768]{1,0:T(8,128)(2,1)} %get-tuple-element.142), channel_id=1, source_target_pairs={{0,8},{2,10},{4,12},{6,14},{8,0},{10,2},{12,4},{14,6},{16,24},{18,... | collective-permute-start | bytes 1327112 | tf_op jit(solution)/shard_map/ppermute | solution.py:901
  367.8 21.2 %collective-permute-start.11 = (bf16[288,768]{1,0:T(8,128)(2,1)}, bf16[288,768]{1,0:T(8,128)(2,1)S(1)}, u32[]{:S(2)}, u32[]{:S(2)}) collective-permute-start(bf16[288,768]{1,0:T(8,128)(2,1)} %get-tuple-element.143), channel_id=1, source_target_pairs={{0,16},{2,18},{4,20},{6,22},{8,24},{10,26},{12,28},{14,30},{16,0},... | collective-permute-start | bytes 1327112 | tf_op jit(solution)/shard_map/ppermute | solution.py:901
  386.5 13.9 %collective-permute-start.12 = (bf16[288,768]{1,0:T(8,128)(2,1)}, bf16[288,768]{1,0:T(8,128)(2,1)S(1)}, u32[]{:S(2)}, u32[]{:S(2)}) collective-permute-start(bf16[288,768]{1,0:T(8,128)(2,1)} %copy-done.22), channel_id=1, source_target_pairs={{0,24},{2,26},{4,28},{6,30},{8,16},{10,18},{12,20},{14,22},{16,8},... | collective-permute-start | bytes 1327112 | tf_op jit(solution)/shard_map/ppermute | solution.py:901
  396.0 9.1 %collective-permute-start.15 = (bf16[4,48,768]{2,1,0:T(8,128)(2,1)S(1)}, bf16[4,48,768]{2,1,0:T(8,128)(2,1)S(1)}, u32[]{:S(2)}, u32[]{:S(2)}) collective-permute-start(bf16[4,48,768]{2,1,0:T(8,128)(2,1)S(1)} %get-tuple-element.149), channel_id=1, source_target_pairs={{0,1},{1,0},{2,3},{3,2},{4,5},{5,4},{6,7},{7,6},{8,9},{9,8},{10,11... | collective-permute-start | bytes 884744 | tf_op jit(solution)/shard_map/ppermute | solution.py:1014
  398.8 12.9 %copy-start.26 = (f32[512,768]{1,0:T(8,128)S(1)}, f32[512,768]{1,0:T(8,128)}, u32[]{:S(2)}) copy-start(f32[512,768]{1,0:T(8,128)} %get-tuple-element.127) | copy-start | bytes 4718596
  398.8 6.2 %collective-permute-start.16 = (bf16[4,40,768]{2,1,0:T(8,128)(2,1)S(1)}, bf16[4,40,768]{2,1,0:T(8,128)(2,1)S(1)}, u32[]{:S(2)}, u32[]{:S(2)}) collective-permute-start(bf16[4,40,768]{2,1,0:T(8,128)(2,1)S(1)} %get-tuple-element.151), channel_id=1, source_target_pairs={{0,4},{2,6},{4,0},{6,2},{8,12},{10,14},{12,8},{14,10},{16,20},{18,... | collective-permute-start | bytes 737288 | tf_op jit(solution)/shard_map/ppermute | solution.py:901
  405.9 7.7 %collective-permute-start.17 = (bf16[88,768]{1,0:T(8,128)(2,1)S(1)}, bf16[88,768]{1,0:T(8,128)(2,1)S(1)}, u32[]{:S(2)}, u32[]{:S(2)}) collective-permute-start(bf16[88,768]{1,0:T(8,128)(2,1)S(1)} %get-tuple-element.153), channel_id=1, source_target_pairs={{0,8},{2,10},{4,12},{6,14},{8,0},{10,2},{12,4},{14,6},{16,24},{18,... | collective-permute-start | bytes 405512 | tf_op jit(solution)/shard_map/ppermute | solution.py:901
  409.3 12.3 %collective-permute-start.18 = (bf16[88,768]{1,0:T(8,128)(2,1)S(1)}, bf16[88,768]{1,0:T(8,128)(2,1)S(1)}, u32[]{:S(2)}, u32[]{:S(2)}) collective-permute-start(bf16[88,768]{1,0:T(8,128)(2,1)S(1)} %get-tuple-element.154), channel_id=1, source_target_pairs={{0,16},{2,18},{4,20},{6,22},{8,24},{10,26},{12,28},{14,30},{16,0},... | collective-permute-start | bytes 405512 | tf_op jit(solution)/shard_map/ppermute | solution.py:901
  410.3 11.3 %collective-permute-start.19 = (bf16[88,768]{1,0:T(8,128)(2,1)S(1)}, bf16[88,768]{1,0:T(8,128)(2,1)S(1)}, u32[]{:S(2)}, u32[]{:S(2)}) collective-permute-start(bf16[88,768]{1,0:T(8,128)(2,1)S(1)} %get-tuple-element.155), channel_id=1, source_target_pairs={{0,24},{2,26},{4,28},{6,30},{8,16},{10,18},{12,20},{14,22},{16,8},... | collective-permute-start | bytes 405512 | tf_op jit(solution)/shard_map/ppermute | solution.py:901
  (28 other events, 96.9 us)
Sparse Core Ops, SparseCore 0:
  170.2 144.1 reduce-scatter.1
